TPU v7x, 32 devices: a whole 2x2x4 slice. The times are simulated.
32 devices in a mesh: dp: 2 (over x), row: 4 (over z), col: 4 (over y, core).
Axes of the slice: x: 2, y: 2, z: 4, core: 2. Of those that a mesh axis runs over, the one named last changes fastest.
Arguments:
- tokens: bfloat16 [4096, 768], P(('dp', 'row')), may hold values from -6 to 6
- segments: int32 [8, 512], P(('dp', 'row')), may hold values from 0 to 5, never falling along the last dimension, each value on 1 to 256 neighbouring positions
- routes: int32 [4096, 1], P(('dp', 'row')), may hold values from 0 to 7; in each aligned block of 512 rows (0 to 511, 512 to 1023, ...) at most 128 rows name the same one
- norm_gain: float32 [768], replicated, may hold values from 0.5 to 1.5
- mix_gain: float32 [768], replicated, may hold values from 0.5 to 1.5
- qkv_weight: bfloat16 [768, 3, 768], P('row', None, 'col'), may hold values from -0.21875 to 0.21875
- proj_weight: bfloat16 [768, 768], P('col', 'row'), may hold values from -1.75 to 1.75
- rel_table: float32 [32, 12], P(None, 'col'), may hold values from -95 to 135
- router_weight: float32 [768, 8], replicated, may hold values from -0.109375 to 0.109375
- expert_in: bfloat16 [8, 768, 3072], P(('dp', 'row'), None, 'col'), may hold values from -0.21875 to 0.21875
- expert_out: bfloat16 [8, 3072, 768], P(('dp', 'row'), 'col'), may hold values from -0.875 to 0.875
- cotangent: float32 [4096, 768], P(('dp', 'row')), may hold values from -6 to 6
Outputs:
- output: float32 [4096, 768], P(('dp', 'row'))
- grad_tokens: float32 [4096, 768], P(('dp', 'row'))
- grad_qkv_weight: float32 [768, 3, 768], P('row', None, 'col')
- grad_proj_weight: float32 [768, 768], P('col', 'row')
- grad_rel_table: float32 [32, 12], P(None, 'col')
- grad_norm_gain: float32 [768], replicated
- grad_mix_gain: float32 [768], replicated
- grad_router_weight: float32 [768, 8], replicated
- grad_expert_in: float32 [8, 768, 3072], P(('dp', 'row'), None, 'col')
- grad_expert_out: float32 [8, 3072, 768], P(('dp', 'row'), 'col')
Inputs may be any that keep to these rules, and one draw needn't show every extreme that they name: `routes`: in each aligned block of 512 rows (the tokens of one index of dp and row) no expert is named more than 128 times, and in some block one expert is named exactly 128 times. `segments`: along each packed sequence the document numbers never fall; each document covers 1 to 256 positions and one covers exactly 256.
All inputs are finite; a program needn't handle non-finite values.
Results may differ from a plain program's by a relative error of at most 0.012.
The roundings to bfloat16 on the way count: a program that leaves them out, or rounds other values in their place, can miss the bound.
Values may be sent and summed in bfloat16 or wider, within the bound.
No kernel may reach another device: no remote copies, remote signals or barrier semaphores. Data moves between devices by JAX's collectives and lax.ppermute only.
A program may use at most 128 MiB of HBM per device.

v0:
```python
from functools import partial
import math

import jax
import jax.numpy as jnp
from jax import lax
from jax.experimental import pallas as pl
from jax.experimental.pallas import tpu as pltpu
from jax.sharding import PartitionSpec as P

BUCKETS = 32
MAX_DIST = 128
EPS = 1e-06
NEG = -1e30
GELU_C = 0.7978845608028654
GELU_K = 0.044715
BF = jnp.bfloat16
F32 = jnp.float32
HI = lax.Precision.HIGHEST
DR = ("dp", "row")


def bucket_edges():
    half_count = BUCKETS // 2
    exact_count = half_count // 2
    edge_list = []
    for target in range(1, half_count):
        if target < exact_count:
            edge_list.append(target)
        else:
            for distance in range(exact_count, MAX_DIST + 1):
                reached = exact_count + int(
                    math.log(distance / exact_count)
                    / math.log(MAX_DIST / exact_count)
                    * (half_count - exact_count)
                )
                if min(reached, half_count - 1) >= target:
                    edge_list.append(distance)
                    break
    return edge_list


def offset_onehot(length):
    offsets = jnp.arange(2 * length, dtype=jnp.int32) - (length - 1)
    magnitude = jnp.abs(offsets)
    ids = jnp.where(offsets > 0, BUCKETS // 2, 0)
    for border in bucket_edges():
        ids = ids + (magnitude >= border).astype(jnp.int32)
    ids = jnp.where(offsets >= length, -1, ids)
    return (ids[:, None] == jnp.arange(128, dtype=jnp.int32)[None, :]).astype(F32)


def bias_kernel(off_ref, out_ref):
    heads, length, _ = out_ref.shape
    for h in range(heads):
        rows = jnp.broadcast_to(off_ref[h : h + 1, :], (length, 2 * length))
        skewed = pltpu.roll(rows, 1, 1, stride=1, stride_axis=0)
        out_ref[h] = skewed[:, length:]


def position_bias(per_offset, length):
    heads = per_offset.shape[0]
    return pl.pallas_call(
        bias_kernel,
        out_shape=jax.ShapeDtypeStruct((heads, length, length), F32),
        name="position_bias",
        cost_estimate=pl.CostEstimate(
            flops=heads * length * length * 4, bytes_accessed=heads * length * length * 4, transcendentals=0
        ),
    )(per_offset)


def dot_n(a, b, precision=None):
    return jnp.dot(a, b, precision=precision, preferred_element_type=F32)


def dot_t(a, b, precision=None):
    return lax.dot_general(a, b, (((1,), (1,)), ((), ())), precision=precision, preferred_element_type=F32)


def t_dot(a, b, precision=None):
    return lax.dot_general(a, b, (((0,), (0,)), ((), ())), precision=precision, preferred_element_type=F32)


def call(kernel, outs, operands, flops, scratch=()):
    moved = sum(o.size * o.dtype.itemsize for o in operands) + sum(
        math.prod(o.shape) * o.dtype.itemsize for o in outs
    )
    return pl.pallas_call(
        kernel,
        out_shape=tuple(outs),
        scratch_shapes=list(scratch),
        cost_estimate=pl.CostEstimate(flops=flops, bytes_accessed=moved, transcendentals=0),
    )(*operands)


def sds(shape, dtype):
    return jax.ShapeDtypeStruct(shape, dtype)


STEP = 256


def unpack_kernel(n_row, index_ref, *refs):
    b_refs, (w_ref, p_ref) = refs[:n_row], refs[n_row:]
    block = b_refs[0].shape[0]
    cols = w_ref.shape[1]
    for k in range(n_row):
        rows = pl.ds(pl.multiple_of((index_ref[0] ^ k) * block, block), block)
        w_ref[rows, :] = b_refs[k][:, :cols]
        p_ref[rows, :] = b_refs[k][:, cols:]


def front_kernel(n_col, heads, normed_ref, w_ref, seg_row_ref, seg_col_ref, bias_ref, perm_ref, *refs):
    qkv_ref, att_ref, probs_ref = refs[:3]
    part_refs = refs[3:]
    qkv_ref[...] = dot_n(normed_ref[...], w_ref[...]).astype(BF)
    length, width = att_ref.shape
    size = width // heads
    seg_row = seg_row_ref[...]

    def body(i, carry):
        rows = pl.ds(pl.multiple_of(i * STEP, STEP), STEP)
        same = seg_col_ref[rows, :] == seg_row
        for h in range(heads):
            q = qkv_ref[rows, h * size : (h + 1) * size]
            k = qkv_ref[:, width + h * size : width + (h + 1) * size]
            v = qkv_ref[:, 2 * width + h * size : 2 * width + (h + 1) * size]
            scores = dot_t(q, k) * size ** (-0.5) + bias_ref[h, rows, :]
            scores = jnp.where(same, scores, NEG)
            top = jnp.max(scores, axis=1, keepdims=True)
            expo = jnp.exp(scores - top)
            probs = expo * (1.0 / jnp.sum(expo, axis=1, keepdims=True))
            probs_ref[h, rows, :] = probs
            att_ref[rows, h * size : (h + 1) * size] = dot_n(probs.astype(BF), v).astype(BF)
        return carry

    lax.fori_loop(0, length // STEP, body, 0)
    own = length // n_col
    for k in range(n_col):
        part_refs[k][...] = dot_n(perm_ref[k * own : (k + 1) * own, :], att_ref[...]).astype(BF)


def router_kernel(n_col, *refs):
    a_refs, p_refs = refs[:n_col], refs[n_col : 2 * n_col]
    tokens_ref, gain_ref, router_ref, picked_ref, slot_ref = refs[2 * n_col : 2 * n_col + 5]
    hidden_ref, probs_ref, gate_ref, send_ref = refs[2 * n_col + 5 :]
    own, width = tokens_ref.shape
    hidden = tokens_ref[...]
    for a_ref, p_ref in zip(a_refs, p_refs):
        hidden = hidden + dot_t(a_ref[...], p_ref[...])
    hidden_ref[...] = hidden
    inverse = lax.rsqrt(jnp.mean(hidden * hidden, axis=1, keepdims=True) + EPS)
    normed = hidden * inverse * gain_ref[...]
    logits = dot_t(normed, router_ref[...], HI)
    expo = jnp.exp(logits - jnp.max(logits, axis=1, keepdims=True))
    probs = expo / jnp.sum(expo, axis=1, keepdims=True)
    probs_ref[...] = probs
    gate = jnp.sum(probs * picked_ref[...], axis=1, keepdims=True)
    gate_ref[...] = gate
    send_ref[:, :width] = dot_n(slot_ref[...], normed.astype(BF)).astype(BF)
    high = gate.astype(BF).astype(F32)
    lane = lax.broadcasted_iota(jnp.int32, (own, 128), 1)
    extra = jnp.where(lane == 0, high, jnp.where(lane == 1, gate - high, 0.0)).astype(BF)
    send_ref[:, width:] = dot_n(slot_ref[...], extra).astype(BF)


def expert_kernel(pairs, *refs):
    row_refs, (w_in_ref, w_out_ref) = refs[:pairs], refs[pairs : pairs + 2]
    mixed_refs, (act_ref, slope_ref) = refs[pairs + 2 : 2 * pairs + 2], refs[2 * pairs + 2 :]
    size, width = mixed_refs[0].shape
    for i in range(pairs):
        part = slice(i * size, (i + 1) * size)
        pre = dot_n(row_refs[i][:, :width], w_in_ref[...])
        bent = jnp.tanh(GELU_C * (pre + GELU_K * pre * pre * pre))
        act = (0.5 * pre * (1.0 + bent)).astype(BF)
        act_ref[part, :] = act
        mixed_refs[i][...] = dot_n(act, w_out_ref[...]).astype(BF)
        slope_ref[part, :] = 0.5 * (1.0 + bent) + 0.5 * pre * (1.0 - bent * bent) * GELU_C * (
            1.0 + 3.0 * GELU_K * pre * pre
        )


def expert_back_kernel(pairs, *refs):
    row_refs, cot_refs = refs[:pairs], refs[pairs : 2 * pairs]
    slope_ref, w_in_ref, w_out_ref = refs[2 * pairs : 2 * pairs + 3]
    back_refs = refs[2 * pairs + 3 : 3 * pairs + 3]
    pre_ref, gated_ref, copy_ref = refs[3 * pairs + 3 :]
    size, width = back_refs[0].shape
    for i in range(pairs):
        part = slice(i * size, (i + 1) * size)
        cot = cot_refs[i][...]
        gate = row_refs[i][:, width : width + 1].astype(F32) + row_refs[i][:, width + 1 : width + 2].astype(F32)
        grad_pre = (gate * dot_t(cot, w_out_ref[...]) * slope_ref[part, :]).astype(BF)
        pre_ref[part, :] = grad_pre
        back_refs[i][...] = dot_t(grad_pre, w_in_ref[...]).astype(BF)
        gated_ref[part, :] = (gate * cot.astype(F32)).astype(BF)
        copy_ref[part, :] = row_refs[i][:, :width]


def pair_kernel(count, *refs):
    total = t_dot(refs[0][...], refs[count][...])
    for k in range(1, count):
        total = total + t_dot(refs[k][...], refs[count + k][...])
    refs[2 * count][...] = total


def token_kernel(
    mixed_ref, back_ref, slot_ref, hidden_ref, tokens_ref, probs_ref, gate_ref, picked_ref, gain_ref,
    router_ref, cot_ref, grad_ref, grad_bf_ref, delta_ref, router_out_ref, mix_ref,
):
    width = hidden_ref.shape[1]
    hidden, gate, cot, gain = hidden_ref[...], gate_ref[...], cot_ref[...], gain_ref[...]
    mixed = t_dot(slot_ref[...], mixed_ref[...])
    back = t_dot(slot_ref[...], back_ref[...])
    delta_ref[...] = (hidden - tokens_ref[...] + gate * mixed).astype(BF)
    grad_gate = jnp.sum(cot * mixed, axis=1, keepdims=True)
    grad_logits = grad_gate * gate * (picked_ref[...] - probs_ref[...])
    inverse = lax.rsqrt(jnp.mean(hidden * hidden, axis=1, keepdims=True) + EPS)
    normed = hidden * inverse * gain
    router_out_ref[...] = t_dot(grad_logits, normed, HI)
    grad_normed = back + dot_n(grad_logits, router_ref[...], HI)
    mix_ref[...] = jnp.sum(grad_normed * hidden * inverse, axis=0, keepdims=True)
    inner = jnp.sum(grad_normed * gain * hidden, axis=1, keepdims=True)
    grad = cot + inverse * gain * grad_normed - hidden * inverse * inverse * inverse * (inner / width)
    grad_ref[...] = grad
    grad_bf_ref[...] = grad.astype(BF)


def back_kernel(n_col, heads, *refs):
    g_refs, a_refs = refs[:n_col], refs[n_col : 2 * n_col]
    proj_ref, perm_ref, qkv_ref, probs_ref, att_ref, normed_ref, onehot_ref = refs[2 * n_col : 2 * n_col + 7]
    wgrad_ref, gq, table_ref = refs[2 * n_col + 7 : 2 * n_col + 10]
    gap, ga, dk, dv, offs = refs[2 * n_col + 10 :]
    length, width = att_ref.shape
    size = width // heads
    scale = size ** (-0.5)
    own = length // n_col
    for k in range(n_col):
        gap[k * own : (k + 1) * own, :] = dot_n(g_refs[k][...], proj_ref[...]).astype(BF)
    ga[...] = dot_n(perm_ref[...], gap[...]).astype(BF)
    dk[...] = jnp.zeros_like(dk)
    dv[...] = jnp.zeros_like(dv)
    offs[...] = jnp.zeros_like(offs)

    def body(i, carry):
        rows = pl.ds(pl.multiple_of(i * STEP, STEP), STEP)
        for h in range(heads):
            cols = slice(h * size, (h + 1) * size)
            q = qkv_ref[rows, cols]
            k = qkv_ref[:, width + h * size : width + (h + 1) * size]
            v = qkv_ref[:, 2 * width + h * size : 2 * width + (h + 1) * size]
            probs = probs_ref[h, rows, :]
            grad_out = ga[rows, cols]
            delta = jnp.sum(
                grad_out.astype(F32) * att_ref[rows, cols].astype(F32), axis=1, keepdims=True
            )
            grad_scores = probs * (dot_t(grad_out, v) - delta)
            grad_bf = grad_scores.astype(BF)
            gq[rows, cols] = (dot_n(grad_bf, k) * scale).astype(BF)
            dk[:, cols] += t_dot(grad_bf, q)
            dv[:, cols] += t_dot(probs.astype(BF), grad_out)
            wide = jnp.concatenate([jnp.zeros_like(grad_scores), grad_scores], axis=1)
            count = STEP // 2
            while count >= 8:
                wide = wide[:count] + pltpu.roll(wide[count:], 2 * length - count, 1)
                count //= 2
            offs[h] += pltpu.roll(wide, 2 * length - 1 - i * STEP, 1)
        return carry

    lax.fori_loop(0, length // STEP, body, 0)
    gq[:, width : 2 * width] = (dk[...] * scale).astype(BF)
    gq[:, 2 * width :] = dv[...].astype(BF)
    wgrad_ref[:, : 3 * width] = t_dot(normed_ref[...], gq[...]).astype(BF)
    total = t_dot(g_refs[0][...], a_refs[0][...])
    for k in range(1, n_col):
        total = total + t_dot(g_refs[k][...], a_refs[k][...])
    wgrad_ref[:, 3 * width :] = total.astype(BF)
    table_ref[...] = jnp.zeros_like(table_ref)
    for h in range(heads):
        rows = offs[h]
        line = rows[0:1]
        for j in range(1, 8):
            line = line + pltpu.roll(rows[j : j + 1], 2 * length - j, 1)
        table_ref[h : h + 1, :] = dot_n(jnp.broadcast_to(line, (8, 2 * length)), onehot_ref[...], HI)[0:1]


def normed_kernel(n_col, gq_ref, perm_ref, w_ref, z_ref, router_ref, mix_ref, table_ref, *refs):
    part_refs, flat_ref = refs[:n_col], refs[n_col]
    own, width = part_refs[0].shape
    experts = router_ref.shape[0]
    total = jnp.zeros((1, width), F32)
    for k in range(n_col):
        rows = slice(k * own, (k + 1) * own)
        moved = dot_n(perm_ref[rows, :], gq_ref[...]).astype(BF)
        part = dot_t(moved, w_ref[...])
        total = total + jnp.sum(part * z_ref[rows, :], axis=0, keepdims=True)
        part_refs[k][...] = part.astype(BF)
    flat_ref[...] = jnp.zeros_like(flat_ref)
    flat_ref[:experts, :] = router_ref[...]
    flat_ref[experts : experts + 1, :] = mix_ref[...]
    flat_ref[experts + 1 : experts + 2, :] = total
    flat_ref[experts + 8 :, :128] = table_ref[...]


def tokens_kernel(mine_ref, came_ref, grad_ref, cot_ref, tokens_ref, inverse_ref, gain_ref, out_ref):
    grad_normed = mine_ref[...].astype(F32) + came_ref[...].astype(F32)
    tokens, inverse, gain = tokens_ref[...], inverse_ref[...], gain_ref[...]
    inner = jnp.sum(grad_normed * gain * tokens, axis=1, keepdims=True)
    delta = (
        (grad_ref[...] - cot_ref[...])
        + inverse * gain * grad_normed
        - tokens * inverse * inverse * inverse * (inner / tokens.shape[1])
    )
    out_ref[...] = delta.astype(BF)


def place_kernel(n_col, *refs):
    b_refs, perm_ref, base_ref, out_ref = refs[:n_col], refs[n_col], refs[n_col + 1], refs[n_col + 2]
    own = b_refs[0].shape[0]
    total = base_ref[...].astype(F32)
    for k in range(n_col):
        total = total + dot_n(perm_ref[:, k * own : (k + 1) * own], b_refs[k][...])
    out_ref[...] = total


def swap(x, axes, count, mask):
    return lax.ppermute(x, axes, [(i, i ^ mask) for i in range(count)])


def bits_of(count):
    return [1 << b for b in range(count.bit_length() - 1)]


def gather_rel(x, axes, count):
    blocks = {0: x}
    for bit in reversed(bits_of(count)):
        new = {}
        for k, v in blocks.items():
            new[k | bit] = swap(v, axes, count, bit)
        blocks.update(new)
    return [blocks[k] for k in range(count)]


def scatter_rel(blocks, axes, count):
    held = dict(enumerate(blocks))
    for bit in bits_of(count):
        got = {k: swap(held[k | bit].astype(BF), axes, count, bit) for k in held if not k & bit}
        held = {k: held[k].astype(F32) + got[k].astype(F32) for k in got}
    return held[0]


def exchange(x, axes):
    return lax.all_to_all(x, axes, split_axis=0, concat_axis=0, tiled=True)


def exchange_rel(blocks, axes, count):
    return [blocks[0]] + [swap(blocks[k], axes, count, k) for k in range(1, count)]


def hold(x, *after):
    return lax.optimization_barrier((x,) + after)[0]


def in_order(blocks, index):
    count = len(blocks)
    if count == 2:
        first = jnp.where(index == 0, blocks[0], blocks[1])
        second = jnp.where(index == 0, blocks[1], blocks[0])
        return jnp.concatenate([first, second], axis=0)
    stacked = jnp.stack(blocks)
    return jnp.concatenate(
        [lax.dynamic_index_in_dim(stacked, index ^ j, 0, keepdims=False) for j in range(count)], axis=0
    )


def body(
    tokens,
    segments,
    routes,
    norm_gain,
    mix_gain,
    qkv_weight,
    proj_weight,
    rel_table,
    router_weight,
    expert_in,
    expert_out,
    cotangent,
):
    n_dp, n_row, n_col = lax.axis_size("dp"), lax.axis_size("row"), lax.axis_size("col")
    experts = n_dp * n_row
    dp, row, col = lax.axis_index("dp"), lax.axis_index("row"), lax.axis_index("col")
    count, width = tokens.shape
    length = segments.shape[1]
    heads = rel_table.shape[1]
    local = proj_weight.shape[0]
    block = width // n_row
    own = count // n_col
    slots = 2 * count // experts // n_col
    total_slots = experts * slots
    w_in, w_out = expert_in[0], expert_out[0]

    packed = jnp.concatenate([qkv_weight.reshape(block, 3 * local), proj_weight.T], axis=1)
    packed_rel = gather_rel(packed, "row", n_row)
    weight, proj_local = pl.pallas_call(
        partial(unpack_kernel, n_row),
        out_shape=(sds((width, 3 * local), BF), sds((width, local), BF)),
        in_specs=[pl.BlockSpec(memory_space=pltpu.SMEM)] + [pl.BlockSpec(memory_space=pltpu.VMEM)] * n_row,
        name="unpack",
        cost_estimate=pl.CostEstimate(flops=0, bytes_accessed=16 * width * local, transcendentals=0),
    )(row.reshape(1).astype(jnp.int32), *packed_rel)

    chosen = routes[:, 0]
    expert_ids = jnp.arange(experts, dtype=jnp.int32)
    hits = (expert_ids[:, None] == chosen[None, :]).astype(F32)
    place = jnp.arange(count, dtype=jnp.int32)
    before = (place[:, None] < place[None, :]).astype(BF)
    earlier = dot_n(hits.astype(BF), before)
    totals = jnp.sum(hits, axis=1)
    starts = jnp.sum(
        jnp.where(expert_ids[None, :] < expert_ids[:, None], totals[None, :], 0.0), axis=1
    )
    start = jnp.sum(hits * starts[:, None], axis=0).astype(jnp.int32)
    rank = jnp.sum(hits * earlier, axis=0).astype(jnp.int32)
    spot = start + rank
    owner, inner = spot % n_col, spot // n_col
    dest = (owner ^ col) * own + inner
    perm = (place[:, None] == dest[None, :]).astype(BF)
    perm_t = (dest[:, None] == place[None, :]).astype(BF)
    perm_own = perm[:own]
    local_rank = inner - (start + n_col - 1 - col) // n_col
    slot = jnp.where(owner == col, chosen * slots + local_rank, -1)
    slot_ids = jnp.arange(total_slots, dtype=jnp.int32)
    slot_of_token = (slot_ids[:, None] == slot[None, :]).astype(BF)
    slot_of_own = dot_t(slot_of_token, perm_own).astype(BF)
    picked = dot_t(perm_own, hits.astype(BF))

    inputs = tokens.astype(F32)
    inverse = lax.rsqrt(jnp.mean(inputs * inputs, axis=1, keepdims=True) + EPS)
    normed_bf = (inputs * inverse * norm_gain).astype(BF)
    tokens_perm = dot_n(perm, tokens)
    inverse_perm = lax.rsqrt(jnp.mean(tokens_perm * tokens_perm, axis=1, keepdims=True) + EPS)
    tokens_own, inverse_own = tokens_perm[:own], inverse_perm[:own]

    onehot = offset_onehot(length)
    per_offset = dot_n(rel_table.T, onehot[:, :BUCKETS].T, HI)
    bias = position_bias(per_offset, length)

    cot_slots = dot_n(slot_of_token, cotangent.astype(BF)).astype(BF)
    cot_slots = hold(cot_slots, packed_rel[n_row // 2])
    cot_came = exchange(cot_slots.reshape(experts, slots, width), DR).reshape(total_slots, width)
    cot_blocks = gather_rel(cot_came, "col", n_col)
    proj_blocks = gather_rel(proj_local, "col", n_col)
    seg_row, seg_col = segments.reshape(1, length), segments.reshape(length, 1)
    qkv_rows, attended, probs, *att_parts = call(
        partial(front_kernel, n_col, heads),
        [sds((length, 3 * local), BF), sds((length, local), BF), sds((heads, length, length), F32)]
        + [sds((own, local), BF)] * n_col,
        [normed_bf, weight, seg_row, seg_col, bias, perm],
        2 * length * local * (3 * width + 3 * length),
    )
    att_own = exchange_rel(att_parts, "col", n_col)

    router_t = router_weight.T
    mix_row, gain_row = mix_gain.reshape(1, width), norm_gain.reshape(1, width)
    hidden, router_probs, gate, token_slots = call(
        partial(router_kernel, n_col),
        [sds((own, width), F32), sds((own, experts), F32), sds((own, 1), F32), sds((total_slots, width + 128), BF)],
        [*att_own, *proj_blocks, tokens_own, mix_row, router_t, picked, slot_of_own],
        2 * own * width * (width + total_slots),
    )

    token_slots = hold(token_slots, cot_came)
    token_came = exchange(token_slots.reshape(experts, slots, width + 128), DR)
    token_blocks = gather_rel(token_came.reshape(total_slots, width + 128), "col", n_col)
    pairs = 2
    row = sds((total_slots, width), BF)
    twice = sds((pairs * total_slots, width), BF)
    work = 4 * pairs * total_slots * width * width
    mixed_parts, back_parts, acts, slopes, behind = [], [], [], [], []
    for k in range(0, n_col, pairs):
        *mixed, act, slope = call(
            partial(expert_kernel, pairs), [row] * pairs + [twice, sds(twice.shape, F32)],
            [*token_blocks[k : k + pairs], w_in, w_out], work,
        )
        mixed_parts += mixed
        acts.append(act)
        slopes.append(slope)
    for k in range(0, n_col, pairs):
        *back, pre, gated, rows = call(
            partial(expert_back_kernel, pairs), [row] * pairs + [twice] * 3,
            [*token_blocks[k : k + pairs], *cot_blocks[k : k + pairs], slopes[k // pairs], w_in, w_out],
            work,
        )
        back_parts += back
        behind.append((pre, gated, rows))

    def to_home(parts):
        summed = scatter_rel(parts, "col", n_col).astype(BF)
        return exchange(summed.reshape(experts, slots, width), DR).reshape(total_slots, width)

    mixed_came = to_home(mixed_parts)
    back_came = to_home(back_parts)
    work = 2 * n_col * total_slots * width * width
    grad_in_local, = call(
        partial(pair_kernel, len(behind)), [sds((width, width), F32)],
        [r for _, _, r in behind] + [p for p, _, _ in behind], work,
    )
    grad_out_local, = call(
        partial(pair_kernel, len(behind)), [sds((width, width), F32)],
        acts + [g for _, g, _ in behind], work,
    )
    mixed_came, grad_in_local, grad_out_local = lax.optimization_barrier(
        (mixed_came, grad_in_local, grad_out_local)
    )

    cot_own = dot_n(perm_own.astype(F32), cotangent, HI)
    z_perm = hold(tokens_perm, mixed_parts[0]) * inverse_perm
    mixed_came, z_perm = lax.optimization_barrier((mixed_came, z_perm))

    grad_hidden, grad_hidden_bf, out_delta, router_local, mix_local = call(
        token_kernel,
        [sds((own, width), F32), sds((own, width), BF), sds((own, width), BF), sds((experts, width), F32),
         sds((1, width), F32)],
        [mixed_came, back_came, slot_of_own, hidden, tokens_own, router_probs, gate, picked, mix_row,
         router_t, cot_own],
        4 * own * width * total_slots,
    )
    grad_blocks = gather_rel(grad_hidden_bf, "col", n_col)
    out_blocks = gather_rel(hold(out_delta, *grad_blocks), "col", n_col)

    wgrad, grad_qkv, table_local = call(
        partial(back_kernel, n_col, heads),
        [sds((width, 4 * local), BF), sds((length, 3 * local), BF), sds((8, 128), F32)],
        [*grad_blocks, *att_parts, proj_local, perm_t, qkv_rows, probs, attended, normed_bf, onehot],
        2 * length * local * (5 * width + 5 * length),
        [pltpu.VMEM((length, local), BF), pltpu.VMEM((length, local), BF),
         pltpu.VMEM((length, local), F32), pltpu.VMEM((length, local), F32), pltpu.VMEM((heads, 8, 2 * length), F32)],
    )
    wgrad_came = exchange(wgrad.reshape(experts, block // n_dp, 4 * local), ("row", "dp"))
    *normed_parts, flat = call(
        partial(normed_kernel, n_col),
        [sds((own, width), BF)] * n_col + [sds((experts + 16, width), F32)],
        [grad_qkv, perm, weight, z_perm, router_local, mix_local, table_local],
        2 * length * local * 3 * (width + length),
    )
    held = dict(enumerate(normed_parts))
    for bit in bits_of(n_col)[:-1]:
        got = {k: swap(held[k | bit], "col", n_col, bit) for k in held if not k & bit}
        held = {k: (held[k].astype(F32) + got[k].astype(F32)).astype(BF) for k in got}
    last = n_col // 2
    normed_came = swap(held[last], "col", n_col, last)
    first_sum = held[0]
    tokens_delta, = call(
        tokens_kernel, [sds((own, width), BF)],
        [first_sum, normed_came, grad_hidden, cot_own, tokens_own, inverse_own, gain_row],
        own * width * 12,
    )
    delta_blocks = gather_rel(tokens_delta, "col", n_col)
    output, = call(
        partial(place_kernel, n_col), [sds((count, width), F32)], [*out_blocks, perm_t, tokens],
        2 * count * count * width,
    )
    grad_tokens, = call(
        partial(place_kernel, n_col), [sds((count, width), F32)], [*delta_blocks, perm_t, cotangent],
        2 * count * count * width,
    )
    summed = jnp.sum(wgrad_came.astype(F32), axis=0).astype(BF)
    summed = in_order(gather_rel(summed, "dp", n_dp), dp).astype(F32)
    grad_qkv_weight = summed[:, : 3 * local].reshape(block, 3, local)
    grad_proj = summed[:, 3 * local :].T

    packed = experts + 8
    most, table = flat[:packed], flat[packed:]
    most = hold(most, first_sum)
    for bit in bits_of(n_col):
        most = most + swap(most, "col", n_col, bit)
    flat = hold(jnp.concatenate([most, table], axis=0), wgrad_came)
    for bit in bits_of(experts):
        flat = flat + swap(flat, DR, experts, bit)
    grad_table = flat[packed : packed + heads, :BUCKETS].T
    grad_router = flat[:experts].T
    grad_mix, grad_norm = flat[experts], flat[experts + 1]
    return (
        output,
        grad_tokens,
        grad_qkv_weight,
        grad_proj,
        grad_table,
        grad_norm,
        grad_mix,
        grad_router,
        grad_in_local[None],
        grad_out_local[None],
    )


def solution(mesh):
    placed = (
        P(("dp", "row"), None),
        P(("dp", "row"), None),
        P(("dp", "row"), None),
        P(),
        P(),
        P("row", None, "col"),
        P("col", "row"),
        P(None, "col"),
        P(),
        P(("dp", "row"), None, "col"),
        P(("dp", "row"), "col", None),
        P(("dp", "row"), None),
    )
    return jax.shard_map(
        body,
        mesh=mesh,
        in_specs=placed,
        out_specs=(
            P(("dp", "row"), None),
            P(("dp", "row"), None),
            P("row", None, "col"),
            P("col", "row"),
            P(None, "col"),
            P(),
            P(),
            P(),
            P(("dp", "row"), None, "col"),
            P(("dp", "row"), "col", None),
        ),
        check_vma=False,
    )
```

profile of v0, /device:TPU:0, one launch (start us, length us, event | category | flops | bytes accessed | tf_op | source)
XLA Modules:
  0.0 247.8 jit_solution(13011871352889546662)
XLA Ops:
  0.7 1.1 copy.46
  1.8 1.1 copy.45
  3.2 4.1 %collective-permute-start.1 = (bf16[192,768]{1,0:T(8,128)(2,1)S(1)}, bf16[192,768]{1,0:T(8,128)(2,1)S(1)}, u32[]{:S(2)}, u32[]{:S(2)}) collective-permute-start(bf16[192,768]{1,0:T(8,128)(2,1)S(1)} %pad_maximum_fusion.refs_0_), channel_id=1, source_target_pairs={{0,8},{4,12},{8,0},{12,4},{1,9},{5,13},{9,1},{13,5},{2,10},{6,14},... | collective-permute-start | bytes 884744 | tf_op jit(solution)/shard_map/ppermute | solution.py:328
  7.3 1.6 collective-permute-start
  9.7 1.0 fusion.19
  10.7 1.2 fusion.4
  11.9 1.2 fusion.2.normed_ref.refs_13_
  13.1 7.6 %collective-permute-done.1.refs_2_ = bf16[192,768]{1,0:T(8,128)(2,1)S(1)} collective-permute-done((bf16[192,768]{1,0:T(8,128)(2,1)S(1)}, bf16[192,768]{1,0:T(8,128)(2,1)S(1)}, u32[]{:S(2)}, u32[]{:S(2)}) %collective-permute-start.1) | collective-permute-done | bytes 294944 | tf_op jit(solution)/shard_map/ppermute | solution.py:328
  21.4 0.9 convolution_bitcast_fusion.off_ref
  22.3 1.1 convolution_convert_fusion
  23.5 5.7 %all-to-all-start = ((bf16[8,32,768]{2,1,0:T(8,128)(2,1)}), bf16[8,32,768]{2,1,0:T(8,128)(2,1)}, u32[]{:S(2)}, u32[]{:S(2)}) async-start(bf16[8,32,768]{2,1,0:T(8,128)(2,1)} %bitcast.7), calls=%async_computation | async-start | bytes 786432 | tf_op jit(solution)/shard_map/all_to_all | solution.py:354
  29.9 2.5 %unpack.1 = (bf16[768,576]{1,0:T(8,128)(2,1)}, bf16[768,192]{1,0:T(8,128)(2,1)}) custom-call(s32[1]{0:T(128)} %bitcast.index_ref, bf16[192,768]{1,0:T(8,128)(2,1)} %copy-done.7, bf16[192,768]{1,0:T(8,128)(2,1)} %copy-done.15, bf16[192,768]{1,0:T(8,128)(2,1)} %copy-done.14, bf16[192,768]{1,0:T(8,128)(2,1)} %collective-permute-done.2.refs_3_), custom_call_target="tpu_custom_call" | custom-call | bytes 2359296 | tf_op jit(solution)/shard_map/unpack/pallas_call | solution.py:406
  32.4 1.5 collective-permute-start.7
  35.7 2.9 %position_bias.1.bias_ref = f32[3,512,512]{2,1,0:T(8,128)} custom-call(f32[3,1024]{1,0:T(4,128)} %convolution_bitcast_fusion.off_ref), custom_call_target="tpu_custom_call" | custom-call | flops 3145728 | bytes 3145728 | tf_op jit(solution)/shard_map/position_bias/pallas_call | solution.py:63
  38.5 2.3 multiply_reduce_fusion
  40.9 2.3 collective-permute-done.7.refs_6_
  43.2 8.5 %shard_map.195 = (bf16[512,576]{1,0:T(8,128)(2,1)}, bf16[512,192]{1,0:T(8,128)(2,1)}, f32[3,512,512]{2,1,0:T(8,128)}, bf16[128,192]{1,0:T(8,128)(2,1)}, bf16[128...) custom-call(bf16[512,768]{1,0:T(8,128)(2,1)} %fusion.2.normed_ref.refs_13_, ...), custom_call_target="tpu_custom_call" | custom-call | flops 754974720 | bytes 9474048 | tf_op jit(solution)/shard_map/pallas_call | solution.py:89
  52.2 1.5 collective-permute-start.4
  53.8 1.5 fusion.15.refs_11_.picked_ref
  56.7 1.6 collective-permute-done.5.refs_3_
  58.9 4.4 %shard_map.196 = (f32[128,768]{1,0:T(8,128)}, f32[128,8]{1,0:T(8,128)}, f32[128,1]{1,0:T(8,128)}, bf16[256,896]{1,0:T(8,128)(2,1)}) custom-call(bf16[128,192]{1,0:T(8,128)(2,1)} %get-tuple-element.66.refs_0_.refs_4_, bf16[128,192]{1,0:T(8,128)(2,1)} %copy-done.28, bf16[128,192]{1,0:T(8,128)(2,1)} %copy-done.29, bf16[128,192]{1,0:T(8,128)(2,1)} %copy-done.30, ...), custom_call_target="tpu_custom_call" | custom-call | flops 201326592 | bytes 2723328 | tf_op jit(solution)/shard_map/pallas_call | solution.py:89
  63.3 20.0 %all_to_all.25 = bf16[8,32,896]{2,1,0:T(8,128)(2,1)} all-to-all(bf16[8,32,896]{2,1,0:T(8,128)(2,1)} %bitcast.49), channel_id=1, replica_groups=mesh['dp'=2,'row'=4,'col'=4] {'dp','row'}, dimensions={0} | all-to-all | bytes 917504 | tf_op jit(solution)/shard_map/all_to_all | solution.py:354
  83.4 1.1 collective-permute-start.11
  84.4 10.5 %collective-permute-done.11.refs_0_ = bf16[256,896]{1,0:T(8,128)(2,1)S(1)} collective-permute-done((bf16[256,896]{1,0:T(8,128)(2,1)}, bf16[256,896]{1,0:T(8,128)(2,1)S(1)}, u32[]{:S(2)}, u32[]{:S(2)}) %collective-permute-start.11) | collective-permute-done | bytes 458784 | tf_op jit(solution)/shard_map/ppermute | solution.py:328
  96.2 1.2 collective-permute-start.16
  98.3 5.1 %shard_map.198 = (bf16[256,768]{1,0:T(8,128)(2,1)}, bf16[256,768]{1,0:T(8,128)(2,1)}, bf16[512,768]{1,0:T(8,128)(2,1)}, f32[512,768]{1,0:T(8,128)}) custom-call(bf16[256,896]{1,0:T(8,128)(2,1)} %copy-done.8, bf16[256,896]{1,0:T(8,128)(2,1)} %copy-done.9, bf16[768,768]{1,0:T(8,128)(2,1)} %bitcast.33, bf16[768,768]{1,0:T(8,128)(2,1)} %bitcast.37), custom_call_target="tpu_custom_call" | custom-call | flops 1207959552 | bytes 6422528 | tf_op jit(solution)/shard_map/pallas_call | solution.py:89
  103.9 3.6 %collective-permute-done.16.refs_2_ = bf16[256,768]{1,0:T(8,128)(2,1)} collective-permute-done((bf16[256,768]{1,0:T(8,128)(2,1)}, bf16[256,768]{1,0:T(8,128)(2,1)}, u32[]{:S(2)}, u32[]{:S(2)}) %collective-permute-start.16) | collective-permute-done | bytes 393248 | tf_op jit(solution)/shard_map/ppermute | solution.py:328
  107.5 5.1 %shard_map.197 = (bf16[256,768]{1,0:T(8,128)(2,1)}, bf16[256,768]{1,0:T(8,128)(2,1)}, bf16[512,768]{1,0:T(8,128)(2,1)}, f32[512,768]{1,0:T(8,128)}) custom-call(bf16[256,896]{1,0:T(8,128)(2,1)} %bitcast.10.refs_0_, bf16[256,896]{1,0:T(8,128)(2,1)} %collective-permute-done.9.refs_1_, bf16[768,768]{1,0:T(8,128)(2,1)} %bitcast.34, bf16[768,768]{1,0:T(8,128)(2,1)} %bitcast.38), custom_call_target="tpu_custom_call" | custom-call | flops 1207959552 | bytes 6422528 | tf_op jit(solution)/shard_map/pallas_call | solution.py:89
  113.2 1.9 add_convert_fusion.3
  115.0 1.2 collective-permute-start.14
  116.3 5.4 %shard_map.200 = (bf16[256,768]{1,0:T(8,128)(2,1)}, bf16[256,768]{1,0:T(8,128)(2,1)}, bf16[512,768]{1,0:T(8,128)(2,1)}, bf16[512,768]{1,0:T(8,128)(2,1)}, bf16[512,768]{1,0:T(8,128)(2,1)}) custom-call(bf16[256,896]{1,0:T(8,128)(2,1)} %copy-done.8, bf16[256,896]{1,0:T(8,128)(2,1)} %copy-done.9, bf16[256,768]{1,0:T(8,128)(2,1)} %collective-permute-done.16.refs_2_, ...), custom_call_target="tpu_custom_call" | custom-call | flops 1207959552 | bytes 8781824 | tf_op jit(solution)/shard_map/pallas_call | solution.py:89
  121.7 5.5 %shard_map.199 = (bf16[256,768]{1,0:T(8,128)(2,1)}, bf16[256,768]{1,0:T(8,128)(2,1)}, bf16[512,768]{1,0:T(8,128)(2,1)}, bf16[512,768]{1,0:T(8,128)(2,1)}, bf16[512,768]{1,0:T(8,128)(2,1)}) custom-call(bf16[256,896]{1,0:T(8,128)(2,1)} %bitcast.10.refs_0_, bf16[256,896]{1,0:T(8,128)(2,1)} %collective-permute-done.9.refs_1_, bf16[256,768]{1,0:T(8,128)(2,1)} %bitcast.8.refs_2_, ...), custom_call_target="tpu_custom_call" | custom-call | flops 1207959552 | bytes 8781824 | tf_op jit(solution)/shard_map/pallas_call | solution.py:89
  127.7 2.0 add_convert_fusion.2
  129.7 3.5 %all-to-all-start.2 = ((bf16[8,32,768]{2,1,0:T(8,128)(2,1)}), bf16[8,32,768]{2,1,0:T(8,128)(2,1)S(1)}, u32[]{:S(2)}, u32[]{:S(2)}) async-start(bf16[8,32,768]{2,1,0:T(8,128)(2,1)} %bitcast.46), calls=%async_computation.2 | async-start | bytes 786432 | tf_op jit(solution)/shard_map/all_to_all | solution.py:354
  133.2 1.3 add_convert_fusion.1
  135.3 2.2 fusion.12.cot_ref
  137.6 8.0 %collective-permute-done.20 = bf16[256,768]{1,0:T(8,128)(2,1)S(1)} collective-permute-done((bf16[256,768]{1,0:T(8,128)(2,1)S(1)}, bf16[256,768]{1,0:T(8,128)(2,1)S(1)}, u32[]{:S(2)}, u32[]{:S(2)}) %collective-permute-start.20) | collective-permute-done | bytes 393248 | tf_op jit(solution)/shard_map/ppermute | solution.py:328
  145.6 1.9 add_convert_fusion
  147.5 5.6 %all-to-all-start.3 = ((bf16[8,32,768]{2,1,0:T(8,128)(2,1)}), bf16[8,32,768]{2,1,0:T(8,128)(2,1)S(1)}, u32[]{:S(2)}, u32[]{:S(2)}) async-start(bf16[8,32,768]{2,1,0:T(8,128)(2,1)} %bitcast.15), calls=%async_computation.3 | async-start | bytes 786432 | tf_op jit(solution)/shard_map/all_to_all | solution.py:354
  153.1 1.3 broadcast_multiply_fusion.z_ref
  154.4 4.7 %shard_map.202 = f32[768,768]{1,0:T(8,128)} custom-call(bf16[512,768]{1,0:T(8,128)(2,1)} %get-tuple-element.84.refs_0_, bf16[512,768]{1,0:T(8,128)(2,1)} %get-tuple-element.85.refs_1_, bf16[512,768]{1,0:T(8,128)(2,1)} %get-tuple-element.86.refs_2_, bf16[512,768]{1,0:T(8,128)(2,1)} %get-tuple-element.87.refs_3_), custom_call_target="tpu_custom_call" | custom-call | flops 1207959552 | bytes 5505024 | tf_op jit(solution)/shard_map/pallas_call | solution.py:89
  159.1 4.7 %shard_map.201 = f32[768,768]{1,0:T(8,128)} custom-call(bf16[512,768]{1,0:T(8,128)(2,1)} %get-tuple-element.79.refs_0_, bf16[512,768]{1,0:T(8,128)(2,1)} %get-tuple-element.81.refs_1_, bf16[512,768]{1,0:T(8,128)(2,1)} %get-tuple-element.82.refs_2_, bf16[512,768]{1,0:T(8,128)(2,1)} %get-tuple-element.83.refs_3_), custom_call_target="tpu_custom_call" | custom-call | flops 1207959552 | bytes 5505024 | tf_op jit(solution)/shard_map/pallas_call | solution.py:89
  163.8 1.0 all-to-all-done.3
  165.5 3.7 %shard_map.203 = (f32[128,768]{1,0:T(8,128)}, bf16[128,768]{1,0:T(8,128)(2,1)}, bf16[128,768]{1,0:T(8,128)(2,1)}, f32[8,768]{1,0:T(8,128)}, f32[1,768]{1,0:T(1,128)}) custom-call(bf16[256,768]{1,0:T(8,128)(2,1)} %bitcast.44, bf16[256,768]{1,0:T(8,128)(2,1)} %bitcast.45, bf16[256,128]{1,0:T(8,128)(2,1)} %convolution_convert_fusion.1.refs_12_.slot_ref, ...), custom_call_target="tpu_custom_call" | custom-call | flops 100663296 | bytes 2882048 | tf_op jit(solution)/shard_map/pallas_call | solution.py:89
  170.0 5.1 %collective-permute-done.22.refs_2_ = bf16[128,768]{1,0:T(8,128)(2,1)S(1)} collective-permute-done((bf16[128,768]{1,0:T(8,128)(2,1)}, bf16[128,768]{1,0:T(8,128)(2,1)S(1)}, u32[]{:S(2)}, u32[]{:S(2)}) %collective-permute-start.22) | collective-permute-done | bytes 196640 | tf_op jit(solution)/shard_map/ppermute | solution.py:328
  175.1 1.4 collective-permute-done.23.refs_3_
  177.2 11.2 %shard_map.205 = (bf16[768,768]{1,0:T(8,128)(2,1)}, bf16[512,576]{1,0:T(8,128)(2,1)}, f32[8,128]{1,0:T(8,128)}) custom-call(bf16[128,768]{1,0:T(8,128)(2,1)} %get-tuple-element.99.refs_0_, bf16[128,768]{1,0:T(8,128)(2,1)} %copy-done.25, bf16[128,768]{1,0:T(8,128)(2,1)} %copy-done.24, bf16[128,768]{1,0:T(8,128)(2,1)} %copy-done.26, ...), custom_call_target="tpu_custom_call" | custom-call | flops 1258291200 | bytes 8818688 | tf_op jit(solution)/shard_map/pallas_call | solution.py:89
  188.4 5.0 %all-to-all-start.4 = ((bf16[8,96,768]{2,1,0:T(8,128)(2,1)}), bf16[8,96,768]{2,1,0:T(8,128)(2,1)S(1)}, u32[]{:S(2)}, u32[]{:S(2)}) async-start(bf16[8,96,768]{2,1,0:T(8,128)(2,1)} %bitcast.47), calls=%async_computation.4 | async-start | bytes 2359296 | tf_op jit(solution)/shard_map/all_to_all | solution.py:354
  194.0 4.6 %shard_map.206 = (bf16[128,768]{1,0:T(8,128)(2,1)}, bf16[128,768]{1,0:T(8,128)(2,1)}, bf16[128,768]{1,0:T(8,128)(2,1)}, bf16[128,768]{1,0:T(8,128)(2,1)}, f32[24,768]{1,0:T(8,128)}) custom-call(bf16[512,576]{1,0:T(8,128)(2,1)} %get-tuple-element.104.gq_ref, bf16[512,512]{1,0:T(8,128)(2,1)} %get-tuple-element.159.perm_ref, ...), custom_call_target="tpu_custom_call" | custom-call | flops 754974720 | bytes 4463616 | tf_op jit(solution)/shard_map/pallas_call | solution.py:89
  200.4 1.0 add_convert_fusion.4
  201.4 1.3 collective-permute-start.29
  202.7 1.7 add_convert_fusion.5.mine_ref
  204.3 6.5 %collective-permute-done.29.came_ref = bf16[128,768]{1,0:T(8,128)(2,1)S(1)} collective-permute-done((bf16[128,768]{1,0:T(8,128)(2,1)S(1)}, bf16[128,768]{1,0:T(8,128)(2,1)S(1)}, u32[]{:S(2)}, u32[]{:S(2)}) %collective-permute-start.29) | collective-permute-done | bytes 196640 | tf_op jit(solution)/shard_map/ppermute | solution.py:328
  211.6 2.4 shard_map.207.refs_0_
  216.0 1.3 collective-permute-start.35
  217.3 3.9 %collective-permute-done.31.refs_2_ = bf16[128,768]{1,0:T(8,128)(2,1)S(1)} collective-permute-done((bf16[128,768]{1,0:T(8,128)(2,1)}, bf16[128,768]{1,0:T(8,128)(2,1)S(1)}, u32[]{:S(2)}, u32[]{:S(2)}) %collective-permute-start.31) | collective-permute-done | bytes 196640 | tf_op jit(solution)/shard_map/ppermute | solution.py:328
  222.5 1.5 collective-permute-start.33
  224.0 1.5 collective-permute-start.36
  226.2 3.8 %shard_map.204 = f32[512,768]{1,0:T(8,128)} custom-call(bf16[128,768]{1,0:T(8,128)(2,1)} %get-tuple-element.100.refs_0_, bf16[128,768]{1,0:T(8,128)(2,1)} %copy-done.19, bf16[128,768]{1,0:T(8,128)(2,1)} %copy-done.17, bf16[128,768]{1,0:T(8,128)(2,1)} %copy-done.20, bf16[512,512]{1,0:T(8,128)(2,1)} %get-tuple-element.158.refs_4_.refs_9_, bf16[512,768]{1,0:T(8,128)(2,1)} %refs_5_.2), custom_call_target="tpu_custom_call" | custom-call | flops 402653184 | bytes 3670016 | tf_op jit(solution)/shard_map/pallas_call | solution.py:89
  231.3 4.0 %shard_map.208 = f32[512,768]{1,0:T(8,128)} custom-call(bf16[128,768]{1,0:T(8,128)(2,1)} %shard_map.207.refs_0_, bf16[128,768]{1,0:T(8,128)(2,1)} %copy-done.21, bf16[128,768]{1,0:T(8,128)(2,1)} %copy-done.18, bf16[128,768]{1,0:T(8,128)(2,1)} %copy-done.22, bf16[512,512]{1,0:T(8,128)(2,1)} %get-tuple-element.158.refs_4_.refs_9_, f32[512,768]{1,0:T(8,128)} %refs_5_.3), custom_call_target="tpu_custom_call" | custom-call | flops 402653184 | bytes 4456448 | tf_op jit(solution)/shard_map/pallas_call | solution.py:89
  235.4 2.4 collective-permute-start.37
  238.7 2.8 %collective-permute-done.37 = f32[24,768]{1,0:T(8,128)S(1)} collective-permute-done((f32[24,768]{1,0:T(8,128)S(1)}, f32[24,768]{1,0:T(8,128)S(1)}, u32[]{:S(2)}, u32[]{:S(2)}) %collective-permute-start.37) | collective-permute-done | bytes 73760 | tf_op jit(solution)/shard_map/ppermute | solution.py:328
  242.5 1.1 copy.53
  243.6 2.4 collective-permute-done.38
  (165 shorter events, 25.7 us)
Async XLA Ops:
  0.6 20.7 %copy-start = (f32[32,3]{0,1:T(4,128)S(1)}, f32[32,3]{0,1:T(4,128)}, u32[]{:S(2)}) copy-start(f32[32,3]{0,1:T(4,128)} %param.19) | copy-start | bytes 1156
  0.7 8.2 %copy-start.31 = (s32[512,1]{0,1:T(1,128)S(1)}, s32[512,1]{0,1:T(1,128)}, u32[]{:S(2)}) copy-start(s32[512,1]{0,1:T(1,128)} %param.14) | copy-start | bytes 6148
  0.7 8.8 %copy-start.2 = (bf16[512,768]{1,0:T(8,128)(2,1)S(1)}, bf16[512,768]{1,0:T(8,128)(2,1)}, u32[]{:S(2)}) copy-start(bf16[512,768]{1,0:T(8,128)(2,1)} %refs_5_.2) | copy-start | bytes 2359300
  3.2 9.9 %copy-start.7 = (bf16[192,768]{1,0:T(8,128)(2,1)}, bf16[192,768]{1,0:T(8,128)(2,1)S(1)}, u32[]{:S(2)}) copy-start(bf16[192,768]{1,0:T(8,128)(2,1)S(1)} %pad_maximum_fusion.refs_0_) | copy-start | bytes 884740
  3.2 8.7 %copy-start.32 = (f32[768]{0:T(1024)S(1)}, f32[768]{0:T(1024)}, u32[]{:S(2)}) copy-start(f32[768]{0:T(1024)} %param.15) | copy-start | bytes 9220
  3.2 17.6 %collective-permute-start.1 = (bf16[192,768]{1,0:T(8,128)(2,1)S(1)}, bf16[192,768]{1,0:T(8,128)(2,1)S(1)}, u32[]{:S(2)}, u32[]{:S(2)}) collective-permute-start(bf16[192,768]{1,0:T(8,128)(2,1)S(1)} %pad_maximum_fusion.refs_0_), channel_id=1, source_target_pairs={{0,8},{4,12},{8,0},{12,4},{1,9},{5,13},{9,1},{13,5},{2,10},{6,14},... | collective-permute-start | bytes 884744 | tf_op jit(solution)/shard_map/ppermute | solution.py:328
  7.3 21.9 %collective-permute-start = (bf16[192,768]{1,0:T(8,128)(2,1)S(1)}, bf16[192,768]{1,0:T(8,128)(2,1)S(1)}, u32[]{:S(2)}, u32[]{:S(2)}) collective-permute-start(bf16[192,768]{1,0:T(8,128)(2,1)S(1)} %pad_maximum_fusion.refs_0_), channel_id=1, source_target_pairs={{0,4},{4,0},{8,12},{12,8},{1,5},{5,1},{9,13},{13,9},{2,6},{6,2},{1... | collective-permute-start | bytes 884744 | tf_op jit(solution)/shard_map/ppermute | solution.py:328
  10.7 11.6 %copy-start.1 = (f32[512,768]{1,0:T(8,128)S(1)}, f32[512,768]{1,0:T(8,128)}, u32[]{:S(2)}) copy-start(f32[512,768]{1,0:T(8,128)} %refs_5_.3) | copy-start | bytes 4718596
  11.9 22.0 %copy-start.10 = (pred[512,512]{1,0:T(32,128)(4,1)}, pred[512,512]{1,0:T(32,128)(4,1)S(1)}, u32[]{:S(2)}) copy-start(pred[512,512]{1,0:T(32,128)(4,1)S(1)} %get-tuple-element.160) | copy-start | bytes 786436
  20.8 8.5 %copy-start.14 = (bf16[192,768]{1,0:T(8,128)(2,1)}, bf16[192,768]{1,0:T(8,128)(2,1)S(1)}, u32[]{:S(2)}) copy-start(bf16[192,768]{1,0:T(8,128)(2,1)S(1)} %collective-permute-done.1.refs_2_) | copy-start | bytes 884740
  20.8 8.5 %collective-permute-start.2 = (bf16[192,768]{1,0:T(8,128)(2,1)S(1)}, bf16[192,768]{1,0:T(8,128)(2,1)}, u32[]{:S(2)}, u32[]{:S(2)}) collective-permute-start(bf16[192,768]{1,0:T(8,128)(2,1)S(1)} %collective-permute-done.1.refs_2_), channel_id=1, source_target_pairs={{0,4},{4,0},{8,12},{12,8},{1,5},{5,1},{9,13},{13,9},{2,6},{6,2},{1... | collective-permute-start | bytes 884744 | tf_op jit(solution)/shard_map/ppermute | solution.py:328
  23.5 11.4 %copy-start.33 = (s32[1,512]{1,0:T(1,128)S(1)}, s32[1,512]{1,0:T(1,128)}, u32[]{:S(2)}) copy-start(s32[1,512]{1,0:T(1,128)} %seg_row_ref.1) | copy-start | bytes 6148
  23.5 39.9 %all-to-all-start = ((bf16[8,32,768]{2,1,0:T(8,128)(2,1)}), bf16[8,32,768]{2,1,0:T(8,128)(2,1)}, u32[]{:S(2)}, u32[]{:S(2)}) async-start(bf16[8,32,768]{2,1,0:T(8,128)(2,1)} %bitcast.7), calls=%async_computation | async-start | bytes 786432 | tf_op jit(solution)/shard_map/all_to_all | solution.py:354
  32.4 10.8 %collective-permute-start.7 = (bf16[768,192]{1,0:T(8,128)(2,1)}, bf16[768,192]{1,0:T(8,128)(2,1)}, u32[]{:S(2)}, u32[]{:S(2)}) collective-permute-start(bf16[768,192]{1,0:T(8,128)(2,1)} %get-tuple-element.70.refs_4_.refs_8_), channel_id=1, source_target_pairs={{0,2},{1,3},{2,0},{3,1},{4,6},{5,7},{6,4},{7,5},{8,10},{9,11},{10,... | collective-permute-start | bytes 884744 | tf_op jit(solution)/shard_map/ppermute | solution.py:328
  38.5 2.3 copy-start.4
  40.9 17.4 %collective-permute-start.6 = (bf16[768,192]{1,0:T(8,128)(2,1)S(1)}, bf16[768,192]{1,0:T(8,128)(2,1)}, u32[]{:S(2)}, u32[]{:S(2)}) collective-permute-start(bf16[768,192]{1,0:T(8,128)(2,1)S(1)} %copy-done.4), channel_id=1, source_target_pairs={{0,1},{1,0},{2,3},{3,2},{4,5},{5,4},{6,7},{7,6},{8,9},{9,8},{10,11... | collective-permute-start | bytes 884744 | tf_op jit(solution)/shard_map/ppermute | solution.py:328
  43.2 15.1 %collective-permute-start.8 = (bf16[768,192]{1,0:T(8,128)(2,1)}, bf16[768,192]{1,0:T(8,128)(2,1)}, u32[]{:S(2)}, u32[]{:S(2)}) collective-permute-start(bf16[768,192]{1,0:T(8,128)(2,1)} %collective-permute-done.7.refs_6_), channel_id=1, source_target_pairs={{0,1},{1,0},{2,3},{3,2},{4,5},{5,4},{6,7},{7,6},{8,9},{9,8},{10,11... | collective-permute-start | bytes 884744 | tf_op jit(solution)/shard_map/ppermute | solution.py:328
  43.2 12.1 %copy-start.34 = (f32[768]{0:T(1024)S(1)}, f32[768]{0:T(1024)}, u32[]{:S(2)}) copy-start(f32[768]{0:T(1024)} %param.16) | copy-start | bytes 9220
  43.2 12.7 %copy-start.3 = (f32[512,768]{1,0:T(8,128)S(1)}, f32[512,768]{1,0:T(8,128)}, u32[]{:S(2)}) copy-start(f32[512,768]{1,0:T(8,128)} %get-tuple-element.89) | copy-start | bytes 4718596
  51.7 4.9 %collective-permute-start.3 = (bf16[128,192]{1,0:T(8,128)(2,1)}, bf16[128,192]{1,0:T(8,128)(2,1)S(1)}, u32[]{:S(2)}, u32[]{:S(2)}) collective-permute-start(bf16[128,192]{1,0:T(8,128)(2,1)} %get-tuple-element.67.refs_5_), channel_id=1, source_target_pairs={{0,1},{1,0},{2,3},{3,2},{4,5},{5,4},{6,7},{7,6},{8,9},{9,8},{10,11... | collective-permute-start | bytes 147464 | tf_op jit(solution)/shard_map/ppermute | solution.py:328
  52.2 4.5 %collective-permute-start.4 = (bf16[128,192]{1,0:T(8,128)(2,1)}, bf16[128,192]{1,0:T(8,128)(2,1)S(1)}, u32[]{:S(2)}, u32[]{:S(2)}) collective-permute-start(bf16[128,192]{1,0:T(8,128)(2,1)} %get-tuple-element.68.refs_6_), channel_id=1, source_target_pairs={{0,2},{1,3},{2,0},{3,1},{4,6},{5,7},{6,4},{7,5},{8,10},{9,11},{10,... | collective-permute-start | bytes 147464 | tf_op jit(solution)/shard_map/ppermute | solution.py:328
  53.8 4.5 %collective-permute-start.5 = (bf16[128,192]{1,0:T(8,128)(2,1)}, bf16[128,192]{1,0:T(8,128)(2,1)S(1)}, u32[]{:S(2)}, u32[]{:S(2)}) collective-permute-start(bf16[128,192]{1,0:T(8,128)(2,1)} %get-tuple-element.69.refs_7_), channel_id=1, source_target_pairs={{0,3},{1,2},{2,1},{3,0},{4,7},{5,6},{6,5},{7,4},{8,11},{9,10},{10,... | collective-permute-start | bytes 147464 | tf_op jit(solution)/shard_map/ppermute | solution.py:328
  83.4 11.5 %collective-permute-start.11 = (bf16[256,896]{1,0:T(8,128)(2,1)}, bf16[256,896]{1,0:T(8,128)(2,1)S(1)}, u32[]{:S(2)}, u32[]{:S(2)}) collective-permute-start(bf16[256,896]{1,0:T(8,128)(2,1)} %bitcast.10.refs_0_), channel_id=1, source_target_pairs={{0,2},{1,3},{2,0},{3,1},{4,6},{5,7},{6,4},{7,5},{8,10},{9,11},{10,... | collective-permute-start | bytes 1376264 | tf_op jit(solution)/shard_map/ppermute | solution.py:328
  95.7 1.8 collective-permute-start.12
  95.7 11.9 %collective-permute-start.9 = (bf16[256,896]{1,0:T(8,128)(2,1)}, bf16[256,896]{1,0:T(8,128)(2,1)}, u32[]{:S(2)}, u32[]{:S(2)}) collective-permute-start(bf16[256,896]{1,0:T(8,128)(2,1)} %bitcast.10.refs_0_), channel_id=1, source_target_pairs={{0,1},{1,0},{2,3},{3,2},{4,5},{5,4},{6,7},{7,6},{8,9},{9,8},{10,11... | collective-permute-start | bytes 1376264 | tf_op jit(solution)/shard_map/ppermute | solution.py:328
  96.2 11.3 %collective-permute-start.16 = (bf16[256,768]{1,0:T(8,128)(2,1)}, bf16[256,768]{1,0:T(8,128)(2,1)}, u32[]{:S(2)}, u32[]{:S(2)}) collective-permute-start(bf16[256,768]{1,0:T(8,128)(2,1)} %bitcast.8.refs_2_), channel_id=1, source_target_pairs={{0,2},{1,3},{2,0},{3,1},{4,6},{5,7},{6,4},{7,5},{8,10},{9,11},{10,... | collective-permute-start | bytes 1179656 | tf_op jit(solution)/shard_map/ppermute | solution.py:328
  103.4 9.8 %copy-start.13 = (bf16[256,768]{1,0:T(8,128)(2,1)S(1)}, bf16[256,768]{1,0:T(8,128)(2,1)}, u32[]{:S(2)}) copy-start(bf16[256,768]{1,0:T(8,128)(2,1)} %get-tuple-element.76) | copy-start | bytes 1179652
  103.4 9.8 %collective-permute-start.13 = (bf16[256,768]{1,0:T(8,128)(2,1)}, bf16[256,768]{1,0:T(8,128)(2,1)}, u32[]{:S(2)}, u32[]{:S(2)}) collective-permute-start(bf16[256,768]{1,0:T(8,128)(2,1)} %get-tuple-element.77), channel_id=1, source_target_pairs={{0,1},{1,0},{2,3},{3,2},{4,5},{5,4},{6,7},{7,6},{8,9},{9,8},{10,11... | collective-permute-start | bytes 1179656 | tf_op jit(solution)/shard_map/ppermute | solution.py:328
  103.5 18.2 %collective-permute-start.15 = (bf16[256,768]{1,0:T(8,128)(2,1)}, bf16[256,768]{1,0:T(8,128)(2,1)}, u32[]{:S(2)}, u32[]{:S(2)}) collective-permute-start(bf16[256,768]{1,0:T(8,128)(2,1)} %bitcast.8.refs_2_), channel_id=1, source_target_pairs={{0,1},{1,0},{2,3},{3,2},{4,5},{5,4},{6,7},{7,6},{8,9},{9,8},{10,11... | collective-permute-start | bytes 1179656 | tf_op jit(solution)/shard_map/ppermute | solution.py:328
  107.5 8.7 %collective-permute-start.17 = (bf16[256,768]{1,0:T(8,128)(2,1)}, bf16[256,768]{1,0:T(8,128)(2,1)}, u32[]{:S(2)}, u32[]{:S(2)}) collective-permute-start(bf16[256,768]{1,0:T(8,128)(2,1)} %collective-permute-done.16.refs_2_), channel_id=1, source_target_pairs={{0,1},{1,0},{2,3},{3,2},{4,5},{5,4},{6,7},{7,6},{8,9},{9,8},{10,11... | collective-permute-start | bytes 1179656 | tf_op jit(solution)/shard_map/ppermute | solution.py:328
  112.7 15.0 %collective-permute-start.10 = (bf16[256,768]{1,0:T(8,128)(2,1)}, bf16[256,768]{1,0:T(8,128)(2,1)}, u32[]{:S(2)}, u32[]{:S(2)}) collective-permute-start(bf16[256,768]{1,0:T(8,128)(2,1)} %get-tuple-element.75), channel_id=1, source_target_pairs={{0,1},{1,0},{2,3},{3,2},{4,5},{5,4},{6,7},{7,6},{8,9},{9,8},{10,11... | collective-permute-start | bytes 1179656 | tf_op jit(solution)/shard_map/ppermute | solution.py:328
  115.0 12.7 %collective-permute-start.14 = (bf16[256,768]{1,0:T(8,128)(2,1)}, bf16[256,768]{1,0:T(8,128)(2,1)}, u32[]{:S(2)}, u32[]{:S(2)}) collective-permute-start(bf16[256,768]{1,0:T(8,128)(2,1)} %add_convert_fusion.3), channel_id=1, source_target_pairs={{0,2},{1,3},{2,0},{3,1},{4,6},{5,7},{6,4},{7,5},{8,10},{9,11},{10,... | collective-permute-start | bytes 1179656 | tf_op jit(solution)/shard_map/ppermute | solution.py:328
  121.7 11.5 %collective-permute-start.19 = (bf16[256,768]{1,0:T(8,128)(2,1)}, bf16[256,768]{1,0:T(8,128)(2,1)}, u32[]{:S(2)}, u32[]{:S(2)}) collective-permute-start(bf16[256,768]{1,0:T(8,128)(2,1)} %get-tuple-element.94), channel_id=1, source_target_pairs={{0,1},{1,0},{2,3},{3,2},{4,5},{5,4},{6,7},{7,6},{8,9},{9,8},{10,11... | collective-permute-start | bytes 1179656 | tf_op jit(solution)/shard_map/ppermute | solution.py:328
  121.7 6.0 %copy-start.11 = (bf16[256,768]{1,0:T(8,128)(2,1)S(1)}, bf16[256,768]{1,0:T(8,128)(2,1)}, u32[]{:S(2)}) copy-start(bf16[256,768]{1,0:T(8,128)(2,1)} %get-tuple-element.74) | copy-start | bytes 1179652
  127.2 10.4 %collective-permute-start.18 = (bf16[256,768]{1,0:T(8,128)(2,1)}, bf16[256,768]{1,0:T(8,128)(2,1)}, u32[]{:S(2)}, u32[]{:S(2)}) collective-permute-start(bf16[256,768]{1,0:T(8,128)(2,1)} %get-tuple-element.92), channel_id=1, source_target_pairs={{0,1},{1,0},{2,3},{3,2},{4,5},{5,4},{6,7},{7,6},{8,9},{9,8},{10,11... | collective-permute-start | bytes 1179656 | tf_op jit(solution)/shard_map/ppermute | solution.py:328
  129.7 17.7 %all-to-all-start.2 = ((bf16[8,32,768]{2,1,0:T(8,128)(2,1)}), bf16[8,32,768]{2,1,0:T(8,128)(2,1)S(1)}, u32[]{:S(2)}, u32[]{:S(2)}) async-start(bf16[8,32,768]{2,1,0:T(8,128)(2,1)} %bitcast.46), calls=%async_computation.2 | async-start | bytes 786432 | tf_op jit(solution)/shard_map/all_to_all | solution.py:354
  133.2 12.4 %copy-start.12 = (bf16[256,768]{1,0:T(8,128)(2,1)S(1)}, bf16[256,768]{1,0:T(8,128)(2,1)}, u32[]{:S(2)}) copy-start(bf16[256,768]{1,0:T(8,128)(2,1)} %get-tuple-element.91) | copy-start | bytes 1179652
  134.5 11.1 %collective-permute-start.20 = (bf16[256,768]{1,0:T(8,128)(2,1)S(1)}, bf16[256,768]{1,0:T(8,128)(2,1)S(1)}, u32[]{:S(2)}, u32[]{:S(2)}) collective-permute-start(bf16[256,768]{1,0:T(8,128)(2,1)S(1)} %add_convert_fusion.1), channel_id=1, source_target_pairs={{0,2},{1,3},{2,0},{3,1},{4,6},{5,7},{6,4},{7,5},{8,10},{9,11},{10,... | collective-permute-start | bytes 1179656 | tf_op jit(solution)/shard_map/ppermute | solution.py:328
  137.6 15.5 %copy-start.35 = (f32[512]{0:T(512)S(1)}, f32[512]{0:T(512)}, u32[]{:S(2)}) copy-start(f32[512]{0:T(512)} %get-tuple-element.161) | copy-start | bytes 6148
  147.5 7.0 %copy-start.5 = (bf16[8,32,768]{2,1,0:T(8,128)(2,1)}, bf16[8,32,768]{2,1,0:T(8,128)(2,1)S(1)}, u32[]{:S(2)}) copy-start(bf16[8,32,768]{2,1,0:T(8,128)(2,1)S(1)} %all-to-all-done.2) | copy-start | bytes 1179652
  147.5 17.3 %all-to-all-start.3 = ((bf16[8,32,768]{2,1,0:T(8,128)(2,1)}), bf16[8,32,768]{2,1,0:T(8,128)(2,1)S(1)}, u32[]{:S(2)}, u32[]{:S(2)}) async-start(bf16[8,32,768]{2,1,0:T(8,128)(2,1)} %bitcast.15), calls=%async_computation.3 | async-start | bytes 786432 | tf_op jit(solution)/shard_map/all_to_all | solution.py:354
  169.2 5.9 %collective-permute-start.22 = (bf16[128,768]{1,0:T(8,128)(2,1)}, bf16[128,768]{1,0:T(8,128)(2,1)S(1)}, u32[]{:S(2)}, u32[]{:S(2)}) collective-permute-start(bf16[128,768]{1,0:T(8,128)(2,1)} %get-tuple-element.99.refs_0_), channel_id=1, source_target_pairs={{0,2},{1,3},{2,0},{3,1},{4,6},{5,7},{6,4},{7,5},{8,10},{9,11},{10,... | collective-permute-start | bytes 589832 | tf_op jit(solution)/shard_map/ppermute | solution.py:328
  170.0 5.1 %collective-permute-start.21 = (bf16[128,768]{1,0:T(8,128)(2,1)}, bf16[128,768]{1,0:T(8,128)(2,1)S(1)}, u32[]{:S(2)}, u32[]{:S(2)}) collective-permute-start(bf16[128,768]{1,0:T(8,128)(2,1)} %get-tuple-element.99.refs_0_), channel_id=1, source_target_pairs={{0,1},{1,0},{2,3},{3,2},{4,5},{5,4},{6,7},{7,6},{8,9},{9,8},{10,11... | collective-permute-start | bytes 589832 | tf_op jit(solution)/shard_map/ppermute | solution.py:328
  175.1 1.4 collective-permute-start.23
  188.4 33.9 %all-to-all-start.4 = ((bf16[8,96,768]{2,1,0:T(8,128)(2,1)}), bf16[8,96,768]{2,1,0:T(8,128)(2,1)S(1)}, u32[]{:S(2)}, u32[]{:S(2)}) async-start(bf16[8,96,768]{2,1,0:T(8,128)(2,1)} %bitcast.47), calls=%async_computation.4 | async-start | bytes 2359296 | tf_op jit(solution)/shard_map/all_to_all | solution.py:354
  194.0 5.3 %copy-start.16 = (bf16[128,768]{1,0:T(8,128)(2,1)S(1)}, bf16[128,768]{1,0:T(8,128)(2,1)}, u32[]{:S(2)}) copy-start(bf16[128,768]{1,0:T(8,128)(2,1)} %get-tuple-element.100.refs_0_) | copy-start | bytes 589828
  198.6 16.2 %copy-start.27 = (f32[24,768]{1,0:T(8,128)S(1)}, f32[24,768]{1,0:T(8,128)}, u32[]{:S(2)}) copy-start(f32[24,768]{1,0:T(8,128)} %get-tuple-element.115) | copy-start | bytes 221188
  198.6 1.8 collective-permute-start.28
  199.4 15.9 %collective-permute-start.25 = (bf16[128,768]{1,0:T(8,128)(2,1)S(1)}, bf16[128,768]{1,0:T(8,128)(2,1)S(1)}, u32[]{:S(2)}, u32[]{:S(2)}) collective-permute-start(bf16[128,768]{1,0:T(8,128)(2,1)S(1)} %copy-done.16), channel_id=1, source_target_pairs={{0,2},{1,3},{2,0},{3,1},{4,6},{5,7},{6,4},{7,5},{8,10},{9,11},{10,... | collective-permute-start | bytes 589832 | tf_op jit(solution)/shard_map/ppermute | solution.py:328
  200.2 2.5 %collective-permute-start.27 = (bf16[128,768]{1,0:T(8,128)(2,1)}, bf16[128,768]{1,0:T(8,128)(2,1)S(1)}, u32[]{:S(2)}, u32[]{:S(2)}) collective-permute-start(bf16[128,768]{1,0:T(8,128)(2,1)} %get-tuple-element.110), channel_id=1, source_target_pairs={{0,1},{1,0},{2,3},{3,2},{4,5},{5,4},{6,7},{7,6},{8,9},{9,8},{10,11... | collective-permute-start | bytes 589832 | tf_op jit(solution)/shard_map/ppermute | solution.py:328
  201.4 9.5 %collective-permute-start.29 = (bf16[128,768]{1,0:T(8,128)(2,1)S(1)}, bf16[128,768]{1,0:T(8,128)(2,1)S(1)}, u32[]{:S(2)}, u32[]{:S(2)}) collective-permute-start(bf16[128,768]{1,0:T(8,128)(2,1)S(1)} %add_convert_fusion.4), channel_id=1, source_target_pairs={{0,2},{1,3},{2,0},{3,1},{4,6},{5,7},{6,4},{7,5},{8,10},{9,11},{10,... | collective-permute-start | bytes 589832 | tf_op jit(solution)/shard_map/ppermute | solution.py:328
  214.0 7.2 %collective-permute-start.31 = (bf16[128,768]{1,0:T(8,128)(2,1)}, bf16[128,768]{1,0:T(8,128)(2,1)S(1)}, u32[]{:S(2)}, u32[]{:S(2)}) collective-permute-start(bf16[128,768]{1,0:T(8,128)(2,1)} %shard_map.207.refs_0_), channel_id=1, source_target_pairs={{0,2},{1,3},{2,0},{3,1},{4,6},{5,7},{6,4},{7,5},{8,10},{9,11},{10,... | collective-permute-start | bytes 589832 | tf_op jit(solution)/shard_map/ppermute | solution.py:328
  214.8 1.2 collective-permute-start.34
  214.8 9.2 %collective-permute-start.24 = (bf16[128,768]{1,0:T(8,128)(2,1)S(1)}, bf16[128,768]{1,0:T(8,128)(2,1)S(1)}, u32[]{:S(2)}, u32[]{:S(2)}) collective-permute-start(bf16[128,768]{1,0:T(8,128)(2,1)S(1)} %copy-done.16), channel_id=1, source_target_pairs={{0,1},{1,0},{2,3},{3,2},{4,5},{5,4},{6,7},{7,6},{8,9},{9,8},{10,11... | collective-permute-start | bytes 589832 | tf_op jit(solution)/shard_map/ppermute | solution.py:328
  215.3 10.2 %copy-start.17 = (bf16[128,768]{1,0:T(8,128)(2,1)}, bf16[128,768]{1,0:T(8,128)(2,1)S(1)}, u32[]{:S(2)}) copy-start(bf16[128,768]{1,0:T(8,128)(2,1)S(1)} %collective-permute-done.25.refs_2_) | copy-start | bytes 589828
  215.3 10.2 %collective-permute-start.26 = (bf16[128,768]{1,0:T(8,128)(2,1)S(1)}, bf16[128,768]{1,0:T(8,128)(2,1)S(1)}, u32[]{:S(2)}, u32[]{:S(2)}) collective-permute-start(bf16[128,768]{1,0:T(8,128)(2,1)S(1)} %collective-permute-done.25.refs_2_), channel_id=1, source_target_pairs={{0,1},{1,0},{2,3},{3,2},{4,5},{5,4},{6,7},{7,6},{8,9},{9,8},{10,11... | collective-permute-start | bytes 589832 | tf_op jit(solution)/shard_map/ppermute | solution.py:328
  216.0 5.7 %collective-permute-start.35 = (f32[16,768]{1,0:T(8,128)S(1)}, f32[16,768]{1,0:T(8,128)S(1)}, u32[]{:S(2)}, u32[]{:S(2)}) collective-permute-start(f32[16,768]{1,0:T(8,128)S(1)} %add.305), channel_id=1, source_target_pairs={{0,2},{1,3},{2,0},{3,1},{4,6},{5,7},{6,4},{7,5},{8,10},{9,11},{10,... | collective-permute-start | bytes 147464 | tf_op jit(solution)/shard_map/ppermute | solution.py:328
  217.3 12.7 %collective-permute-start.30 = (bf16[128,768]{1,0:T(8,128)(2,1)}, bf16[128,768]{1,0:T(8,128)(2,1)S(1)}, u32[]{:S(2)}, u32[]{:S(2)}) collective-permute-start(bf16[128,768]{1,0:T(8,128)(2,1)} %shard_map.207.refs_0_), channel_id=1, source_target_pairs={{0,1},{1,0},{2,3},{3,2},{4,5},{5,4},{6,7},{7,6},{8,9},{9,8},{10,11... | collective-permute-start | bytes 589832 | tf_op jit(solution)/shard_map/ppermute | solution.py:328
  221.2 8.8 %copy-start.18 = (bf16[128,768]{1,0:T(8,128)(2,1)}, bf16[128,768]{1,0:T(8,128)(2,1)S(1)}, u32[]{:S(2)}) copy-start(bf16[128,768]{1,0:T(8,128)(2,1)S(1)} %collective-permute-done.31.refs_2_) | copy-start | bytes 589828
  221.2 8.8 %collective-permute-start.32 = (bf16[128,768]{1,0:T(8,128)(2,1)S(1)}, bf16[128,768]{1,0:T(8,128)(2,1)S(1)}, u32[]{:S(2)}, u32[]{:S(2)}) collective-permute-start(bf16[128,768]{1,0:T(8,128)(2,1)S(1)} %collective-permute-done.31.refs_2_), channel_id=1, source_target_pairs={{0,1},{1,0},{2,3},{3,2},{4,5},{5,4},{6,7},{7,6},{8,9},{9,8},{10,11... | collective-permute-start | bytes 589832 | tf_op jit(solution)/shard_map/ppermute | solution.py:328
  222.5 15.3 %collective-permute-start.33 = (bf16[96,768]{1,0:T(8,128)(2,1)S(1)}, bf16[96,768]{1,0:T(8,128)(2,1)S(1)}, u32[]{:S(2)}, u32[]{:S(2)}) collective-permute-start(bf16[96,768]{1,0:T(8,128)(2,1)S(1)} %reduce_sum.72), channel_id=1, source_target_pairs={{0,16},{16,0},{1,17},{17,1},{2,18},{18,2},{3,19},{19,3},{4,20},{20... | collective-permute-start | bytes 442376 | tf_op jit(solution)/shard_map/ppermute | solution.py:328
  224.0 11.4 %collective-permute-start.36 = (f32[24,768]{1,0:T(8,128)S(1)}, f32[24,768]{1,0:T(8,128)S(1)}, u32[]{:S(2)}, u32[]{:S(2)}) collective-permute-start(f32[24,768]{1,0:T(8,128)S(1)} %pad_maximum_fusion.1), channel_id=1, source_target_pairs={{0,4},{4,0},{8,12},{12,8},{16,20},{20,16},{24,28},{28,24},{1,5},{5... | collective-permute-start | bytes 221192 | tf_op jit(solution)/shard_map/ppermute | solution.py:328
  235.4 6.2 %collective-permute-start.37 = (f32[24,768]{1,0:T(8,128)S(1)}, f32[24,768]{1,0:T(8,128)S(1)}, u32[]{:S(2)}, u32[]{:S(2)}) collective-permute-start(f32[24,768]{1,0:T(8,128)S(1)} %add.307), channel_id=1, source_target_pairs={{0,8},{4,12},{8,0},{12,4},{16,24},{20,28},{24,16},{28,20},{1,9},{5... | collective-permute-start | bytes 221192 | tf_op jit(solution)/shard_map/ppermute | solution.py:328
  241.5 4.4 %collective-permute-start.38 = (f32[24,768]{1,0:T(8,128)S(1)}, f32[24,768]{1,0:T(8,128)S(1)}, u32[]{:S(2)}, u32[]{:S(2)}) collective-permute-start(f32[24,768]{1,0:T(8,128)S(1)} %add.308), channel_id=1, source_target_pairs={{0,16},{4,20},{8,24},{12,28},{16,0},{20,4},{24,8},{28,12},{1,17},{... | collective-permute-start | bytes 221192 | tf_op jit(solution)/shard_map/ppermute | solution.py:328
  (15 other events, 14.8 us)
where the time goes:
time: 249 us; the launch traced here: 248 us
  Pallas kernels  78.4 us (31%)
  waiting for transfers between devices  58.6 us (24%)
  starting transfers between devices  48 us (19%)
  blocking collectives  20 us (8%)
  local copies, waits for them, and re-layouts  17 us (7%)
  other arithmetic  15.4 us (6%)
  matrix products  9.25 us (4%)
    pallas_call x14, Pallas kernels, call(): pl.pallas_call(kernel, out_shape=tuple(outs), scratch_shapes=list(scratch...  73.1 us
    ppermute x39, waiting for transfers between devices, swap(): return lax.ppermute(x, axes, [(i, i ^ mask) for i in range(count)])  57.1 us
    ppermute x39, starting transfers between devices, swap(): return lax.ppermute(x, axes, [(i, i ^ mask) for i in range(count)])  28.2 us
    all_to_all x1, blocking collectives, exchange(): return lax.all_to_all(x, axes, split_axis=0, concat_axis=0, tiled=True)  20 us
    all_to_all x4, starting transfers between devices, exchange(): return lax.all_to_all(x, axes, split_axis=0, concat_axis=0, tiled=True)  19.9 us
    unnamed x76, local copies, waits for them, and re-layouts  11.2 us
    dot_general x5, matrix products, dot_n(): return jnp.dot(a, b, precision=precision, preferred_element_type=F32)  6.83 us
  transfers between devices with their start and end apart: 43, of which 17 were waited for; matrix products, arithmetic and copies ran while one was open for 12% of the time, Pallas kernels for 26%

commit v1 on v0

--- a/solution.py
+++ b/solution.py
@@ -82,16 +82,22 @@
     return lax.dot_general(a, b, (((0,), (0,)), ((), ())), precision=precision, preferred_element_type=F32)
 
 
-def call(kernel, outs, operands, flops, scratch=()):
+def call(kernel, outs, operands, flops, scratch=(), scalars=()):
     moved = sum(o.size * o.dtype.itemsize for o in operands) + sum(
         math.prod(o.shape) * o.dtype.itemsize for o in outs
     )
     return pl.pallas_call(
         kernel,
         out_shape=tuple(outs),
+        in_specs=[pl.BlockSpec(memory_space=pltpu.SMEM)] * len(scalars)
+        + [pl.BlockSpec(memory_space=pltpu.VMEM)] * len(operands),
         scratch_shapes=list(scratch),
         cost_estimate=pl.CostEstimate(flops=flops, bytes_accessed=moved, transcendentals=0),
-    )(*operands)
+    )(*scalars, *operands)
+
+
+def chunk_rows(me_ref, k, size):
+    return pl.ds(pl.multiple_of((me_ref[0] ^ k) * size, size), size)
 
 
 def sds(shape, dtype):
@@ -130,9 +136,9 @@
             scores = jnp.where(same, scores, NEG)
             top = jnp.max(scores, axis=1, keepdims=True)
             expo = jnp.exp(scores - top)
-            probs = expo * (1.0 / jnp.sum(expo, axis=1, keepdims=True))
+            probs = (expo * (1.0 / jnp.sum(expo, axis=1, keepdims=True))).astype(BF)
             probs_ref[h, rows, :] = probs
-            att_ref[rows, h * size : (h + 1) * size] = dot_n(probs.astype(BF), v).astype(BF)
+            att_ref[rows, h * size : (h + 1) * size] = dot_n(probs, v).astype(BF)
         return carry
 
     lax.fori_loop(0, length // STEP, body, 0)
@@ -151,7 +157,7 @@
         hidden = hidden + dot_t(a_ref[...], p_ref[...])
     hidden_ref[...] = hidden
     inverse = lax.rsqrt(jnp.mean(hidden * hidden, axis=1, keepdims=True) + EPS)
-    normed = hidden * inverse * gain_ref[...]
+    normed = hidden * inverse * gain_ref[0:1, :]
     logits = dot_t(normed, router_ref[...], HI)
     expo = jnp.exp(logits - jnp.max(logits, axis=1, keepdims=True))
     probs = expo / jnp.sum(expo, axis=1, keepdims=True)
@@ -163,6 +169,14 @@
     lane = lax.broadcasted_iota(jnp.int32, (own, 128), 1)
     extra = jnp.where(lane == 0, high, jnp.where(lane == 1, gate - high, 0.0)).astype(BF)
     send_ref[:, width:] = dot_n(slot_ref[...], extra).astype(BF)
+
+
+def split_kernel(me_ref, a_ref, b_ref, c_ref, *refs):
+    size = refs[0].shape[0]
+    for k, part_ref in enumerate(refs):
+        rows = chunk_rows(me_ref, k, size)
+        total = a_ref[rows, :].astype(F32) + b_ref[rows, :].astype(F32) + c_ref[rows, :].astype(F32)
+        part_ref[...] = total.astype(BF)
 
 
 def expert_kernel(pairs, *refs):
@@ -205,15 +219,23 @@
     refs[2 * count][...] = total
 
 
-def token_kernel(
-    mixed_ref, back_ref, slot_ref, hidden_ref, tokens_ref, probs_ref, gate_ref, picked_ref, gain_ref,
-    router_ref, cot_ref, grad_ref, grad_bf_ref, delta_ref, router_out_ref, mix_ref,
-):
+def mixed_kernel(came_ref, slot_ref, hidden_ref, tokens_ref, gate_ref, mixed_ref, delta_ref):
+    mixed = t_dot(slot_ref[...], came_ref[...])
+    mixed_ref[...] = mixed
+    delta_ref[...] = (hidden_ref[...] - tokens_ref[...] + gate_ref[...] * mixed).astype(BF)
+
+
+def token_kernel(chunks, me_ref, mixed_ref, *refs):
+    back_refs = refs[:chunks]
+    (slot_ref, hidden_ref, probs_ref, gate_ref, picked_ref, gain_ref, router_ref, cot_ref,
+     grad_ref, grad_bf_ref, router_out_ref, mix_ref, all_ref) = refs[chunks:]
+    size = back_refs[0].shape[0]
+    for k in range(chunks):
+        all_ref[chunk_rows(me_ref, k, size), :] = back_refs[k][...]
     width = hidden_ref.shape[1]
-    hidden, gate, cot, gain = hidden_ref[...], gate_ref[...], cot_ref[...], gain_ref[...]
-    mixed = t_dot(slot_ref[...], mixed_ref[...])
-    back = t_dot(slot_ref[...], back_ref[...])
-    delta_ref[...] = (hidden - tokens_ref[...] + gate * mixed).astype(BF)
+    hidden, gate, cot, gain = hidden_ref[...], gate_ref[...], cot_ref[...], gain_ref[0:1, :]
+    mixed = mixed_ref[...]
+    back = t_dot(slot_ref[...], all_ref[...])
     grad_gate = jnp.sum(cot * mixed, axis=1, keepdims=True)
     grad_logits = grad_gate * gate * (picked_ref[...] - probs_ref[...])
     inverse = lax.rsqrt(jnp.mean(hidden * hidden, axis=1, keepdims=True) + EPS)
@@ -255,11 +277,11 @@
             delta = jnp.sum(
                 grad_out.astype(F32) * att_ref[rows, cols].astype(F32), axis=1, keepdims=True
             )
-            grad_scores = probs * (dot_t(grad_out, v) - delta)
+            grad_scores = probs.astype(F32) * (dot_t(grad_out, v) - delta)
             grad_bf = grad_scores.astype(BF)
             gq[rows, cols] = (dot_n(grad_bf, k) * scale).astype(BF)
             dk[:, cols] += t_dot(grad_bf, q)
-            dv[:, cols] += t_dot(probs.astype(BF), grad_out)
+            dv[:, cols] += t_dot(probs, grad_out)
             wide = jnp.concatenate([jnp.zeros_like(grad_scores), grad_scores], axis=1)
             count = STEP // 2
             while count >= 8:
@@ -285,7 +307,7 @@
         table_ref[h : h + 1, :] = dot_n(jnp.broadcast_to(line, (8, 2 * length)), onehot_ref[...], HI)[0:1]
 
 
-def normed_kernel(n_col, gq_ref, perm_ref, w_ref, z_ref, router_ref, mix_ref, table_ref, *refs):
+def normed_kernel(n_col, col_ref, gq_ref, perm_ref, w_ref, z_ref, router_ref, mix_ref, table_ref, *refs):
     part_refs, flat_ref = refs[:n_col], refs[n_col]
     own, width = part_refs[0].shape
     experts = router_ref.shape[0]
@@ -300,12 +322,13 @@
     flat_ref[:experts, :] = router_ref[...]
     flat_ref[experts : experts + 1, :] = mix_ref[...]
     flat_ref[experts + 1 : experts + 2, :] = total
-    flat_ref[experts + 8 :, :128] = table_ref[...]
-
-
-def tokens_kernel(mine_ref, came_ref, grad_ref, cot_ref, tokens_ref, inverse_ref, gain_ref, out_ref):
-    grad_normed = mine_ref[...].astype(F32) + came_ref[...].astype(F32)
-    tokens, inverse, gain = tokens_ref[...], inverse_ref[...], gain_ref[...]
+    flat_ref[experts + 8 :, pl.ds(pl.multiple_of(col_ref[0] * 128, 128), 128)] = table_ref[...]
+
+
+def tokens_kernel(a_ref, b_ref, c_ref, grad_ref, cot_ref, tokens_ref, gain_ref, out_ref):
+    grad_normed = a_ref[...].astype(F32) + b_ref[...].astype(F32) + c_ref[...].astype(F32)
+    tokens, gain = tokens_ref[...], gain_ref[1:2, :]
+    inverse = lax.rsqrt(jnp.mean(tokens * tokens, axis=1, keepdims=True) + EPS)
     inner = jnp.sum(grad_normed * gain * tokens, axis=1, keepdims=True)
     delta = (
         (grad_ref[...] - cot_ref[...])
@@ -322,6 +345,14 @@
     for k in range(n_col):
         total = total + dot_n(perm_ref[:, k * own : (k + 1) * own], b_refs[k][...])
     out_ref[...] = total
+
+
+def place_rows(blocks, perm_t, base):
+    count, width = base.shape
+    return call(
+        partial(place_kernel, len(blocks)), [sds(base.shape, F32)], [*blocks, perm_t, base],
+        2 * count * count * width,
+    )[0]
 
 
 def swap(x, axes, count, mask):
@@ -342,12 +373,13 @@
     return [blocks[k] for k in range(count)]
 
 
-def scatter_rel(blocks, axes, count):
-    held = dict(enumerate(blocks))
-    for bit in bits_of(count):
-        got = {k: swap(held[k | bit].astype(BF), axes, count, bit) for k in held if not k & bit}
-        held = {k: held[k].astype(F32) + got[k].astype(F32) for k in got}
-    return held[0]
+def sum_all(x, axes, count):
+    terms = [x]
+    for k in range(1, count):
+        terms.append(swap(x, axes, count, k))
+    while len(terms) > 1:
+        terms = [terms[i] + terms[i + 1] for i in range(0, len(terms), 2)]
+    return terms[0]
 
 
 def exchange(x, axes):
@@ -391,6 +423,7 @@
     n_dp, n_row, n_col = lax.axis_size("dp"), lax.axis_size("row"), lax.axis_size("col")
     experts = n_dp * n_row
     dp, row, col = lax.axis_index("dp"), lax.axis_index("row"), lax.axis_index("col")
+    me = dp * n_row + row
     count, width = tokens.shape
     length = segments.shape[1]
     heads = rel_table.shape[1]
@@ -441,7 +474,11 @@
     normed_bf = (inputs * inverse * norm_gain).astype(BF)
     tokens_perm = dot_n(perm, tokens)
     inverse_perm = lax.rsqrt(jnp.mean(tokens_perm * tokens_perm, axis=1, keepdims=True) + EPS)
-    tokens_own, inverse_own = tokens_perm[:own], inverse_perm[:own]
+    tokens_own = tokens_perm[:own]
+
+    gains = jnp.stack([mix_gain, norm_gain])
+    seg_row = segments.reshape(1, length)
+    seg_col = jnp.sum(jnp.where(place[:, None] == place[None, :], seg_row, 0), axis=1, keepdims=True)
 
     onehot = offset_onehot(length)
     per_offset = dot_n(rel_table.T, onehot[:, :BUCKETS].T, HI)
@@ -452,10 +489,9 @@
     cot_came = exchange(cot_slots.reshape(experts, slots, width), DR).reshape(total_slots, width)
     cot_blocks = gather_rel(cot_came, "col", n_col)
     proj_blocks = gather_rel(proj_local, "col", n_col)
-    seg_row, seg_col = segments.reshape(1, length), segments.reshape(length, 1)
     qkv_rows, attended, probs, *att_parts = call(
         partial(front_kernel, n_col, heads),
-        [sds((length, 3 * local), BF), sds((length, local), BF), sds((heads, length, length), F32)]
+        [sds((length, 3 * local), BF), sds((length, local), BF), sds((heads, length, length), BF)]
         + [sds((own, local), BF)] * n_col,
         [normed_bf, weight, seg_row, seg_col, bias, perm],
         2 * length * local * (3 * width + 3 * length),
@@ -463,17 +499,32 @@
     att_own = exchange_rel(att_parts, "col", n_col)
 
     router_t = router_weight.T
-    mix_row, gain_row = mix_gain.reshape(1, width), norm_gain.reshape(1, width)
+    cot_own = dot_n(perm_own.astype(F32), cotangent, HI)
+    z_perm = tokens_perm * inverse_perm
+    chunks = experts if experts <= 8 else 1
+    chunk = total_slots // chunks
+    wide = width + 128
+    here = me.reshape(1).astype(jnp.int32)
+    zero = jnp.zeros((1,), jnp.int32)
+    where = here if chunks > 1 else zero
     hidden, router_probs, gate, token_slots = call(
         partial(router_kernel, n_col),
-        [sds((own, width), F32), sds((own, experts), F32), sds((own, 1), F32), sds((total_slots, width + 128), BF)],
-        [*att_own, *proj_blocks, tokens_own, mix_row, router_t, picked, slot_of_own],
+        [sds((own, width), F32), sds((own, experts), F32), sds((own, 1), F32), sds((total_slots, wide), BF)],
+        [*att_own, *proj_blocks, tokens_own, gains, router_t, picked, slot_of_own],
         2 * own * width * (width + total_slots),
     )
 
+    def trade(parts):
+        if chunks == 1:
+            return [exchange(parts[0].reshape(experts, slots, -1), DR).reshape(total_slots, -1)]
+        out = [parts[0]]
+        for k in range(1, chunks):
+            out.append(swap(parts[k], DR, experts, k))
+        return out
+
     token_slots = hold(token_slots, cot_came)
-    token_came = exchange(token_slots.reshape(experts, slots, width + 128), DR)
-    token_blocks = gather_rel(token_came.reshape(total_slots, width + 128), "col", n_col)
+    token_came = exchange(token_slots.reshape(experts, slots, wide), DR).reshape(total_slots, wide)
+    token_blocks = gather_rel(token_came, "col", n_col)
     pairs = 2
     row = sds((total_slots, width), BF)
     twice = sds((pairs * total_slots, width), BF)
@@ -496,12 +547,23 @@
         back_parts += back
         behind.append((pre, gated, rows))
 
-    def to_home(parts):
-        summed = scatter_rel(parts, "col", n_col).astype(BF)
-        return exchange(summed.reshape(experts, slots, width), DR).reshape(total_slots, width)
-
-    mixed_came = to_home(mixed_parts)
-    back_came = to_home(back_parts)
+    def to_col(parts):
+        held = {k: [p] for k, p in enumerate(parts)}
+        for bit in bits_of(n_col)[:-1]:
+            ready = {k: v[0] if len(v) == 1 else sum(t.astype(F32) for t in v).astype(BF) for k, v in held.items()}
+            held = {
+                k: [ready[k], swap(ready[k | bit], "col", n_col, bit)] for k in sorted(held) if not k & bit
+            }
+        return held[0], sum(t.astype(F32) for t in held[n_col // 2]).astype(BF)
+
+    mine, other = to_col(mixed_parts)
+    came = swap(other, "col", n_col, n_col // 2)
+    mixed_sum = sum(t.astype(F32) for t in (*mine, came)).astype(BF)
+    mixed_came = exchange(mixed_sum.reshape(experts, slots, width), DR).reshape(total_slots, width)
+    mine, other = to_col(back_parts)
+    came = swap(other, "col", n_col, n_col // 2)
+    back_split = call(split_kernel, [sds((chunk, width), BF)] * chunks, [*mine, came], 0, scalars=[where])
+    back_came = trade(back_split)
     work = 2 * n_col * total_slots * width * width
     grad_in_local, = call(
         partial(pair_kernel, len(behind)), [sds((width, width), F32)],
@@ -511,24 +573,20 @@
         partial(pair_kernel, len(behind)), [sds((width, width), F32)],
         acts + [g for _, g, _ in behind], work,
     )
-    mixed_came, grad_in_local, grad_out_local = lax.optimization_barrier(
-        (mixed_came, grad_in_local, grad_out_local)
-    )
-
-    cot_own = dot_n(perm_own.astype(F32), cotangent, HI)
-    z_perm = hold(tokens_perm, mixed_parts[0]) * inverse_perm
-    mixed_came, z_perm = lax.optimization_barrier((mixed_came, z_perm))
-
-    grad_hidden, grad_hidden_bf, out_delta, router_local, mix_local = call(
-        token_kernel,
-        [sds((own, width), F32), sds((own, width), BF), sds((own, width), BF), sds((experts, width), F32),
-         sds((1, width), F32)],
-        [mixed_came, back_came, slot_of_own, hidden, tokens_own, router_probs, gate, picked, mix_row,
-         router_t, cot_own],
-        4 * own * width * total_slots,
+
+    mixed, out_delta = call(
+        mixed_kernel, [sds((own, width), F32), sds((own, width), BF)],
+        [mixed_came, slot_of_own, hidden, tokens_own, gate], 2 * own * width * total_slots,
+    )
+    out_blocks = gather_rel(out_delta, "col", n_col)
+    output = place_rows(out_blocks, perm_t, tokens)
+    grad_hidden, grad_hidden_bf, router_local, mix_local = call(
+        partial(token_kernel, chunks),
+        [sds((own, width), F32), sds((own, width), BF), sds((experts, width), F32), sds((1, width), F32)],
+        [mixed, *back_came, slot_of_own, hidden, router_probs, gate, picked, gains, router_t, cot_own],
+        2 * own * width * total_slots, [pltpu.VMEM((total_slots, width), BF)], [where],
     )
     grad_blocks = gather_rel(grad_hidden_bf, "col", n_col)
-    out_blocks = gather_rel(hold(out_delta, *grad_blocks), "col", n_col)
 
     wgrad, grad_qkv, table_local = call(
         partial(back_kernel, n_col, heads),
@@ -543,43 +601,27 @@
         partial(normed_kernel, n_col),
         [sds((own, width), BF)] * n_col + [sds((experts + 16, width), F32)],
         [grad_qkv, perm, weight, z_perm, router_local, mix_local, table_local],
-        2 * length * local * 3 * (width + length),
-    )
-    held = dict(enumerate(normed_parts))
-    for bit in bits_of(n_col)[:-1]:
-        got = {k: swap(held[k | bit], "col", n_col, bit) for k in held if not k & bit}
-        held = {k: (held[k].astype(F32) + got[k].astype(F32)).astype(BF) for k in got}
-    last = n_col // 2
-    normed_came = swap(held[last], "col", n_col, last)
-    first_sum = held[0]
+        2 * length * local * 3 * (width + length), scalars=[col.reshape(1).astype(jnp.int32)],
+    )
+    mine, other = to_col(normed_parts)
+    normed_came = swap(other, "col", n_col, n_col // 2)
     tokens_delta, = call(
         tokens_kernel, [sds((own, width), BF)],
-        [first_sum, normed_came, grad_hidden, cot_own, tokens_own, inverse_own, gain_row],
+        [*mine, normed_came, grad_hidden, cot_own, tokens_own, gains],
         own * width * 12,
     )
     delta_blocks = gather_rel(tokens_delta, "col", n_col)
-    output, = call(
-        partial(place_kernel, n_col), [sds((count, width), F32)], [*out_blocks, perm_t, tokens],
-        2 * count * count * width,
-    )
-    grad_tokens, = call(
-        partial(place_kernel, n_col), [sds((count, width), F32)], [*delta_blocks, perm_t, cotangent],
-        2 * count * count * width,
-    )
+    grad_tokens = place_rows(delta_blocks, perm_t, cotangent)
     summed = jnp.sum(wgrad_came.astype(F32), axis=0).astype(BF)
     summed = in_order(gather_rel(summed, "dp", n_dp), dp).astype(F32)
     grad_qkv_weight = summed[:, : 3 * local].reshape(block, 3, local)
     grad_proj = summed[:, 3 * local :].T
 
     packed = experts + 8
-    most, table = flat[:packed], flat[packed:]
-    most = hold(most, first_sum)
-    for bit in bits_of(n_col):
-        most = most + swap(most, "col", n_col, bit)
-    flat = hold(jnp.concatenate([most, table], axis=0), wgrad_came)
-    for bit in bits_of(experts):
-        flat = flat + swap(flat, DR, experts, bit)
-    grad_table = flat[packed : packed + heads, :BUCKETS].T
+    flat = sum_all(hold(flat, other), "col", n_col)
+    flat = sum_all(flat, "row", n_row)
+    flat = sum_all(flat, "dp", n_dp)
+    grad_table = lax.dynamic_slice(flat, (packed, col * 128), (heads, BUCKETS)).T
     grad_router = flat[:experts].T
     grad_mix, grad_norm = flat[experts], flat[experts + 1]
     return (

time: 249 us -> 265 us (1.064)
  waiting for transfers between devices: 58.6 us -> 69.7 us
  starting transfers between devices: 48 us -> 53.1 us
  Pallas kernels: 78.4 us -> 81.7 us
    ppermute x39 -> x48, waiting for transfers between devices: 57.1 us -> 69.7 us  [swap(): return lax.ppermute(x, axes, [(i, i ^ mask) for i in range(count)])]
    ppermute x39 -> x48, starting transfers between devices: 28.2 us -> 39.9 us  [swap(): return lax.ppermute(x, axes, [(i, i ^ mask) for i in range(count)])]
    all_to_all x4 -> x3, starting transfers between devices: 19.9 us -> 13.3 us  [exchange(): return lax.all_to_all(x, axes, split_axis=0, concat_axis=0, tiled=True)]
    pallas_call x14 -> x16, Pallas kernels: 73.1 us -> 76.3 us  [call(): pl.pallas_call(kernel, out_shape=tuple(outs), in_specs=[pl.BlockSpec(memo...]
    convert_element_type x6 -> x4, other arithmetic: 9.65 us -> 6.82 us  [the longest x3 4.81 us: to_col(): return (held[0], sum((t.astype(F32) for t in held[n_col // 2])).astype(BF))]
    unnamed x76 -> x74, local copies, waits for them, and re-layouts: 11.2 us -> 11.8 us
  transfers between devices with their start and end apart: 43 -> 51, of which waited for: 17 -> 18; matrix products, arithmetic and copies ran while one was open for 12% -> 10% of each run, Pallas kernels for 26% -> 26%
where the time goes in v1:
time: 265 us; the launch traced here: 264 us
  Pallas kernels  81.7 us (31%)
  waiting for transfers between devices  69.7 us (26%)
  starting transfers between devices  53.1 us (20%)
  blocking collectives  20 us (8%)
  local copies, waits for them, and re-layouts  15.8 us (6%)
  other arithmetic  14.2 us (5%)
  matrix products  7.91 us (3%)
    pallas_call x16, Pallas kernels, call(): pl.pallas_call(kernel, out_shape=tuple(outs), in_specs=[pl.BlockSpec(memo...  76.3 us
    ppermute x48, waiting for transfers between devices, swap(): return lax.ppermute(x, axes, [(i, i ^ mask) for i in range(count)])  69.7 us
    ppermute x48, starting transfers between devices, swap(): return lax.ppermute(x, axes, [(i, i ^ mask) for i in range(count)])  39.9 us
    all_to_all x1, blocking collectives, exchange(): return lax.all_to_all(x, axes, split_axis=0, concat_axis=0, tiled=True)  20 us
    all_to_all x3, starting transfers between devices, exchange(): return lax.all_to_all(x, axes, split_axis=0, concat_axis=0, tiled=True)  13.3 us
    unnamed x74, local copies, waits for them, and re-layouts  11.8 us
    dot_general x5, matrix products, dot_n(): return jnp.dot(a, b, precision=precision, preferred_element_type=F32)  6.23 us
  transfers between devices with their start and end apart: 51, of which 18 were waited for; matrix products, arithmetic and copies ran while one was open for 10% of the time, Pallas kernels for 26%

profile of v1, /device:TPU:0, one launch (start us, length us, event | category | flops | bytes accessed | tf_op | source)
XLA Modules:
  0.0 263.5 jit_solution(1120321568858377471)
XLA Ops:
  0.7 1.1 copy.42
  3.2 4.1 %collective-permute-start.1 = (bf16[192,768]{1,0:T(8,128)(2,1)S(1)}, bf16[192,768]{1,0:T(8,128)(2,1)S(1)}, u32[]{:S(2)}, u32[]{:S(2)}) collective-permute-start(bf16[192,768]{1,0:T(8,128)(2,1)S(1)} %pad_maximum_fusion.refs_0_), channel_id=1, source_target_pairs={{0,8},{4,12},{8,0},{12,4},{1,9},{5,13},{9,1},{13,5},{2,10},{6,14},... | collective-permute-start | bytes 884744 | tf_op jit(solution)/shard_map/ppermute | solution.py:359
  7.3 1.6 collective-permute-start
  9.5 1.2 fusion.4
  12.9 1.1 fusion.2.normed_ref.refs_13_
  14.0 6.7 %collective-permute-done.1.refs_2_ = bf16[192,768]{1,0:T(8,128)(2,1)S(1)} collective-permute-done((bf16[192,768]{1,0:T(8,128)(2,1)S(1)}, bf16[192,768]{1,0:T(8,128)(2,1)S(1)}, u32[]{:S(2)}, u32[]{:S(2)}) %collective-permute-start.1) | collective-permute-done | bytes 294944 | tf_op jit(solution)/shard_map/ppermute | solution.py:359
  22.3 1.1 convolution_convert_fusion
  23.4 5.6 %all-to-all-start = ((bf16[8,32,768]{2,1,0:T(8,128)(2,1)}), bf16[8,32,768]{2,1,0:T(8,128)(2,1)}, u32[]{:S(2)}, u32[]{:S(2)}) async-start(bf16[8,32,768]{2,1,0:T(8,128)(2,1)} %bitcast.8), calls=%async_computation | async-start | bytes 786432 | tf_op jit(solution)/shard_map/all_to_all | solution.py:386
  29.7 2.5 unpack.1
  32.2 1.6 collective-permute-start.7
  34.6 1.7 multiply_reduce_fusion
  36.3 6.7 %collective-permute-done.7.refs_6_ = bf16[768,192]{1,0:T(8,128)(2,1)} collective-permute-done((bf16[768,192]{1,0:T(8,128)(2,1)}, bf16[768,192]{1,0:T(8,128)(2,1)}, u32[]{:S(2)}, u32[]{:S(2)}) %collective-permute-start.7) | collective-permute-done | bytes 294944 | tf_op jit(solution)/shard_map/ppermute | solution.py:359
  44.1 2.9 %position_bias.1.bias_ref = f32[3,512,512]{2,1,0:T(8,128)} custom-call(f32[3,1024]{1,0:T(4,128)} %convolution_bitcast_fusion.off_ref), custom_call_target="tpu_custom_call" | custom-call | flops 3145728 | bytes 3145728 | tf_op jit(solution)/shard_map/position_bias/pallas_call | solution.py:63
  47.0 8.0 %shard_map.195 = (bf16[512,576]{1,0:T(8,128)(2,1)}, bf16[512,192]{1,0:T(8,128)(2,1)}, bf16[3,512,512]{2,1,0:T(8,128)(2,1)}, bf16[128,192]{1,0:T(8,128)(2,1)}, bf...) custom-call(bf16[512,768]{1,0:T(8,128)(2,1)} %fusion.2.normed_ref.refs_13_, ...), custom_call_target="tpu_custom_call" | custom-call | flops 754974720 | bytes 7901184 | tf_op jit(solution)/shard_map/pallas_call | solution.py:89
  55.5 1.5 collective-permute-start.4
  58.4 1.6 collective-permute-done.4.refs_2_
  60.0 1.6 collective-permute-done.5.refs_3_
  62.2 4.4 %shard_map.196 = (f32[128,768]{1,0:T(8,128)}, f32[128,8]{1,0:T(8,128)}, f32[128,1]{1,0:T(8,128)}, bf16[256,896]{1,0:T(8,128)(2,1)}) custom-call(bf16[128,192]{1,0:T(8,128)(2,1)} %get-tuple-element.67.refs_0_.refs_4_, bf16[128,192]{1,0:T(8,128)(2,1)} %copy-done.27, bf16[128,192]{1,0:T(8,128)(2,1)} %copy-done.28, bf16[128,192]{1,0:T(8,128)(2,1)} %copy-done.29, ...), custom_call_target="tpu_custom_call" | custom-call | flops 201326592 | bytes 2726400 | tf_op jit(solution)/shard_map/pallas_call | solution.py:89
  66.6 20.0 %all_to_all.20 = bf16[8,32,896]{2,1,0:T(8,128)(2,1)} all-to-all(bf16[8,32,896]{2,1,0:T(8,128)(2,1)} %bitcast.47), channel_id=1, replica_groups=mesh['dp'=2,'row'=4,'col'=4] {'dp','row'}, dimensions={0} | all-to-all | bytes 917504 | tf_op jit(solution)/shard_map/all_to_all | solution.py:386
  87.6 10.5 %collective-permute-done.11.refs_0_ = bf16[256,896]{1,0:T(8,128)(2,1)S(1)} collective-permute-done((bf16[256,896]{1,0:T(8,128)(2,1)}, bf16[256,896]{1,0:T(8,128)(2,1)S(1)}, u32[]{:S(2)}, u32[]{:S(2)}) %collective-permute-start.11) | collective-permute-done | bytes 458784 | tf_op jit(solution)/shard_map/ppermute | solution.py:359
  98.9 1.2 collective-permute-start.20
  100.3 10.3 %collective-permute-done.20.refs_2_ = bf16[256,768]{1,0:T(8,128)(2,1)S(1)} collective-permute-done((bf16[256,768]{1,0:T(8,128)(2,1)}, bf16[256,768]{1,0:T(8,128)(2,1)S(1)}, u32[]{:S(2)}, u32[]{:S(2)}) %collective-permute-start.20) | collective-permute-done | bytes 393248 | tf_op jit(solution)/shard_map/ppermute | solution.py:359
  111.5 5.1 %shard_map.198 = (bf16[256,768]{1,0:T(8,128)(2,1)}, bf16[256,768]{1,0:T(8,128)(2,1)}, bf16[512,768]{1,0:T(8,128)(2,1)}, f32[512,768]{1,0:T(8,128)}) custom-call(bf16[256,896]{1,0:T(8,128)(2,1)} %copy-done.7, bf16[256,896]{1,0:T(8,128)(2,1)} %copy-done.8, bf16[768,768]{1,0:T(8,128)(2,1)} %bitcast.32, bf16[768,768]{1,0:T(8,128)(2,1)} %bitcast.36), custom_call_target="tpu_custom_call" | custom-call | flops 1207959552 | bytes 6422528 | tf_op jit(solution)/shard_map/pallas_call | solution.py:89
  117.2 5.1 %shard_map.197 = (bf16[256,768]{1,0:T(8,128)(2,1)}, bf16[256,768]{1,0:T(8,128)(2,1)}, bf16[512,768]{1,0:T(8,128)(2,1)}, f32[512,768]{1,0:T(8,128)}) custom-call(bf16[256,896]{1,0:T(8,128)(2,1)} %bitcast.11.refs_0_, bf16[256,896]{1,0:T(8,128)(2,1)} %collective-permute-done.9.refs_1_, bf16[768,768]{1,0:T(8,128)(2,1)} %bitcast.33, bf16[768,768]{1,0:T(8,128)(2,1)} %bitcast.37), custom_call_target="tpu_custom_call" | custom-call | flops 1207959552 | bytes 6422528 | tf_op jit(solution)/shard_map/pallas_call | solution.py:89
  122.3 5.5 %shard_map.202 = (bf16[256,768]{1,0:T(8,128)(2,1)}, bf16[256,768]{1,0:T(8,128)(2,1)}, bf16[512,768]{1,0:T(8,128)(2,1)}, bf16[512,768]{1,0:T(8,128)(2,1)}, bf16[512,768]{1,0:T(8,128)(2,1)}) custom-call(bf16[256,896]{1,0:T(8,128)(2,1)} %copy-done.7, bf16[256,896]{1,0:T(8,128)(2,1)} %copy-done.8, bf16[256,768]{1,0:T(8,128)(2,1)} %copy-done.12, ...), custom_call_target="tpu_custom_call" | custom-call | flops 1207959552 | bytes 8781824 | tf_op jit(solution)/shard_map/pallas_call | solution.py:89
  128.4 1.9 add_convert_fusion.2
  130.2 1.2 collective-permute-start.14
  131.4 5.5 %shard_map.201 = (bf16[256,768]{1,0:T(8,128)(2,1)}, bf16[256,768]{1,0:T(8,128)(2,1)}, bf16[512,768]{1,0:T(8,128)(2,1)}, bf16[512,768]{1,0:T(8,128)(2,1)}, bf16[512,768]{1,0:T(8,128)(2,1)}) custom-call(bf16[256,896]{1,0:T(8,128)(2,1)} %bitcast.11.refs_0_, bf16[256,896]{1,0:T(8,128)(2,1)} %collective-permute-done.9.refs_1_, bf16[256,768]{1,0:T(8,128)(2,1)} %bitcast.9.refs_2_, ...), custom_call_target="tpu_custom_call" | custom-call | flops 1207959552 | bytes 8781824 | tf_op jit(solution)/shard_map/pallas_call | solution.py:89
  137.0 2.0 add_convert_fusion
  139.9 2.1 collective-permute-done.14
  142.0 2.0 add_convert_fusion.1
  144.0 3.7 %all-to-all-start.2 = ((bf16[8,32,768]{2,1,0:T(8,128)(2,1)}), bf16[8,32,768]{2,1,0:T(8,128)(2,1)S(1)}, u32[]{:S(2)}, u32[]{:S(2)}) async-start(bf16[8,32,768]{2,1,0:T(8,128)(2,1)} %bitcast.44), calls=%async_computation.2 | async-start | bytes 786432 | tf_op jit(solution)/shard_map/all_to_all | solution.py:386
  147.7 3.0 %collective-permute-done.23.c_ref = bf16[256,768]{1,0:T(8,128)(2,1)} collective-permute-done((bf16[256,768]{1,0:T(8,128)(2,1)}, bf16[256,768]{1,0:T(8,128)(2,1)}, u32[]{:S(2)}, u32[]{:S(2)}) %collective-permute-start.23) | collective-permute-done | bytes 393248 | tf_op jit(solution)/shard_map/ppermute | solution.py:359
  150.7 2.0 shard_map.203
  152.7 1.4 collective-permute-start.25
  154.2 2.9 %collective-permute-start.26 = (bf16[32,768]{1,0:T(8,128)(2,1)}, bf16[32,768]{1,0:T(8,128)(2,1)}, u32[]{:S(2)}, u32[]{:S(2)}) collective-permute-start(bf16[32,768]{1,0:T(8,128)(2,1)} %get-tuple-element.92), channel_id=1, source_target_pairs={{0,12},{4,8},{8,4},{12,0},{16,28},{20,24},{24,20},{28,16},{1,13},{... | collective-permute-start | bytes 147464 | tf_op jit(solution)/shard_map/ppermute | solution.py:359
  157.8 4.1 %collective-permute-start.29 = (bf16[32,768]{1,0:T(8,128)(2,1)}, bf16[32,768]{1,0:T(8,128)(2,1)}, u32[]{:S(2)}, u32[]{:S(2)}) collective-permute-start(bf16[32,768]{1,0:T(8,128)(2,1)} %get-tuple-element.95), channel_id=1, source_target_pairs={{0,24},{4,28},{8,16},{12,20},{16,8},{20,12},{24,0},{28,4},{1,25},{... | collective-permute-start | bytes 147464 | tf_op jit(solution)/shard_map/ppermute | solution.py:359
  161.9 2.0 collective-permute-done.25.refs_2_
  163.9 1.4 collective-permute-start.30
  165.4 2.2 fusion.12.refs_15_.cot_ref
  168.3 2.3 shard_map.199
  171.0 3.4 %shard_map.204 = (f32[128,768]{1,0:T(8,128)}, bf16[128,768]{1,0:T(8,128)(2,1)}, f32[8,768]{1,0:T(8,128)}, f32[1,768]{1,0:T(1,128)}) custom-call(s32[1]{0:T(128)} %bitcast.17.me_ref, f32[128,768]{1,0:T(8,128)} %get-tuple-element.82.mixed_ref, bf16[32,768]{1,0:T(8,128)(2,1)} %get-tuple-element.89.refs_0_, bf16[32,768]{1,0:T(8,128)(2,1)} %collective-permute-done.24.refs_1_, ...), custom_call_target="tpu_custom_call" | custom-call | flops 50331648 | bytes 2295296 | tf_op jit(solution)/shard_map/pallas_call | solution.py:89
  174.4 1.2 collective-permute-start.32
  175.6 5.1 %collective-permute-done.32.refs_2_ = bf16[128,768]{1,0:T(8,128)(2,1)S(1)} collective-permute-done((bf16[128,768]{1,0:T(8,128)(2,1)}, bf16[128,768]{1,0:T(8,128)(2,1)S(1)}, u32[]{:S(2)}, u32[]{:S(2)}) %collective-permute-start.32) | collective-permute-done | bytes 196640 | tf_op jit(solution)/shard_map/ppermute | solution.py:359
  180.8 1.4 collective-permute-done.33.refs_3_
  182.9 10.8 %shard_map.205 = (bf16[768,768]{1,0:T(8,128)(2,1)}, bf16[512,576]{1,0:T(8,128)(2,1)}, f32[8,128]{1,0:T(8,128)}) custom-call(bf16[128,768]{1,0:T(8,128)(2,1)} %get-tuple-element.98.refs_0_, bf16[128,768]{1,0:T(8,128)(2,1)} %copy-done.22, bf16[128,768]{1,0:T(8,128)(2,1)} %copy-done.21, bf16[128,768]{1,0:T(8,128)(2,1)} %copy-done.24, ...), custom_call_target="tpu_custom_call" | custom-call | flops 1258291200 | bytes 7245824 | tf_op jit(solution)/shard_map/pallas_call | solution.py:89
  193.7 4.0 %all-to-all-start.3 = ((bf16[8,96,768]{2,1,0:T(8,128)(2,1)}), bf16[8,96,768]{2,1,0:T(8,128)(2,1)S(1)}, u32[]{:S(2)}, u32[]{:S(2)}) async-start(bf16[8,96,768]{2,1,0:T(8,128)(2,1)} %bitcast.45), calls=%async_computation.3 | async-start | bytes 2359296 | tf_op jit(solution)/shard_map/all_to_all | solution.py:386
  197.7 1.3 broadcast_multiply_fusion.z_ref
  199.0 4.6 %shard_map.206 = (bf16[128,768]{1,0:T(8,128)(2,1)}, bf16[128,768]{1,0:T(8,128)(2,1)}, bf16[128,768]{1,0:T(8,128)(2,1)}, bf16[128,768]{1,0:T(8,128)(2,1)}, f32[24,768]{1,0:T(8,128)}) custom-call(s32[1]{0:T(128)} %bitcast.16.col_ref, bf16[512,576]{1,0:T(8,128)(2,1)} %get-tuple-element.102.gq_ref, bf16[512,512]{1,0:T(8,128)(2,1)} %get-tuple-element.161.perm_ref, ...), custom_call_target="tpu_custom_call" | custom-call | flops 754974720 | bytes 4463616 | tf_op jit(solution)/shard_map/pallas_call | solution.py:89
  203.6 1.6 collective-permute-done.35
  206.4 1.3 collective-permute-start.42
  208.2 1.3 collective-permute-start.16
  209.5 2.0 collective-permute-done.42
  213.4 2.1 collective-permute-start.44
  215.5 2.4 collective-permute-start.45
  217.9 4.7 %shard_map.210 = f32[768,768]{1,0:T(8,128)} custom-call(bf16[512,768]{1,0:T(8,128)(2,1)} %get-tuple-element.118.refs_0_, bf16[512,768]{1,0:T(8,128)(2,1)} %get-tuple-element.119.refs_1_, bf16[512,768]{1,0:T(8,128)(2,1)} %get-tuple-element.120.refs_2_, bf16[512,768]{1,0:T(8,128)(2,1)} %get-tuple-element.121.refs_3_), custom_call_target="tpu_custom_call" | custom-call | flops 1207959552 | bytes 5505024 | tf_op jit(solution)/shard_map/pallas_call | solution.py:89
  223.3 8.8 %collective-permute-done.45 = f32[24,768]{1,0:T(8,128)S(1)} collective-permute-done((f32[24,768]{1,0:T(8,128)S(1)}, f32[24,768]{1,0:T(8,128)S(1)}, u32[]{:S(2)}, u32[]{:S(2)}) %collective-permute-start.45) | collective-permute-done | bytes 73760 | tf_op jit(solution)/shard_map/ppermute | solution.py:359
  232.1 1.3 collective-permute-start.36
  233.4 1.5 collective-permute-start.47
  234.9 4.7 %shard_map.209 = f32[768,768]{1,0:T(8,128)} custom-call(bf16[512,768]{1,0:T(8,128)(2,1)} %get-tuple-element.114.refs_0_, bf16[512,768]{1,0:T(8,128)(2,1)} %get-tuple-element.115.refs_1_, bf16[512,768]{1,0:T(8,128)(2,1)} %get-tuple-element.116.refs_2_, bf16[512,768]{1,0:T(8,128)(2,1)} %get-tuple-element.117.refs_3_), custom_call_target="tpu_custom_call" | custom-call | flops 1207959552 | bytes 5505024 | tf_op jit(solution)/shard_map/pallas_call | solution.py:89
  240.9 3.8 %shard_map.200 = f32[512,768]{1,0:T(8,128)} custom-call(bf16[128,768]{1,0:T(8,128)(2,1)} %get-tuple-element.81.refs_0_, bf16[128,768]{1,0:T(8,128)(2,1)} %copy-done.17, bf16[128,768]{1,0:T(8,128)(2,1)} %copy-done.16, bf16[128,768]{1,0:T(8,128)(2,1)} %copy-done.19, bf16[512,512]{1,0:T(8,128)(2,1)} %get-tuple-element.160.refs_4_.refs_9_, bf16[512,768]{1,0:T(8,128)(2,1)} %refs_5_.2), custom_call_target="tpu_custom_call" | custom-call | flops 402653184 | bytes 3670016 | tf_op jit(solution)/shard_map/pallas_call | solution.py:89
  245.4 2.4 shard_map.207.refs_0_
  249.2 4.5 %collective-permute-done.38.refs_2_ = bf16[128,768]{1,0:T(8,128)(2,1)S(1)} collective-permute-done((bf16[128,768]{1,0:T(8,128)(2,1)}, bf16[128,768]{1,0:T(8,128)(2,1)S(1)}, u32[]{:S(2)}, u32[]{:S(2)}) %collective-permute-start.38) | collective-permute-done | bytes 196640 | tf_op jit(solution)/shard_map/ppermute | solution.py:359
  257.2 4.0 %shard_map.208 = f32[512,768]{1,0:T(8,128)} custom-call(bf16[128,768]{1,0:T(8,128)(2,1)} %shard_map.207.refs_0_, bf16[128,768]{1,0:T(8,128)(2,1)} %copy-done.20, bf16[128,768]{1,0:T(8,128)(2,1)} %copy-done.18, bf16[128,768]{1,0:T(8,128)(2,1)} %copy-done.23, bf16[512,512]{1,0:T(8,128)(2,1)} %get-tuple-element.160.refs_4_.refs_9_, f32[512,768]{1,0:T(8,128)} %refs_5_.3), custom_call_target="tpu_custom_call" | custom-call | flops 402653184 | bytes 4456448 | tf_op jit(solution)/shard_map/pallas_call | solution.py:89
  (174 shorter events, 31.6 us)
Async XLA Ops:
  0.6 11.3 %copy-start = (f32[32,3]{0,1:T(4,128)S(1)}, f32[32,3]{0,1:T(4,128)}, u32[]{:S(2)}) copy-start(f32[32,3]{0,1:T(4,128)} %param.19) | copy-start | bytes 1156
  0.7 8.2 %copy-start.30 = (s32[512,1]{0,1:T(1,128)S(1)}, s32[512,1]{0,1:T(1,128)}, u32[]{:S(2)}) copy-start(s32[512,1]{0,1:T(1,128)} %param.14) | copy-start | bytes 6148
  2.0 9.7 %copy-start.2 = (bf16[512,768]{1,0:T(8,128)(2,1)S(1)}, bf16[512,768]{1,0:T(8,128)(2,1)}, u32[]{:S(2)}) copy-start(bf16[512,768]{1,0:T(8,128)(2,1)} %refs_5_.2) | copy-start | bytes 2359300
  3.2 9.7 %copy-start.6 = (bf16[192,768]{1,0:T(8,128)(2,1)}, bf16[192,768]{1,0:T(8,128)(2,1)S(1)}, u32[]{:S(2)}) copy-start(bf16[192,768]{1,0:T(8,128)(2,1)S(1)} %pad_maximum_fusion.refs_0_) | copy-start | bytes 884740
  3.2 17.6 %collective-permute-start.1 = (bf16[192,768]{1,0:T(8,128)(2,1)S(1)}, bf16[192,768]{1,0:T(8,128)(2,1)S(1)}, u32[]{:S(2)}, u32[]{:S(2)}) collective-permute-start(bf16[192,768]{1,0:T(8,128)(2,1)S(1)} %pad_maximum_fusion.refs_0_), channel_id=1, source_target_pairs={{0,8},{4,12},{8,0},{12,4},{1,9},{5,13},{9,1},{13,5},{2,10},{6,14},... | collective-permute-start | bytes 884744 | tf_op jit(solution)/shard_map/ppermute | solution.py:359
  7.3 21.7 %collective-permute-start = (bf16[192,768]{1,0:T(8,128)(2,1)S(1)}, bf16[192,768]{1,0:T(8,128)(2,1)S(1)}, u32[]{:S(2)}, u32[]{:S(2)}) collective-permute-start(bf16[192,768]{1,0:T(8,128)(2,1)S(1)} %pad_maximum_fusion.refs_0_), channel_id=1, source_target_pairs={{0,4},{4,0},{8,12},{12,8},{1,5},{5,1},{9,13},{13,9},{2,6},{6,2},{1... | collective-permute-start | bytes 884744 | tf_op jit(solution)/shard_map/ppermute | solution.py:359
  10.7 23.1 %copy-start.9 = (pred[512,512]{1,0:T(32,128)(4,1)}, pred[512,512]{1,0:T(32,128)(4,1)S(1)}, u32[]{:S(2)}) copy-start(pred[512,512]{1,0:T(32,128)(4,1)S(1)} %get-tuple-element.162) | copy-start | bytes 786436
  11.7 10.6 %copy-start.1 = (f32[512,768]{1,0:T(8,128)S(1)}, f32[512,768]{1,0:T(8,128)}, u32[]{:S(2)}) copy-start(f32[512,768]{1,0:T(8,128)} %refs_5_.3) | copy-start | bytes 4718596
  20.8 8.2 %collective-permute-start.2 = (bf16[192,768]{1,0:T(8,128)(2,1)S(1)}, bf16[192,768]{1,0:T(8,128)(2,1)}, u32[]{:S(2)}, u32[]{:S(2)}) collective-permute-start(bf16[192,768]{1,0:T(8,128)(2,1)S(1)} %collective-permute-done.1.refs_2_), channel_id=1, source_target_pairs={{0,4},{4,0},{8,12},{12,8},{1,5},{5,1},{9,13},{13,9},{2,6},{6,2},{1... | collective-permute-start | bytes 884744 | tf_op jit(solution)/shard_map/ppermute | solution.py:359
  23.4 43.2 %all-to-all-start = ((bf16[8,32,768]{2,1,0:T(8,128)(2,1)}), bf16[8,32,768]{2,1,0:T(8,128)(2,1)}, u32[]{:S(2)}, u32[]{:S(2)}) async-start(bf16[8,32,768]{2,1,0:T(8,128)(2,1)} %bitcast.8), calls=%async_computation | async-start | bytes 786432 | tf_op jit(solution)/shard_map/all_to_all | solution.py:386
  32.2 10.9 %copy-start.32 = (s32[1,512]{1,0:T(1,128)S(1)}, s32[1,512]{1,0:T(1,128)}, u32[]{:S(2)}) copy-start(s32[1,512]{1,0:T(1,128)} %seg_row_ref.1) | copy-start | bytes 6148
  32.2 11.9 %copy-start.33 = (f32[768]{0:T(1024)S(1)}, f32[768]{0:T(1024)}, u32[]{:S(2)}) copy-start(f32[768]{0:T(1024)} %param.16) | copy-start | bytes 9220
  32.2 10.9 %collective-permute-start.7 = (bf16[768,192]{1,0:T(8,128)(2,1)}, bf16[768,192]{1,0:T(8,128)(2,1)}, u32[]{:S(2)}, u32[]{:S(2)}) collective-permute-start(bf16[768,192]{1,0:T(8,128)(2,1)} %get-tuple-element.71.refs_4_.refs_8_), channel_id=1, source_target_pairs={{0,2},{1,3},{2,0},{3,1},{4,6},{5,7},{6,4},{7,5},{8,10},{9,11},{10,... | collective-permute-start | bytes 884744 | tf_op jit(solution)/shard_map/ppermute | solution.py:359
  36.3 25.2 %collective-permute-start.6 = (bf16[768,192]{1,0:T(8,128)(2,1)S(1)}, bf16[768,192]{1,0:T(8,128)(2,1)}, u32[]{:S(2)}, u32[]{:S(2)}) collective-permute-start(bf16[768,192]{1,0:T(8,128)(2,1)S(1)} %copy-done.5), channel_id=1, source_target_pairs={{0,1},{1,0},{2,3},{3,2},{4,5},{5,4},{6,7},{7,6},{8,9},{9,8},{10,11... | collective-permute-start | bytes 884744 | tf_op jit(solution)/shard_map/ppermute | solution.py:359
  43.0 18.5 %collective-permute-start.8 = (bf16[768,192]{1,0:T(8,128)(2,1)}, bf16[768,192]{1,0:T(8,128)(2,1)}, u32[]{:S(2)}, u32[]{:S(2)}) collective-permute-start(bf16[768,192]{1,0:T(8,128)(2,1)} %collective-permute-done.7.refs_6_), channel_id=1, source_target_pairs={{0,1},{1,0},{2,3},{3,2},{4,5},{5,4},{6,7},{7,6},{8,9},{9,8},{10,11... | collective-permute-start | bytes 884744 | tf_op jit(solution)/shard_map/ppermute | solution.py:359
  47.0 10.6 %copy-start.3 = (f32[512,768]{1,0:T(8,128)S(1)}, f32[512,768]{1,0:T(8,128)}, u32[]{:S(2)}) copy-start(f32[512,768]{1,0:T(8,128)} %get-tuple-element.164) | copy-start | bytes 4718596
  55.0 3.4 %collective-permute-start.3 = (bf16[128,192]{1,0:T(8,128)(2,1)}, bf16[128,192]{1,0:T(8,128)(2,1)S(1)}, u32[]{:S(2)}, u32[]{:S(2)}) collective-permute-start(bf16[128,192]{1,0:T(8,128)(2,1)} %get-tuple-element.68.refs_5_), channel_id=1, source_target_pairs={{0,1},{1,0},{2,3},{3,2},{4,5},{5,4},{6,7},{7,6},{8,9},{9,8},{10,11... | collective-permute-start | bytes 147464 | tf_op jit(solution)/shard_map/ppermute | solution.py:359
  55.5 4.5 %collective-permute-start.4 = (bf16[128,192]{1,0:T(8,128)(2,1)}, bf16[128,192]{1,0:T(8,128)(2,1)S(1)}, u32[]{:S(2)}, u32[]{:S(2)}) collective-permute-start(bf16[128,192]{1,0:T(8,128)(2,1)} %get-tuple-element.69.refs_6_), channel_id=1, source_target_pairs={{0,2},{1,3},{2,0},{3,1},{4,6},{5,7},{6,4},{7,5},{8,10},{9,11},{10,... | collective-permute-start | bytes 147464 | tf_op jit(solution)/shard_map/ppermute | solution.py:359
  57.0 4.5 %collective-permute-start.5 = (bf16[128,192]{1,0:T(8,128)(2,1)}, bf16[128,192]{1,0:T(8,128)(2,1)S(1)}, u32[]{:S(2)}, u32[]{:S(2)}) collective-permute-start(bf16[128,192]{1,0:T(8,128)(2,1)} %get-tuple-element.70.refs_7_), channel_id=1, source_target_pairs={{0,3},{1,2},{2,1},{3,0},{4,7},{5,6},{6,5},{7,4},{8,11},{9,10},{10,... | collective-permute-start | bytes 147464 | tf_op jit(solution)/shard_map/ppermute | solution.py:359
  86.6 11.6 %collective-permute-start.11 = (bf16[256,896]{1,0:T(8,128)(2,1)}, bf16[256,896]{1,0:T(8,128)(2,1)S(1)}, u32[]{:S(2)}, u32[]{:S(2)}) collective-permute-start(bf16[256,896]{1,0:T(8,128)(2,1)} %bitcast.11.refs_0_), channel_id=1, source_target_pairs={{0,2},{1,3},{2,0},{3,1},{4,6},{5,7},{6,4},{7,5},{8,10},{9,11},{10,... | collective-permute-start | bytes 1376264 | tf_op jit(solution)/shard_map/ppermute | solution.py:359
  98.9 11.7 %collective-permute-start.12 = (bf16[256,896]{1,0:T(8,128)(2,1)S(1)}, bf16[256,896]{1,0:T(8,128)(2,1)S(1)}, u32[]{:S(2)}, u32[]{:S(2)}) collective-permute-start(bf16[256,896]{1,0:T(8,128)(2,1)S(1)} %collective-permute-done.11.refs_0_), channel_id=1, source_target_pairs={{0,1},{1,0},{2,3},{3,2},{4,5},{5,4},{6,7},{7,6},{8,9},{9,8},{10,11... | collective-permute-start | bytes 1376264 | tf_op jit(solution)/shard_map/ppermute | solution.py:359
  98.9 11.7 %collective-permute-start.20 = (bf16[256,768]{1,0:T(8,128)(2,1)}, bf16[256,768]{1,0:T(8,128)(2,1)S(1)}, u32[]{:S(2)}, u32[]{:S(2)}) collective-permute-start(bf16[256,768]{1,0:T(8,128)(2,1)} %bitcast.9.refs_2_), channel_id=1, source_target_pairs={{0,2},{1,3},{2,0},{3,1},{4,6},{5,7},{6,4},{7,5},{8,10},{9,11},{10,... | collective-permute-start | bytes 1179656 | tf_op jit(solution)/shard_map/ppermute | solution.py:359
  100.1 17.1 %collective-permute-start.9 = (bf16[256,896]{1,0:T(8,128)(2,1)}, bf16[256,896]{1,0:T(8,128)(2,1)}, u32[]{:S(2)}, u32[]{:S(2)}) collective-permute-start(bf16[256,896]{1,0:T(8,128)(2,1)} %bitcast.11.refs_0_), channel_id=1, source_target_pairs={{0,1},{1,0},{2,3},{3,2},{4,5},{5,4},{6,7},{7,6},{8,9},{9,8},{10,11... | collective-permute-start | bytes 1376264 | tf_op jit(solution)/shard_map/ppermute | solution.py:359
  110.7 11.6 %copy-start.12 = (bf16[256,768]{1,0:T(8,128)(2,1)}, bf16[256,768]{1,0:T(8,128)(2,1)S(1)}, u32[]{:S(2)}) copy-start(bf16[256,768]{1,0:T(8,128)(2,1)S(1)} %collective-permute-done.20.refs_2_) | copy-start | bytes 1179652
  110.7 11.6 %collective-permute-start.21 = (bf16[256,768]{1,0:T(8,128)(2,1)S(1)}, bf16[256,768]{1,0:T(8,128)(2,1)}, u32[]{:S(2)}, u32[]{:S(2)}) collective-permute-start(bf16[256,768]{1,0:T(8,128)(2,1)S(1)} %collective-permute-done.20.refs_2_), channel_id=1, source_target_pairs={{0,1},{1,0},{2,3},{3,2},{4,5},{5,4},{6,7},{7,6},{8,9},{9,8},{10,11... | collective-permute-start | bytes 1179656 | tf_op jit(solution)/shard_map/ppermute | solution.py:359
  116.7 11.7 %collective-permute-start.13 = (bf16[256,768]{1,0:T(8,128)(2,1)}, bf16[256,768]{1,0:T(8,128)(2,1)}, u32[]{:S(2)}, u32[]{:S(2)}) collective-permute-start(bf16[256,768]{1,0:T(8,128)(2,1)} %get-tuple-element.78), channel_id=1, source_target_pairs={{0,1},{1,0},{2,3},{3,2},{4,5},{5,4},{6,7},{7,6},{8,9},{9,8},{10,11... | collective-permute-start | bytes 1179656 | tf_op jit(solution)/shard_map/ppermute | solution.py:359
  117.1 14.3 %collective-permute-start.18 = (bf16[256,768]{1,0:T(8,128)(2,1)}, bf16[256,768]{1,0:T(8,128)(2,1)}, u32[]{:S(2)}, u32[]{:S(2)}) collective-permute-start(bf16[256,768]{1,0:T(8,128)(2,1)} %bitcast.9.refs_2_), channel_id=1, source_target_pairs={{0,1},{1,0},{2,3},{3,2},{4,5},{5,4},{6,7},{7,6},{8,9},{9,8},{10,11... | collective-permute-start | bytes 1179656 | tf_op jit(solution)/shard_map/ppermute | solution.py:359
  127.8 9.2 %collective-permute-start.22 = (bf16[256,768]{1,0:T(8,128)(2,1)}, bf16[256,768]{1,0:T(8,128)(2,1)}, u32[]{:S(2)}, u32[]{:S(2)}) collective-permute-start(bf16[256,768]{1,0:T(8,128)(2,1)} %get-tuple-element.88), channel_id=1, source_target_pairs={{0,1},{1,0},{2,3},{3,2},{4,5},{5,4},{6,7},{7,6},{8,9},{9,8},{10,11... | collective-permute-start | bytes 1179656 | tf_op jit(solution)/shard_map/ppermute | solution.py:359
  128.3 11.6 %collective-permute-start.10 = (bf16[256,768]{1,0:T(8,128)(2,1)}, bf16[256,768]{1,0:T(8,128)(2,1)}, u32[]{:S(2)}, u32[]{:S(2)}) collective-permute-start(bf16[256,768]{1,0:T(8,128)(2,1)} %get-tuple-element.76), channel_id=1, source_target_pairs={{0,1},{1,0},{2,3},{3,2},{4,5},{5,4},{6,7},{7,6},{8,9},{9,8},{10,11... | collective-permute-start | bytes 1179656 | tf_op jit(solution)/shard_map/ppermute | solution.py:359
  130.2 11.8 %collective-permute-start.14 = (bf16[256,768]{1,0:T(8,128)(2,1)}, bf16[256,768]{1,0:T(8,128)(2,1)}, u32[]{:S(2)}, u32[]{:S(2)}) collective-permute-start(bf16[256,768]{1,0:T(8,128)(2,1)} %add_convert_fusion.2), channel_id=1, source_target_pairs={{0,2},{1,3},{2,0},{3,1},{4,6},{5,7},{6,4},{7,5},{8,10},{9,11},{10,... | collective-permute-start | bytes 1179656 | tf_op jit(solution)/shard_map/ppermute | solution.py:359
  131.4 10.6 %copy-start.10 = (bf16[256,768]{1,0:T(8,128)(2,1)S(1)}, bf16[256,768]{1,0:T(8,128)(2,1)}, u32[]{:S(2)}) copy-start(bf16[256,768]{1,0:T(8,128)(2,1)} %get-tuple-element.75) | copy-start | bytes 1179652
  136.9 10.8 %collective-permute-start.19 = (bf16[256,768]{1,0:T(8,128)(2,1)}, bf16[256,768]{1,0:T(8,128)(2,1)}, u32[]{:S(2)}, u32[]{:S(2)}) collective-permute-start(bf16[256,768]{1,0:T(8,128)(2,1)} %get-tuple-element.85), channel_id=1, source_target_pairs={{0,1},{1,0},{2,3},{3,2},{4,5},{5,4},{6,7},{7,6},{8,9},{9,8},{10,11... | collective-permute-start | bytes 1179656 | tf_op jit(solution)/shard_map/ppermute | solution.py:359
  139.0 11.7 %collective-permute-start.23 = (bf16[256,768]{1,0:T(8,128)(2,1)}, bf16[256,768]{1,0:T(8,128)(2,1)}, u32[]{:S(2)}, u32[]{:S(2)}) collective-permute-start(bf16[256,768]{1,0:T(8,128)(2,1)} %add_convert_fusion), channel_id=1, source_target_pairs={{0,2},{1,3},{2,0},{3,1},{4,6},{5,7},{6,4},{7,5},{8,10},{9,11},{10,... | collective-permute-start | bytes 1179656 | tf_op jit(solution)/shard_map/ppermute | solution.py:359
  144.0 23.6 %all-to-all-start.2 = ((bf16[8,32,768]{2,1,0:T(8,128)(2,1)}), bf16[8,32,768]{2,1,0:T(8,128)(2,1)S(1)}, u32[]{:S(2)}, u32[]{:S(2)}) async-start(bf16[8,32,768]{2,1,0:T(8,128)(2,1)} %bitcast.44), calls=%async_computation.2 | async-start | bytes 786432 | tf_op jit(solution)/shard_map/all_to_all | solution.py:386
  152.7 5.1 %collective-permute-start.24 = (bf16[32,768]{1,0:T(8,128)(2,1)}, bf16[32,768]{1,0:T(8,128)(2,1)}, u32[]{:S(2)}, u32[]{:S(2)}) collective-permute-start(bf16[32,768]{1,0:T(8,128)(2,1)} %get-tuple-element.90), channel_id=1, source_target_pairs={{0,4},{4,0},{8,12},{12,8},{16,20},{20,16},{24,28},{28,24},{1,5},{5... | collective-permute-start | bytes 147464 | tf_op jit(solution)/shard_map/ppermute | solution.py:359
  152.7 11.2 %collective-permute-start.25 = (bf16[32,768]{1,0:T(8,128)(2,1)}, bf16[32,768]{1,0:T(8,128)(2,1)}, u32[]{:S(2)}, u32[]{:S(2)}) collective-permute-start(bf16[32,768]{1,0:T(8,128)(2,1)} %get-tuple-element.91), channel_id=1, source_target_pairs={{0,8},{4,12},{8,0},{12,4},{16,24},{20,28},{24,16},{28,20},{1,9},{5... | collective-permute-start | bytes 147464 | tf_op jit(solution)/shard_map/ppermute | solution.py:359
  154.2 16.5 %collective-permute-start.26 = (bf16[32,768]{1,0:T(8,128)(2,1)}, bf16[32,768]{1,0:T(8,128)(2,1)}, u32[]{:S(2)}, u32[]{:S(2)}) collective-permute-start(bf16[32,768]{1,0:T(8,128)(2,1)} %get-tuple-element.92), channel_id=1, source_target_pairs={{0,12},{4,8},{8,4},{12,0},{16,28},{20,24},{24,20},{28,16},{1,13},{... | collective-permute-start | bytes 147464 | tf_op jit(solution)/shard_map/ppermute | solution.py:359
  157.1 13.5 %collective-permute-start.27 = (bf16[32,768]{1,0:T(8,128)(2,1)}, bf16[32,768]{1,0:T(8,128)(2,1)}, u32[]{:S(2)}, u32[]{:S(2)}) collective-permute-start(bf16[32,768]{1,0:T(8,128)(2,1)} %get-tuple-element.93), channel_id=1, source_target_pairs={{0,16},{4,20},{8,24},{12,28},{16,0},{20,4},{24,8},{28,12},{1,17},{... | collective-permute-start | bytes 147464 | tf_op jit(solution)/shard_map/ppermute | solution.py:359
  157.7 13.0 %collective-permute-start.28 = (bf16[32,768]{1,0:T(8,128)(2,1)}, bf16[32,768]{1,0:T(8,128)(2,1)}, u32[]{:S(2)}, u32[]{:S(2)}) collective-permute-start(bf16[32,768]{1,0:T(8,128)(2,1)} %get-tuple-element.94), channel_id=1, source_target_pairs={{0,20},{4,16},{8,28},{12,24},{16,4},{20,0},{24,12},{28,8},{1,21},{... | collective-permute-start | bytes 147464 | tf_op jit(solution)/shard_map/ppermute | solution.py:359
  157.8 12.9 %collective-permute-start.29 = (bf16[32,768]{1,0:T(8,128)(2,1)}, bf16[32,768]{1,0:T(8,128)(2,1)}, u32[]{:S(2)}, u32[]{:S(2)}) collective-permute-start(bf16[32,768]{1,0:T(8,128)(2,1)} %get-tuple-element.95), channel_id=1, source_target_pairs={{0,24},{4,28},{8,16},{12,20},{16,8},{20,12},{24,0},{28,4},{1,25},{... | collective-permute-start | bytes 147464 | tf_op jit(solution)/shard_map/ppermute | solution.py:359
  163.9 7.1 %collective-permute-start.30 = (bf16[32,768]{1,0:T(8,128)(2,1)}, bf16[32,768]{1,0:T(8,128)(2,1)}, u32[]{:S(2)}, u32[]{:S(2)}) collective-permute-start(bf16[32,768]{1,0:T(8,128)(2,1)} %get-tuple-element.96), channel_id=1, source_target_pairs={{0,28},{4,24},{8,20},{12,16},{16,12},{20,8},{24,4},{28,0},{1,29},{... | collective-permute-start | bytes 147464 | tf_op jit(solution)/shard_map/ppermute | solution.py:359
  174.4 6.3 %collective-permute-start.32 = (bf16[128,768]{1,0:T(8,128)(2,1)}, bf16[128,768]{1,0:T(8,128)(2,1)S(1)}, u32[]{:S(2)}, u32[]{:S(2)}) collective-permute-start(bf16[128,768]{1,0:T(8,128)(2,1)} %get-tuple-element.98.refs_0_), channel_id=1, source_target_pairs={{0,2},{1,3},{2,0},{3,1},{4,6},{5,7},{6,4},{7,5},{8,10},{9,11},{10,... | collective-permute-start | bytes 589832 | tf_op jit(solution)/shard_map/ppermute | solution.py:359
  175.6 5.1 %collective-permute-start.31 = (bf16[128,768]{1,0:T(8,128)(2,1)}, bf16[128,768]{1,0:T(8,128)(2,1)S(1)}, u32[]{:S(2)}, u32[]{:S(2)}) collective-permute-start(bf16[128,768]{1,0:T(8,128)(2,1)} %get-tuple-element.98.refs_0_), channel_id=1, source_target_pairs={{0,1},{1,0},{2,3},{3,2},{4,5},{5,4},{6,7},{7,6},{8,9},{9,8},{10,11... | collective-permute-start | bytes 589832 | tf_op jit(solution)/shard_map/ppermute | solution.py:359
  180.8 1.4 collective-permute-start.33
  193.7 60.7 %all-to-all-start.3 = ((bf16[8,96,768]{2,1,0:T(8,128)(2,1)}), bf16[8,96,768]{2,1,0:T(8,128)(2,1)S(1)}, u32[]{:S(2)}, u32[]{:S(2)}) async-start(bf16[8,96,768]{2,1,0:T(8,128)(2,1)} %bitcast.45), calls=%async_computation.3 | async-start | bytes 2359296 | tf_op jit(solution)/shard_map/all_to_all | solution.py:386
  199.0 9.2 %copy-start.15 = (bf16[128,768]{1,0:T(8,128)(2,1)S(1)}, bf16[128,768]{1,0:T(8,128)(2,1)}, u32[]{:S(2)}) copy-start(bf16[128,768]{1,0:T(8,128)(2,1)} %get-tuple-element.81.refs_0_) | copy-start | bytes 589828
  203.6 1.7 collective-permute-start.35
  206.2 3.2 %collective-permute-start.41 = (f32[24,768]{1,0:T(8,128)}, f32[24,768]{1,0:T(8,128)S(1)}, u32[]{:S(2)}, u32[]{:S(2)}) collective-permute-start(f32[24,768]{1,0:T(8,128)} %get-tuple-element.113), channel_id=1, source_target_pairs={{0,1},{1,0},{2,3},{3,2},{4,5},{5,4},{6,7},{7,6},{8,9},{9,8},{10,11... | collective-permute-start | bytes 221192 | tf_op jit(solution)/shard_map/ppermute | solution.py:359
  206.4 5.0 %collective-permute-start.42 = (f32[24,768]{1,0:T(8,128)}, f32[24,768]{1,0:T(8,128)S(1)}, u32[]{:S(2)}, u32[]{:S(2)}) collective-permute-start(f32[24,768]{1,0:T(8,128)} %get-tuple-element.113), channel_id=1, source_target_pairs={{0,2},{1,3},{2,0},{3,1},{4,6},{5,7},{6,4},{7,5},{8,10},{9,11},{10,... | collective-permute-start | bytes 221192 | tf_op jit(solution)/shard_map/ppermute | solution.py:359
  207.7 4.8 %collective-permute-start.43 = (f32[24,768]{1,0:T(8,128)}, f32[24,768]{1,0:T(8,128)S(1)}, u32[]{:S(2)}, u32[]{:S(2)}) collective-permute-start(f32[24,768]{1,0:T(8,128)} %get-tuple-element.113), channel_id=1, source_target_pairs={{0,3},{1,2},{2,1},{3,0},{4,7},{5,6},{6,5},{7,4},{8,11},{9,10},{10,... | collective-permute-start | bytes 221192 | tf_op jit(solution)/shard_map/ppermute | solution.py:359
  208.2 14.6 %collective-permute-start.16 = (bf16[128,768]{1,0:T(8,128)(2,1)S(1)}, bf16[128,768]{1,0:T(8,128)(2,1)S(1)}, u32[]{:S(2)}, u32[]{:S(2)}) collective-permute-start(bf16[128,768]{1,0:T(8,128)(2,1)S(1)} %copy-done.15), channel_id=1, source_target_pairs={{0,2},{1,3},{2,0},{3,1},{4,6},{5,7},{6,4},{7,5},{8,10},{9,11},{10,... | collective-permute-start | bytes 589832 | tf_op jit(solution)/shard_map/ppermute | solution.py:359
  213.4 9.8 %collective-permute-start.44 = (f32[24,768]{1,0:T(8,128)S(1)}, f32[24,768]{1,0:T(8,128)S(1)}, u32[]{:S(2)}, u32[]{:S(2)}) collective-permute-start(f32[24,768]{1,0:T(8,128)S(1)} %add_add_fusion.1), channel_id=1, source_target_pairs={{0,4},{4,0},{8,12},{12,8},{1,5},{5,1},{9,13},{13,9},{2,6},{6,2},{1... | collective-permute-start | bytes 221192 | tf_op jit(solution)/shard_map/ppermute | solution.py:359
  215.5 16.6 %collective-permute-start.45 = (f32[24,768]{1,0:T(8,128)S(1)}, f32[24,768]{1,0:T(8,128)S(1)}, u32[]{:S(2)}, u32[]{:S(2)}) collective-permute-start(f32[24,768]{1,0:T(8,128)S(1)} %add_add_fusion.1), channel_id=1, source_target_pairs={{0,8},{4,12},{8,0},{12,4},{1,9},{5,13},{9,1},{13,5},{2,10},{6,14},... | collective-permute-start | bytes 221192 | tf_op jit(solution)/shard_map/ppermute | solution.py:359
  217.9 15.5 %collective-permute-start.46 = (f32[24,768]{1,0:T(8,128)S(1)}, f32[24,768]{1,0:T(8,128)S(1)}, u32[]{:S(2)}, u32[]{:S(2)}) collective-permute-start(f32[24,768]{1,0:T(8,128)S(1)} %add_add_fusion.1), channel_id=1, source_target_pairs={{0,12},{4,8},{8,4},{12,0},{1,13},{5,9},{9,5},{13,1},{2,14},{6,10},... | collective-permute-start | bytes 221192 | tf_op jit(solution)/shard_map/ppermute | solution.py:359
  222.7 16.9 %collective-permute-start.15 = (bf16[128,768]{1,0:T(8,128)(2,1)S(1)}, bf16[128,768]{1,0:T(8,128)(2,1)S(1)}, u32[]{:S(2)}, u32[]{:S(2)}) collective-permute-start(bf16[128,768]{1,0:T(8,128)(2,1)S(1)} %copy-done.15), channel_id=1, source_target_pairs={{0,1},{1,0},{2,3},{3,2},{4,5},{5,4},{6,7},{7,6},{8,9},{9,8},{10,11... | collective-permute-start | bytes 589832 | tf_op jit(solution)/shard_map/ppermute | solution.py:359
  222.7 16.8 %copy-start.16 = (bf16[128,768]{1,0:T(8,128)(2,1)}, bf16[128,768]{1,0:T(8,128)(2,1)S(1)}, u32[]{:S(2)}) copy-start(bf16[128,768]{1,0:T(8,128)(2,1)S(1)} %collective-permute-done.16.refs_2_) | copy-start | bytes 589828
  222.7 16.8 %collective-permute-start.17 = (bf16[128,768]{1,0:T(8,128)(2,1)S(1)}, bf16[128,768]{1,0:T(8,128)(2,1)S(1)}, u32[]{:S(2)}, u32[]{:S(2)}) collective-permute-start(bf16[128,768]{1,0:T(8,128)(2,1)S(1)} %collective-permute-done.16.refs_2_), channel_id=1, source_target_pairs={{0,1},{1,0},{2,3},{3,2},{4,5},{5,4},{6,7},{7,6},{8,9},{9,8},{10,11... | collective-permute-start | bytes 589832 | tf_op jit(solution)/shard_map/ppermute | solution.py:359
  223.2 21.5 %collective-permute-start.34 = (bf16[128,768]{1,0:T(8,128)(2,1)S(1)}, bf16[128,768]{1,0:T(8,128)(2,1)S(1)}, u32[]{:S(2)}, u32[]{:S(2)}) collective-permute-start(bf16[128,768]{1,0:T(8,128)(2,1)S(1)} %copy-done.34), channel_id=1, source_target_pairs={{0,1},{1,0},{2,3},{3,2},{4,5},{5,4},{6,7},{7,6},{8,9},{9,8},{10,11... | collective-permute-start | bytes 589832 | tf_op jit(solution)/shard_map/ppermute | solution.py:359
  232.1 12.6 %collective-permute-start.36 = (bf16[128,768]{1,0:T(8,128)(2,1)S(1)}, bf16[128,768]{1,0:T(8,128)(2,1)S(1)}, u32[]{:S(2)}, u32[]{:S(2)}) collective-permute-start(bf16[128,768]{1,0:T(8,128)(2,1)S(1)} %add_convert_fusion.3), channel_id=1, source_target_pairs={{0,2},{1,3},{2,0},{3,1},{4,6},{5,7},{6,4},{7,5},{8,10},{9,11},{10,... | collective-permute-start | bytes 589832 | tf_op jit(solution)/shard_map/ppermute | solution.py:359
  233.4 15.1 %collective-permute-start.47 = (f32[24,768]{1,0:T(8,128)S(1)}, f32[24,768]{1,0:T(8,128)S(1)}, u32[]{:S(2)}, u32[]{:S(2)}) collective-permute-start(f32[24,768]{1,0:T(8,128)S(1)} %add_add_fusion), channel_id=1, source_target_pairs={{0,16},{16,0},{1,17},{17,1},{2,18},{18,2},{3,19},{19,3},{4,20},{20... | collective-permute-start | bytes 221192 | tf_op jit(solution)/shard_map/ppermute | solution.py:359
  247.8 5.9 %collective-permute-start.38 = (bf16[128,768]{1,0:T(8,128)(2,1)}, bf16[128,768]{1,0:T(8,128)(2,1)S(1)}, u32[]{:S(2)}, u32[]{:S(2)}) collective-permute-start(bf16[128,768]{1,0:T(8,128)(2,1)} %shard_map.207.refs_0_), channel_id=1, source_target_pairs={{0,2},{1,3},{2,0},{3,1},{4,6},{5,7},{6,4},{7,5},{8,10},{9,11},{10,... | collective-permute-start | bytes 589832 | tf_op jit(solution)/shard_map/ppermute | solution.py:359
  248.5 7.3 %collective-permute-start.37 = (bf16[128,768]{1,0:T(8,128)(2,1)}, bf16[128,768]{1,0:T(8,128)(2,1)S(1)}, u32[]{:S(2)}, u32[]{:S(2)}) collective-permute-start(bf16[128,768]{1,0:T(8,128)(2,1)} %shard_map.207.refs_0_), channel_id=1, source_target_pairs={{0,1},{1,0},{2,3},{3,2},{4,5},{5,4},{6,7},{7,6},{8,9},{9,8},{10,11... | collective-permute-start | bytes 589832 | tf_op jit(solution)/shard_map/ppermute | solution.py:359
  253.7 2.2 collective-permute-start.39
  254.5 6.7 %collective-permute-start.40 = (bf16[96,768]{1,0:T(8,128)(2,1)S(1)}, bf16[96,768]{1,0:T(8,128)(2,1)S(1)}, u32[]{:S(2)}, u32[]{:S(2)}) collective-permute-start(bf16[96,768]{1,0:T(8,128)(2,1)S(1)} %reduce_sum.82), channel_id=1, source_target_pairs={{0,16},{16,0},{1,17},{17,1},{2,18},{18,2},{3,19},{19,3},{4,20},{20... | collective-permute-start | bytes 442376 | tf_op jit(solution)/shard_map/ppermute | solution.py:359
  (22 other events, 39.7 us)

commit v2 on v1

--- a/solution.py
+++ b/solution.py
@@ -104,7 +104,7 @@
     return jax.ShapeDtypeStruct(shape, dtype)
 
 
-STEP = 256
+STEP = 512
 
 
 def unpack_kernel(n_row, index_ref, *refs):
@@ -322,7 +322,7 @@
     flat_ref[:experts, :] = router_ref[...]
     flat_ref[experts : experts + 1, :] = mix_ref[...]
     flat_ref[experts + 1 : experts + 2, :] = total
-    flat_ref[experts + 8 :, pl.ds(pl.multiple_of(col_ref[0] * 128, 128), 128)] = table_ref[...]
+    flat_ref[experts + 2 :, pl.ds(pl.multiple_of(col_ref[0] * 128, 128), 128)] = table_ref[:6, :]
 
 
 def tokens_kernel(a_ref, b_ref, c_ref, grad_ref, cot_ref, tokens_ref, gain_ref, out_ref):
@@ -466,8 +466,6 @@
     slot = jnp.where(owner == col, chosen * slots + local_rank, -1)
     slot_ids = jnp.arange(total_slots, dtype=jnp.int32)
     slot_of_token = (slot_ids[:, None] == slot[None, :]).astype(BF)
-    slot_of_own = dot_t(slot_of_token, perm_own).astype(BF)
-    picked = dot_t(perm_own, hits.astype(BF))
 
     inputs = tokens.astype(F32)
     inverse = lax.rsqrt(jnp.mean(inputs * inputs, axis=1, keepdims=True) + EPS)
@@ -476,7 +474,6 @@
     inverse_perm = lax.rsqrt(jnp.mean(tokens_perm * tokens_perm, axis=1, keepdims=True) + EPS)
     tokens_own = tokens_perm[:own]
 
-    gains = jnp.stack([mix_gain, norm_gain])
     seg_row = segments.reshape(1, length)
     seg_col = jnp.sum(jnp.where(place[:, None] == place[None, :], seg_row, 0), axis=1, keepdims=True)
 
@@ -488,6 +485,10 @@
     cot_slots = hold(cot_slots, packed_rel[n_row // 2])
     cot_came = exchange(cot_slots.reshape(experts, slots, width), DR).reshape(total_slots, width)
     cot_blocks = gather_rel(cot_came, "col", n_col)
+    slot_of_own = dot_t(slot_of_token, perm_own).astype(BF)
+    picked = dot_t(perm_own, hits.astype(BF))
+    gains = jnp.stack([mix_gain, norm_gain])
+
     proj_blocks = gather_rel(proj_local, "col", n_col)
     qkv_rows, attended, probs, *att_parts = call(
         partial(front_kernel, n_col, heads),
@@ -599,7 +600,7 @@
     wgrad_came = exchange(wgrad.reshape(experts, block // n_dp, 4 * local), ("row", "dp"))
     *normed_parts, flat = call(
         partial(normed_kernel, n_col),
-        [sds((own, width), BF)] * n_col + [sds((experts + 16, width), F32)],
+        [sds((own, width), BF)] * n_col + [sds((experts + 8, width), F32)],
         [grad_qkv, perm, weight, z_perm, router_local, mix_local, table_local],
         2 * length * local * 3 * (width + length), scalars=[col.reshape(1).astype(jnp.int32)],
     )
@@ -617,7 +618,7 @@
     grad_qkv_weight = summed[:, : 3 * local].reshape(block, 3, local)
     grad_proj = summed[:, 3 * local :].T
 
-    packed = experts + 8
+    packed = experts + 2
     flat = sum_all(hold(flat, other), "col", n_col)
     flat = sum_all(flat, "row", n_row)
     flat = sum_all(flat, "dp", n_dp)

time: 265 us -> 260 us (0.981)
  no operation moved by 1% of the time
where the time goes in v2:
time: 260 us; the launch traced here: 259 us
  Pallas kernels  79.2 us (30%)
  waiting for transfers between devices  68 us (26%)
  starting transfers between devices  53.1 us (20%)
  blocking collectives  20 us (8%)
  local copies, waits for them, and re-layouts  15.8 us (6%)
  other arithmetic  14.1 us (5%)
  matrix products  7.91 us (3%)
    pallas_call x16, Pallas kernels, call(): pl.pallas_call(kernel, out_shape=tuple(outs), in_specs=[pl.BlockSpec(memo...  73.8 us
    ppermute x48, waiting for transfers between devices, swap(): return lax.ppermute(x, axes, [(i, i ^ mask) for i in range(count)])  68 us
    ppermute x48, starting transfers between devices, swap(): return lax.ppermute(x, axes, [(i, i ^ mask) for i in range(count)])  39.8 us
    all_to_all x1, blocking collectives, exchange(): return lax.all_to_all(x, axes, split_axis=0, concat_axis=0, tiled=True)  20 us
    all_to_all x3, starting transfers between devices, exchange(): return lax.all_to_all(x, axes, split_axis=0, concat_axis=0, tiled=True)  13.3 us
    unnamed x74, local copies, waits for them, and re-layouts  11.8 us
    dot_general x5, matrix products, dot_n(): return jnp.dot(a, b, precision=precision, preferred_element_type=F32)  6.23 us
  transfers between devices with their start and end apart: 51, of which 18 were waited for; matrix products, arithmetic and copies ran while one was open for 10% of the time, Pallas kernels for 26%

profile of v2, /device:TPU:0, one launch (start us, length us, event | category | flops | bytes accessed | tf_op | source)
XLA Modules:
  0.0 259.2 jit_solution(14756245878463272942)
XLA Ops:
  0.7 1.1 copy.42
  3.2 4.1 %collective-permute-start.1 = (bf16[192,768]{1,0:T(8,128)(2,1)S(1)}, bf16[192,768]{1,0:T(8,128)(2,1)S(1)}, u32[]{:S(2)}, u32[]{:S(2)}) collective-permute-start(bf16[192,768]{1,0:T(8,128)(2,1)S(1)} %pad_maximum_fusion.refs_0_), channel_id=1, source_target_pairs={{0,8},{4,12},{8,0},{12,4},{1,9},{5,13},{9,1},{13,5},{2,10},{6,14},... | collective-permute-start | bytes 884744 | tf_op jit(solution)/shard_map/ppermute | solution.py:359
  7.3 1.6 collective-permute-start
  9.5 1.2 fusion.4
  12.9 1.1 fusion.2.normed_ref.refs_13_
  14.0 6.7 %collective-permute-done.1.refs_2_ = bf16[192,768]{1,0:T(8,128)(2,1)S(1)} collective-permute-done((bf16[192,768]{1,0:T(8,128)(2,1)S(1)}, bf16[192,768]{1,0:T(8,128)(2,1)S(1)}, u32[]{:S(2)}, u32[]{:S(2)}) %collective-permute-start.1) | collective-permute-done | bytes 294944 | tf_op jit(solution)/shard_map/ppermute | solution.py:359
  22.3 1.1 convolution_convert_fusion
  23.4 5.6 %all-to-all-start = ((bf16[8,32,768]{2,1,0:T(8,128)(2,1)}), bf16[8,32,768]{2,1,0:T(8,128)(2,1)}, u32[]{:S(2)}, u32[]{:S(2)}) async-start(bf16[8,32,768]{2,1,0:T(8,128)(2,1)} %bitcast.8), calls=%async_computation | async-start | bytes 786432 | tf_op jit(solution)/shard_map/all_to_all | solution.py:386
  29.7 2.5 unpack.1
  32.2 1.6 collective-permute-start.7
  34.6 1.7 multiply_reduce_fusion
  36.3 6.7 %collective-permute-done.7.refs_6_ = bf16[768,192]{1,0:T(8,128)(2,1)} collective-permute-done((bf16[768,192]{1,0:T(8,128)(2,1)}, bf16[768,192]{1,0:T(8,128)(2,1)}, u32[]{:S(2)}, u32[]{:S(2)}) %collective-permute-start.7) | collective-permute-done | bytes 294944 | tf_op jit(solution)/shard_map/ppermute | solution.py:359
  44.1 2.9 %position_bias.1.bias_ref = f32[3,512,512]{2,1,0:T(8,128)} custom-call(f32[3,1024]{1,0:T(4,128)} %convolution_bitcast_fusion.off_ref), custom_call_target="tpu_custom_call" | custom-call | flops 3145728 | bytes 3145728 | tf_op jit(solution)/shard_map/position_bias/pallas_call | solution.py:63
  47.0 6.7 %shard_map.195 = (bf16[512,576]{1,0:T(8,128)(2,1)}, bf16[512,192]{1,0:T(8,128)(2,1)}, bf16[3,512,512]{2,1,0:T(8,128)(2,1)}, bf16[128,192]{1,0:T(8,128)(2,1)}, bf...) custom-call(bf16[512,768]{1,0:T(8,128)(2,1)} %fusion.2.normed_ref.refs_13_, ...), custom_call_target="tpu_custom_call" | custom-call | flops 754974720 | bytes 7901184 | tf_op jit(solution)/shard_map/pallas_call | solution.py:89
  54.2 1.5 collective-permute-start.4
  57.1 1.6 collective-permute-done.4.refs_2_
  58.7 1.6 collective-permute-done.5.refs_3_
  60.9 4.4 %shard_map.196 = (f32[128,768]{1,0:T(8,128)}, f32[128,8]{1,0:T(8,128)}, f32[128,1]{1,0:T(8,128)}, bf16[256,896]{1,0:T(8,128)(2,1)}) custom-call(bf16[128,192]{1,0:T(8,128)(2,1)} %get-tuple-element.67.refs_0_.refs_4_, bf16[128,192]{1,0:T(8,128)(2,1)} %copy-done.27, bf16[128,192]{1,0:T(8,128)(2,1)} %copy-done.28, bf16[128,192]{1,0:T(8,128)(2,1)} %copy-done.29, ...), custom_call_target="tpu_custom_call" | custom-call | flops 201326592 | bytes 2726400 | tf_op jit(solution)/shard_map/pallas_call | solution.py:89
  65.3 20.0 %all_to_all.20 = bf16[8,32,896]{2,1,0:T(8,128)(2,1)} all-to-all(bf16[8,32,896]{2,1,0:T(8,128)(2,1)} %bitcast.47), channel_id=1, replica_groups=mesh['dp'=2,'row'=4,'col'=4] {'dp','row'}, dimensions={0} | all-to-all | bytes 917504 | tf_op jit(solution)/shard_map/all_to_all | solution.py:386
  86.4 10.5 %collective-permute-done.11.refs_0_ = bf16[256,896]{1,0:T(8,128)(2,1)S(1)} collective-permute-done((bf16[256,896]{1,0:T(8,128)(2,1)}, bf16[256,896]{1,0:T(8,128)(2,1)S(1)}, u32[]{:S(2)}, u32[]{:S(2)}) %collective-permute-start.11) | collective-permute-done | bytes 458784 | tf_op jit(solution)/shard_map/ppermute | solution.py:359
  97.7 1.1 collective-permute-start.20
  99.1 10.4 %collective-permute-done.20.refs_2_ = bf16[256,768]{1,0:T(8,128)(2,1)S(1)} collective-permute-done((bf16[256,768]{1,0:T(8,128)(2,1)}, bf16[256,768]{1,0:T(8,128)(2,1)S(1)}, u32[]{:S(2)}, u32[]{:S(2)}) %collective-permute-start.20) | collective-permute-done | bytes 393248 | tf_op jit(solution)/shard_map/ppermute | solution.py:359
  110.3 5.1 %shard_map.198 = (bf16[256,768]{1,0:T(8,128)(2,1)}, bf16[256,768]{1,0:T(8,128)(2,1)}, bf16[512,768]{1,0:T(8,128)(2,1)}, f32[512,768]{1,0:T(8,128)}) custom-call(bf16[256,896]{1,0:T(8,128)(2,1)} %copy-done.7, bf16[256,896]{1,0:T(8,128)(2,1)} %copy-done.8, bf16[768,768]{1,0:T(8,128)(2,1)} %bitcast.32, bf16[768,768]{1,0:T(8,128)(2,1)} %bitcast.36), custom_call_target="tpu_custom_call" | custom-call | flops 1207959552 | bytes 6422528 | tf_op jit(solution)/shard_map/pallas_call | solution.py:89
  115.9 5.1 %shard_map.197 = (bf16[256,768]{1,0:T(8,128)(2,1)}, bf16[256,768]{1,0:T(8,128)(2,1)}, bf16[512,768]{1,0:T(8,128)(2,1)}, f32[512,768]{1,0:T(8,128)}) custom-call(bf16[256,896]{1,0:T(8,128)(2,1)} %bitcast.11.refs_0_, bf16[256,896]{1,0:T(8,128)(2,1)} %collective-permute-done.9.refs_1_, bf16[768,768]{1,0:T(8,128)(2,1)} %bitcast.33, bf16[768,768]{1,0:T(8,128)(2,1)} %bitcast.37), custom_call_target="tpu_custom_call" | custom-call | flops 1207959552 | bytes 6422528 | tf_op jit(solution)/shard_map/pallas_call | solution.py:89
  121.1 5.5 %shard_map.202 = (bf16[256,768]{1,0:T(8,128)(2,1)}, bf16[256,768]{1,0:T(8,128)(2,1)}, bf16[512,768]{1,0:T(8,128)(2,1)}, bf16[512,768]{1,0:T(8,128)(2,1)}, bf16[512,768]{1,0:T(8,128)(2,1)}) custom-call(bf16[256,896]{1,0:T(8,128)(2,1)} %copy-done.7, bf16[256,896]{1,0:T(8,128)(2,1)} %copy-done.8, bf16[256,768]{1,0:T(8,128)(2,1)} %copy-done.12, ...), custom_call_target="tpu_custom_call" | custom-call | flops 1207959552 | bytes 8781824 | tf_op jit(solution)/shard_map/pallas_call | solution.py:89
  127.1 1.9 add_convert_fusion.2
  129.0 1.1 collective-permute-start.14
  130.1 5.5 %shard_map.201 = (bf16[256,768]{1,0:T(8,128)(2,1)}, bf16[256,768]{1,0:T(8,128)(2,1)}, bf16[512,768]{1,0:T(8,128)(2,1)}, bf16[512,768]{1,0:T(8,128)(2,1)}, bf16[512,768]{1,0:T(8,128)(2,1)}) custom-call(bf16[256,896]{1,0:T(8,128)(2,1)} %bitcast.11.refs_0_, bf16[256,896]{1,0:T(8,128)(2,1)} %collective-permute-done.9.refs_1_, bf16[256,768]{1,0:T(8,128)(2,1)} %bitcast.9.refs_2_, ...), custom_call_target="tpu_custom_call" | custom-call | flops 1207959552 | bytes 8781824 | tf_op jit(solution)/shard_map/pallas_call | solution.py:89
  135.8 2.0 add_convert_fusion
  138.7 2.1 collective-permute-done.14
  140.8 2.0 add_convert_fusion.1
  142.8 3.7 %all-to-all-start.2 = ((bf16[8,32,768]{2,1,0:T(8,128)(2,1)}), bf16[8,32,768]{2,1,0:T(8,128)(2,1)S(1)}, u32[]{:S(2)}, u32[]{:S(2)}) async-start(bf16[8,32,768]{2,1,0:T(8,128)(2,1)} %bitcast.44), calls=%async_computation.2 | async-start | bytes 786432 | tf_op jit(solution)/shard_map/all_to_all | solution.py:386
  146.5 3.0 %collective-permute-done.23.c_ref = bf16[256,768]{1,0:T(8,128)(2,1)} collective-permute-done((bf16[256,768]{1,0:T(8,128)(2,1)}, bf16[256,768]{1,0:T(8,128)(2,1)}, u32[]{:S(2)}, u32[]{:S(2)}) %collective-permute-start.23) | collective-permute-done | bytes 393248 | tf_op jit(solution)/shard_map/ppermute | solution.py:359
  149.4 2.0 shard_map.203
  151.5 1.4 collective-permute-start.25
  152.9 2.9 %collective-permute-start.26 = (bf16[32,768]{1,0:T(8,128)(2,1)}, bf16[32,768]{1,0:T(8,128)(2,1)}, u32[]{:S(2)}, u32[]{:S(2)}) collective-permute-start(bf16[32,768]{1,0:T(8,128)(2,1)} %get-tuple-element.92), channel_id=1, source_target_pairs={{0,12},{4,8},{8,4},{12,0},{16,28},{20,24},{24,20},{28,16},{1,13},{... | collective-permute-start | bytes 147464 | tf_op jit(solution)/shard_map/ppermute | solution.py:359
  156.6 4.1 %collective-permute-start.29 = (bf16[32,768]{1,0:T(8,128)(2,1)}, bf16[32,768]{1,0:T(8,128)(2,1)}, u32[]{:S(2)}, u32[]{:S(2)}) collective-permute-start(bf16[32,768]{1,0:T(8,128)(2,1)} %get-tuple-element.95), channel_id=1, source_target_pairs={{0,24},{4,28},{8,16},{12,20},{16,8},{20,12},{24,0},{28,4},{1,25},{... | collective-permute-start | bytes 147464 | tf_op jit(solution)/shard_map/ppermute | solution.py:359
  160.7 2.0 collective-permute-done.25.refs_2_
  162.7 1.4 collective-permute-start.30
  164.1 2.2 fusion.12.refs_15_.cot_ref
  167.1 2.3 shard_map.199
  169.8 3.4 %shard_map.204 = (f32[128,768]{1,0:T(8,128)}, bf16[128,768]{1,0:T(8,128)(2,1)}, f32[8,768]{1,0:T(8,128)}, f32[1,768]{1,0:T(1,128)}) custom-call(s32[1]{0:T(128)} %bitcast.17.me_ref, f32[128,768]{1,0:T(8,128)} %get-tuple-element.82.mixed_ref, bf16[32,768]{1,0:T(8,128)(2,1)} %get-tuple-element.89.refs_0_, bf16[32,768]{1,0:T(8,128)(2,1)} %collective-permute-done.24.refs_1_, ...), custom_call_target="tpu_custom_call" | custom-call | flops 50331648 | bytes 2295296 | tf_op jit(solution)/shard_map/pallas_call | solution.py:89
  173.2 1.2 collective-permute-start.32
  174.4 5.2 %collective-permute-done.32.refs_2_ = bf16[128,768]{1,0:T(8,128)(2,1)S(1)} collective-permute-done((bf16[128,768]{1,0:T(8,128)(2,1)}, bf16[128,768]{1,0:T(8,128)(2,1)S(1)}, u32[]{:S(2)}, u32[]{:S(2)}) %collective-permute-start.32) | collective-permute-done | bytes 196640 | tf_op jit(solution)/shard_map/ppermute | solution.py:359
  179.6 1.4 collective-permute-done.33.refs_3_
  181.7 9.5 %shard_map.205 = (bf16[768,768]{1,0:T(8,128)(2,1)}, bf16[512,576]{1,0:T(8,128)(2,1)}, f32[8,128]{1,0:T(8,128)}) custom-call(bf16[128,768]{1,0:T(8,128)(2,1)} %get-tuple-element.98.refs_0_, bf16[128,768]{1,0:T(8,128)(2,1)} %copy-done.22, bf16[128,768]{1,0:T(8,128)(2,1)} %copy-done.20, bf16[128,768]{1,0:T(8,128)(2,1)} %copy-done.24, ...), custom_call_target="tpu_custom_call" | custom-call | flops 1258291200 | bytes 7245824 | tf_op jit(solution)/shard_map/pallas_call | solution.py:89
  191.2 4.0 %all-to-all-start.3 = ((bf16[8,96,768]{2,1,0:T(8,128)(2,1)}), bf16[8,96,768]{2,1,0:T(8,128)(2,1)S(1)}, u32[]{:S(2)}, u32[]{:S(2)}) async-start(bf16[8,96,768]{2,1,0:T(8,128)(2,1)} %bitcast.45), calls=%async_computation.3 | async-start | bytes 2359296 | tf_op jit(solution)/shard_map/all_to_all | solution.py:386
  195.2 1.3 broadcast_multiply_fusion.z_ref
  196.5 4.6 %shard_map.206 = (bf16[128,768]{1,0:T(8,128)(2,1)}, bf16[128,768]{1,0:T(8,128)(2,1)}, bf16[128,768]{1,0:T(8,128)(2,1)}, bf16[128,768]{1,0:T(8,128)(2,1)}, f32[16,768]{1,0:T(8,128)}) custom-call(s32[1]{0:T(128)} %bitcast.16.col_ref, bf16[512,576]{1,0:T(8,128)(2,1)} %get-tuple-element.102.gq_ref, bf16[512,512]{1,0:T(8,128)(2,1)} %get-tuple-element.161.perm_ref, ...), custom_call_target="tpu_custom_call" | custom-call | flops 754974720 | bytes 4439040 | tf_op jit(solution)/shard_map/pallas_call | solution.py:89
  201.1 1.6 collective-permute-done.35
  204.0 1.3 collective-permute-start.42
  205.7 1.3 collective-permute-start.16
  207.0 1.3 collective-permute-done.42
  210.0 2.1 collective-permute-start.44
  212.1 2.4 collective-permute-start.45
  214.6 4.7 %shard_map.210 = f32[768,768]{1,0:T(8,128)} custom-call(bf16[512,768]{1,0:T(8,128)(2,1)} %get-tuple-element.118.refs_0_, bf16[512,768]{1,0:T(8,128)(2,1)} %get-tuple-element.119.refs_1_, bf16[512,768]{1,0:T(8,128)(2,1)} %get-tuple-element.120.refs_2_, bf16[512,768]{1,0:T(8,128)(2,1)} %get-tuple-element.121.refs_3_), custom_call_target="tpu_custom_call" | custom-call | flops 1207959552 | bytes 5505024 | tf_op jit(solution)/shard_map/pallas_call | solution.py:89
  219.9 7.9 %collective-permute-done.45 = f32[16,768]{1,0:T(8,128)S(1)} collective-permute-done((f32[16,768]{1,0:T(8,128)S(1)}, f32[16,768]{1,0:T(8,128)S(1)}, u32[]{:S(2)}, u32[]{:S(2)}) %collective-permute-start.45) | collective-permute-done | bytes 49184 | tf_op jit(solution)/shard_map/ppermute | solution.py:359
  227.8 1.3 collective-permute-start.36
  229.1 1.5 collective-permute-start.47
  230.5 4.7 %shard_map.209 = f32[768,768]{1,0:T(8,128)} custom-call(bf16[512,768]{1,0:T(8,128)(2,1)} %get-tuple-element.114.refs_0_, bf16[512,768]{1,0:T(8,128)(2,1)} %get-tuple-element.115.refs_1_, bf16[512,768]{1,0:T(8,128)(2,1)} %get-tuple-element.116.refs_2_, bf16[512,768]{1,0:T(8,128)(2,1)} %get-tuple-element.117.refs_3_), custom_call_target="tpu_custom_call" | custom-call | flops 1207959552 | bytes 5505024 | tf_op jit(solution)/shard_map/pallas_call | solution.py:89
  236.6 3.8 %shard_map.200 = f32[512,768]{1,0:T(8,128)} custom-call(bf16[128,768]{1,0:T(8,128)(2,1)} %get-tuple-element.81.refs_0_, bf16[128,768]{1,0:T(8,128)(2,1)} %copy-done.17, bf16[128,768]{1,0:T(8,128)(2,1)} %copy-done.16, bf16[128,768]{1,0:T(8,128)(2,1)} %copy-done.18, bf16[512,512]{1,0:T(8,128)(2,1)} %get-tuple-element.160.refs_4_.refs_9_, bf16[512,768]{1,0:T(8,128)(2,1)} %refs_5_.2), custom_call_target="tpu_custom_call" | custom-call | flops 402653184 | bytes 3670016 | tf_op jit(solution)/shard_map/pallas_call | solution.py:89
  241.1 2.4 shard_map.207.refs_0_
  244.8 4.5 %collective-permute-done.38.refs_2_ = bf16[128,768]{1,0:T(8,128)(2,1)S(1)} collective-permute-done((bf16[128,768]{1,0:T(8,128)(2,1)}, bf16[128,768]{1,0:T(8,128)(2,1)S(1)}, u32[]{:S(2)}, u32[]{:S(2)}) %collective-permute-start.38) | collective-permute-done | bytes 196640 | tf_op jit(solution)/shard_map/ppermute | solution.py:359
  252.9 4.0 %shard_map.208 = f32[512,768]{1,0:T(8,128)} custom-call(bf16[128,768]{1,0:T(8,128)(2,1)} %shard_map.207.refs_0_, bf16[128,768]{1,0:T(8,128)(2,1)} %copy-done.21, bf16[128,768]{1,0:T(8,128)(2,1)} %copy-done.19, bf16[128,768]{1,0:T(8,128)(2,1)} %copy-done.23, bf16[512,512]{1,0:T(8,128)(2,1)} %get-tuple-element.160.refs_4_.refs_9_, f32[512,768]{1,0:T(8,128)} %refs_5_.3), custom_call_target="tpu_custom_call" | custom-call | flops 402653184 | bytes 4456448 | tf_op jit(solution)/shard_map/pallas_call | solution.py:89
  (174 shorter events, 31.4 us)
Async XLA Ops:
  0.6 11.3 %copy-start = (f32[32,3]{0,1:T(4,128)S(1)}, f32[32,3]{0,1:T(4,128)}, u32[]{:S(2)}) copy-start(f32[32,3]{0,1:T(4,128)} %param.19) | copy-start | bytes 1156
  0.7 8.2 %copy-start.30 = (s32[512,1]{0,1:T(1,128)S(1)}, s32[512,1]{0,1:T(1,128)}, u32[]{:S(2)}) copy-start(s32[512,1]{0,1:T(1,128)} %param.14) | copy-start | bytes 6148
  2.0 9.7 %copy-start.2 = (bf16[512,768]{1,0:T(8,128)(2,1)S(1)}, bf16[512,768]{1,0:T(8,128)(2,1)}, u32[]{:S(2)}) copy-start(bf16[512,768]{1,0:T(8,128)(2,1)} %refs_5_.2) | copy-start | bytes 2359300
  3.2 9.7 %copy-start.6 = (bf16[192,768]{1,0:T(8,128)(2,1)}, bf16[192,768]{1,0:T(8,128)(2,1)S(1)}, u32[]{:S(2)}) copy-start(bf16[192,768]{1,0:T(8,128)(2,1)S(1)} %pad_maximum_fusion.refs_0_) | copy-start | bytes 884740
  3.2 17.6 %collective-permute-start.1 = (bf16[192,768]{1,0:T(8,128)(2,1)S(1)}, bf16[192,768]{1,0:T(8,128)(2,1)S(1)}, u32[]{:S(2)}, u32[]{:S(2)}) collective-permute-start(bf16[192,768]{1,0:T(8,128)(2,1)S(1)} %pad_maximum_fusion.refs_0_), channel_id=1, source_target_pairs={{0,8},{4,12},{8,0},{12,4},{1,9},{5,13},{9,1},{13,5},{2,10},{6,14},... | collective-permute-start | bytes 884744 | tf_op jit(solution)/shard_map/ppermute | solution.py:359
  7.3 21.7 %collective-permute-start = (bf16[192,768]{1,0:T(8,128)(2,1)S(1)}, bf16[192,768]{1,0:T(8,128)(2,1)S(1)}, u32[]{:S(2)}, u32[]{:S(2)}) collective-permute-start(bf16[192,768]{1,0:T(8,128)(2,1)S(1)} %pad_maximum_fusion.refs_0_), channel_id=1, source_target_pairs={{0,4},{4,0},{8,12},{12,8},{1,5},{5,1},{9,13},{13,9},{2,6},{6,2},{1... | collective-permute-start | bytes 884744 | tf_op jit(solution)/shard_map/ppermute | solution.py:359
  10.7 23.1 %copy-start.9 = (pred[512,512]{1,0:T(32,128)(4,1)}, pred[512,512]{1,0:T(32,128)(4,1)S(1)}, u32[]{:S(2)}) copy-start(pred[512,512]{1,0:T(32,128)(4,1)S(1)} %get-tuple-element.162) | copy-start | bytes 786436
  11.7 10.6 %copy-start.1 = (f32[512,768]{1,0:T(8,128)S(1)}, f32[512,768]{1,0:T(8,128)}, u32[]{:S(2)}) copy-start(f32[512,768]{1,0:T(8,128)} %refs_5_.3) | copy-start | bytes 4718596
  20.8 8.2 %collective-permute-start.2 = (bf16[192,768]{1,0:T(8,128)(2,1)S(1)}, bf16[192,768]{1,0:T(8,128)(2,1)}, u32[]{:S(2)}, u32[]{:S(2)}) collective-permute-start(bf16[192,768]{1,0:T(8,128)(2,1)S(1)} %collective-permute-done.1.refs_2_), channel_id=1, source_target_pairs={{0,4},{4,0},{8,12},{12,8},{1,5},{5,1},{9,13},{13,9},{2,6},{6,2},{1... | collective-permute-start | bytes 884744 | tf_op jit(solution)/shard_map/ppermute | solution.py:359
  23.4 41.9 %all-to-all-start = ((bf16[8,32,768]{2,1,0:T(8,128)(2,1)}), bf16[8,32,768]{2,1,0:T(8,128)(2,1)}, u32[]{:S(2)}, u32[]{:S(2)}) async-start(bf16[8,32,768]{2,1,0:T(8,128)(2,1)} %bitcast.8), calls=%async_computation | async-start | bytes 786432 | tf_op jit(solution)/shard_map/all_to_all | solution.py:386
  32.2 10.9 %copy-start.32 = (s32[1,512]{1,0:T(1,128)S(1)}, s32[1,512]{1,0:T(1,128)}, u32[]{:S(2)}) copy-start(s32[1,512]{1,0:T(1,128)} %seg_row_ref.1) | copy-start | bytes 6148
  32.2 11.9 %copy-start.33 = (f32[768]{0:T(1024)S(1)}, f32[768]{0:T(1024)}, u32[]{:S(2)}) copy-start(f32[768]{0:T(1024)} %param.16) | copy-start | bytes 9220
  32.2 10.9 %collective-permute-start.7 = (bf16[768,192]{1,0:T(8,128)(2,1)}, bf16[768,192]{1,0:T(8,128)(2,1)}, u32[]{:S(2)}, u32[]{:S(2)}) collective-permute-start(bf16[768,192]{1,0:T(8,128)(2,1)} %get-tuple-element.71.refs_4_.refs_8_), channel_id=1, source_target_pairs={{0,2},{1,3},{2,0},{3,1},{4,6},{5,7},{6,4},{7,5},{8,10},{9,11},{10,... | collective-permute-start | bytes 884744 | tf_op jit(solution)/shard_map/ppermute | solution.py:359
  36.3 24.0 %collective-permute-start.6 = (bf16[768,192]{1,0:T(8,128)(2,1)S(1)}, bf16[768,192]{1,0:T(8,128)(2,1)}, u32[]{:S(2)}, u32[]{:S(2)}) collective-permute-start(bf16[768,192]{1,0:T(8,128)(2,1)S(1)} %copy-done.5), channel_id=1, source_target_pairs={{0,1},{1,0},{2,3},{3,2},{4,5},{5,4},{6,7},{7,6},{8,9},{9,8},{10,11... | collective-permute-start | bytes 884744 | tf_op jit(solution)/shard_map/ppermute | solution.py:359
  43.0 17.3 %collective-permute-start.8 = (bf16[768,192]{1,0:T(8,128)(2,1)}, bf16[768,192]{1,0:T(8,128)(2,1)}, u32[]{:S(2)}, u32[]{:S(2)}) collective-permute-start(bf16[768,192]{1,0:T(8,128)(2,1)} %collective-permute-done.7.refs_6_), channel_id=1, source_target_pairs={{0,1},{1,0},{2,3},{3,2},{4,5},{5,4},{6,7},{7,6},{8,9},{9,8},{10,11... | collective-permute-start | bytes 884744 | tf_op jit(solution)/shard_map/ppermute | solution.py:359
  47.0 9.4 %copy-start.3 = (f32[512,768]{1,0:T(8,128)S(1)}, f32[512,768]{1,0:T(8,128)}, u32[]{:S(2)}) copy-start(f32[512,768]{1,0:T(8,128)} %get-tuple-element.164) | copy-start | bytes 4718596
  53.7 3.4 %collective-permute-start.3 = (bf16[128,192]{1,0:T(8,128)(2,1)}, bf16[128,192]{1,0:T(8,128)(2,1)S(1)}, u32[]{:S(2)}, u32[]{:S(2)}) collective-permute-start(bf16[128,192]{1,0:T(8,128)(2,1)} %get-tuple-element.68.refs_5_), channel_id=1, source_target_pairs={{0,1},{1,0},{2,3},{3,2},{4,5},{5,4},{6,7},{7,6},{8,9},{9,8},{10,11... | collective-permute-start | bytes 147464 | tf_op jit(solution)/shard_map/ppermute | solution.py:359
  54.2 4.5 %collective-permute-start.4 = (bf16[128,192]{1,0:T(8,128)(2,1)}, bf16[128,192]{1,0:T(8,128)(2,1)S(1)}, u32[]{:S(2)}, u32[]{:S(2)}) collective-permute-start(bf16[128,192]{1,0:T(8,128)(2,1)} %get-tuple-element.69.refs_6_), channel_id=1, source_target_pairs={{0,2},{1,3},{2,0},{3,1},{4,6},{5,7},{6,4},{7,5},{8,10},{9,11},{10,... | collective-permute-start | bytes 147464 | tf_op jit(solution)/shard_map/ppermute | solution.py:359
  55.8 4.6 %collective-permute-start.5 = (bf16[128,192]{1,0:T(8,128)(2,1)}, bf16[128,192]{1,0:T(8,128)(2,1)S(1)}, u32[]{:S(2)}, u32[]{:S(2)}) collective-permute-start(bf16[128,192]{1,0:T(8,128)(2,1)} %get-tuple-element.70.refs_7_), channel_id=1, source_target_pairs={{0,3},{1,2},{2,1},{3,0},{4,7},{5,6},{6,5},{7,4},{8,11},{9,10},{10,... | collective-permute-start | bytes 147464 | tf_op jit(solution)/shard_map/ppermute | solution.py:359
  85.4 11.6 %collective-permute-start.11 = (bf16[256,896]{1,0:T(8,128)(2,1)}, bf16[256,896]{1,0:T(8,128)(2,1)S(1)}, u32[]{:S(2)}, u32[]{:S(2)}) collective-permute-start(bf16[256,896]{1,0:T(8,128)(2,1)} %bitcast.11.refs_0_), channel_id=1, source_target_pairs={{0,2},{1,3},{2,0},{3,1},{4,6},{5,7},{6,4},{7,5},{8,10},{9,11},{10,... | collective-permute-start | bytes 1376264 | tf_op jit(solution)/shard_map/ppermute | solution.py:359
  97.7 11.7 %collective-permute-start.12 = (bf16[256,896]{1,0:T(8,128)(2,1)S(1)}, bf16[256,896]{1,0:T(8,128)(2,1)S(1)}, u32[]{:S(2)}, u32[]{:S(2)}) collective-permute-start(bf16[256,896]{1,0:T(8,128)(2,1)S(1)} %collective-permute-done.11.refs_0_), channel_id=1, source_target_pairs={{0,1},{1,0},{2,3},{3,2},{4,5},{5,4},{6,7},{7,6},{8,9},{9,8},{10,11... | collective-permute-start | bytes 1376264 | tf_op jit(solution)/shard_map/ppermute | solution.py:359
  97.7 11.7 %collective-permute-start.20 = (bf16[256,768]{1,0:T(8,128)(2,1)}, bf16[256,768]{1,0:T(8,128)(2,1)S(1)}, u32[]{:S(2)}, u32[]{:S(2)}) collective-permute-start(bf16[256,768]{1,0:T(8,128)(2,1)} %bitcast.9.refs_2_), channel_id=1, source_target_pairs={{0,2},{1,3},{2,0},{3,1},{4,6},{5,7},{6,4},{7,5},{8,10},{9,11},{10,... | collective-permute-start | bytes 1179656 | tf_op jit(solution)/shard_map/ppermute | solution.py:359
  98.9 17.1 %collective-permute-start.9 = (bf16[256,896]{1,0:T(8,128)(2,1)}, bf16[256,896]{1,0:T(8,128)(2,1)}, u32[]{:S(2)}, u32[]{:S(2)}) collective-permute-start(bf16[256,896]{1,0:T(8,128)(2,1)} %bitcast.11.refs_0_), channel_id=1, source_target_pairs={{0,1},{1,0},{2,3},{3,2},{4,5},{5,4},{6,7},{7,6},{8,9},{9,8},{10,11... | collective-permute-start | bytes 1376264 | tf_op jit(solution)/shard_map/ppermute | solution.py:359
  109.4 11.6 %copy-start.12 = (bf16[256,768]{1,0:T(8,128)(2,1)}, bf16[256,768]{1,0:T(8,128)(2,1)S(1)}, u32[]{:S(2)}) copy-start(bf16[256,768]{1,0:T(8,128)(2,1)S(1)} %collective-permute-done.20.refs_2_) | copy-start | bytes 1179652
  109.5 11.6 %collective-permute-start.21 = (bf16[256,768]{1,0:T(8,128)(2,1)S(1)}, bf16[256,768]{1,0:T(8,128)(2,1)}, u32[]{:S(2)}, u32[]{:S(2)}) collective-permute-start(bf16[256,768]{1,0:T(8,128)(2,1)S(1)} %collective-permute-done.20.refs_2_), channel_id=1, source_target_pairs={{0,1},{1,0},{2,3},{3,2},{4,5},{5,4},{6,7},{7,6},{8,9},{9,8},{10,11... | collective-permute-start | bytes 1179656 | tf_op jit(solution)/shard_map/ppermute | solution.py:359
  115.4 11.7 %collective-permute-start.13 = (bf16[256,768]{1,0:T(8,128)(2,1)}, bf16[256,768]{1,0:T(8,128)(2,1)}, u32[]{:S(2)}, u32[]{:S(2)}) collective-permute-start(bf16[256,768]{1,0:T(8,128)(2,1)} %get-tuple-element.78), channel_id=1, source_target_pairs={{0,1},{1,0},{2,3},{3,2},{4,5},{5,4},{6,7},{7,6},{8,9},{9,8},{10,11... | collective-permute-start | bytes 1179656 | tf_op jit(solution)/shard_map/ppermute | solution.py:359
  115.9 14.2 %collective-permute-start.18 = (bf16[256,768]{1,0:T(8,128)(2,1)}, bf16[256,768]{1,0:T(8,128)(2,1)}, u32[]{:S(2)}, u32[]{:S(2)}) collective-permute-start(bf16[256,768]{1,0:T(8,128)(2,1)} %bitcast.9.refs_2_), channel_id=1, source_target_pairs={{0,1},{1,0},{2,3},{3,2},{4,5},{5,4},{6,7},{7,6},{8,9},{9,8},{10,11... | collective-permute-start | bytes 1179656 | tf_op jit(solution)/shard_map/ppermute | solution.py:359
  126.6 9.2 %collective-permute-start.22 = (bf16[256,768]{1,0:T(8,128)(2,1)}, bf16[256,768]{1,0:T(8,128)(2,1)}, u32[]{:S(2)}, u32[]{:S(2)}) collective-permute-start(bf16[256,768]{1,0:T(8,128)(2,1)} %get-tuple-element.88), channel_id=1, source_target_pairs={{0,1},{1,0},{2,3},{3,2},{4,5},{5,4},{6,7},{7,6},{8,9},{9,8},{10,11... | collective-permute-start | bytes 1179656 | tf_op jit(solution)/shard_map/ppermute | solution.py:359
  127.1 11.6 %collective-permute-start.10 = (bf16[256,768]{1,0:T(8,128)(2,1)}, bf16[256,768]{1,0:T(8,128)(2,1)}, u32[]{:S(2)}, u32[]{:S(2)}) collective-permute-start(bf16[256,768]{1,0:T(8,128)(2,1)} %get-tuple-element.76), channel_id=1, source_target_pairs={{0,1},{1,0},{2,3},{3,2},{4,5},{5,4},{6,7},{7,6},{8,9},{9,8},{10,11... | collective-permute-start | bytes 1179656 | tf_op jit(solution)/shard_map/ppermute | solution.py:359
  129.0 11.8 %collective-permute-start.14 = (bf16[256,768]{1,0:T(8,128)(2,1)}, bf16[256,768]{1,0:T(8,128)(2,1)}, u32[]{:S(2)}, u32[]{:S(2)}) collective-permute-start(bf16[256,768]{1,0:T(8,128)(2,1)} %add_convert_fusion.2), channel_id=1, source_target_pairs={{0,2},{1,3},{2,0},{3,1},{4,6},{5,7},{6,4},{7,5},{8,10},{9,11},{10,... | collective-permute-start | bytes 1179656 | tf_op jit(solution)/shard_map/ppermute | solution.py:359
  130.1 10.6 %copy-start.10 = (bf16[256,768]{1,0:T(8,128)(2,1)S(1)}, bf16[256,768]{1,0:T(8,128)(2,1)}, u32[]{:S(2)}) copy-start(bf16[256,768]{1,0:T(8,128)(2,1)} %get-tuple-element.75) | copy-start | bytes 1179652
  135.6 10.8 %collective-permute-start.19 = (bf16[256,768]{1,0:T(8,128)(2,1)}, bf16[256,768]{1,0:T(8,128)(2,1)}, u32[]{:S(2)}, u32[]{:S(2)}) collective-permute-start(bf16[256,768]{1,0:T(8,128)(2,1)} %get-tuple-element.85), channel_id=1, source_target_pairs={{0,1},{1,0},{2,3},{3,2},{4,5},{5,4},{6,7},{7,6},{8,9},{9,8},{10,11... | collective-permute-start | bytes 1179656 | tf_op jit(solution)/shard_map/ppermute | solution.py:359
  137.8 11.7 %collective-permute-start.23 = (bf16[256,768]{1,0:T(8,128)(2,1)}, bf16[256,768]{1,0:T(8,128)(2,1)}, u32[]{:S(2)}, u32[]{:S(2)}) collective-permute-start(bf16[256,768]{1,0:T(8,128)(2,1)} %add_convert_fusion), channel_id=1, source_target_pairs={{0,2},{1,3},{2,0},{3,1},{4,6},{5,7},{6,4},{7,5},{8,10},{9,11},{10,... | collective-permute-start | bytes 1179656 | tf_op jit(solution)/shard_map/ppermute | solution.py:359
  142.8 23.6 %all-to-all-start.2 = ((bf16[8,32,768]{2,1,0:T(8,128)(2,1)}), bf16[8,32,768]{2,1,0:T(8,128)(2,1)S(1)}, u32[]{:S(2)}, u32[]{:S(2)}) async-start(bf16[8,32,768]{2,1,0:T(8,128)(2,1)} %bitcast.44), calls=%async_computation.2 | async-start | bytes 786432 | tf_op jit(solution)/shard_map/all_to_all | solution.py:386
  151.5 5.1 %collective-permute-start.24 = (bf16[32,768]{1,0:T(8,128)(2,1)}, bf16[32,768]{1,0:T(8,128)(2,1)}, u32[]{:S(2)}, u32[]{:S(2)}) collective-permute-start(bf16[32,768]{1,0:T(8,128)(2,1)} %get-tuple-element.90), channel_id=1, source_target_pairs={{0,4},{4,0},{8,12},{12,8},{16,20},{20,16},{24,28},{28,24},{1,5},{5... | collective-permute-start | bytes 147464 | tf_op jit(solution)/shard_map/ppermute | solution.py:359
  151.5 11.2 %collective-permute-start.25 = (bf16[32,768]{1,0:T(8,128)(2,1)}, bf16[32,768]{1,0:T(8,128)(2,1)}, u32[]{:S(2)}, u32[]{:S(2)}) collective-permute-start(bf16[32,768]{1,0:T(8,128)(2,1)} %get-tuple-element.91), channel_id=1, source_target_pairs={{0,8},{4,12},{8,0},{12,4},{16,24},{20,28},{24,16},{28,20},{1,9},{5... | collective-permute-start | bytes 147464 | tf_op jit(solution)/shard_map/ppermute | solution.py:359
  152.9 16.5 %collective-permute-start.26 = (bf16[32,768]{1,0:T(8,128)(2,1)}, bf16[32,768]{1,0:T(8,128)(2,1)}, u32[]{:S(2)}, u32[]{:S(2)}) collective-permute-start(bf16[32,768]{1,0:T(8,128)(2,1)} %get-tuple-element.92), channel_id=1, source_target_pairs={{0,12},{4,8},{8,4},{12,0},{16,28},{20,24},{24,20},{28,16},{1,13},{... | collective-permute-start | bytes 147464 | tf_op jit(solution)/shard_map/ppermute | solution.py:359
  155.9 13.6 %collective-permute-start.27 = (bf16[32,768]{1,0:T(8,128)(2,1)}, bf16[32,768]{1,0:T(8,128)(2,1)}, u32[]{:S(2)}, u32[]{:S(2)}) collective-permute-start(bf16[32,768]{1,0:T(8,128)(2,1)} %get-tuple-element.93), channel_id=1, source_target_pairs={{0,16},{4,20},{8,24},{12,28},{16,0},{20,4},{24,8},{28,12},{1,17},{... | collective-permute-start | bytes 147464 | tf_op jit(solution)/shard_map/ppermute | solution.py:359
  156.4 13.0 %collective-permute-start.28 = (bf16[32,768]{1,0:T(8,128)(2,1)}, bf16[32,768]{1,0:T(8,128)(2,1)}, u32[]{:S(2)}, u32[]{:S(2)}) collective-permute-start(bf16[32,768]{1,0:T(8,128)(2,1)} %get-tuple-element.94), channel_id=1, source_target_pairs={{0,20},{4,16},{8,28},{12,24},{16,4},{20,0},{24,12},{28,8},{1,21},{... | collective-permute-start | bytes 147464 | tf_op jit(solution)/shard_map/ppermute | solution.py:359
  156.6 12.9 %collective-permute-start.29 = (bf16[32,768]{1,0:T(8,128)(2,1)}, bf16[32,768]{1,0:T(8,128)(2,1)}, u32[]{:S(2)}, u32[]{:S(2)}) collective-permute-start(bf16[32,768]{1,0:T(8,128)(2,1)} %get-tuple-element.95), channel_id=1, source_target_pairs={{0,24},{4,28},{8,16},{12,20},{16,8},{20,12},{24,0},{28,4},{1,25},{... | collective-permute-start | bytes 147464 | tf_op jit(solution)/shard_map/ppermute | solution.py:359
  162.7 7.1 %collective-permute-start.30 = (bf16[32,768]{1,0:T(8,128)(2,1)}, bf16[32,768]{1,0:T(8,128)(2,1)}, u32[]{:S(2)}, u32[]{:S(2)}) collective-permute-start(bf16[32,768]{1,0:T(8,128)(2,1)} %get-tuple-element.96), channel_id=1, source_target_pairs={{0,28},{4,24},{8,20},{12,16},{16,12},{20,8},{24,4},{28,0},{1,29},{... | collective-permute-start | bytes 147464 | tf_op jit(solution)/shard_map/ppermute | solution.py:359
  173.2 6.3 %collective-permute-start.32 = (bf16[128,768]{1,0:T(8,128)(2,1)}, bf16[128,768]{1,0:T(8,128)(2,1)S(1)}, u32[]{:S(2)}, u32[]{:S(2)}) collective-permute-start(bf16[128,768]{1,0:T(8,128)(2,1)} %get-tuple-element.98.refs_0_), channel_id=1, source_target_pairs={{0,2},{1,3},{2,0},{3,1},{4,6},{5,7},{6,4},{7,5},{8,10},{9,11},{10,... | collective-permute-start | bytes 589832 | tf_op jit(solution)/shard_map/ppermute | solution.py:359
  174.4 5.2 %collective-permute-start.31 = (bf16[128,768]{1,0:T(8,128)(2,1)}, bf16[128,768]{1,0:T(8,128)(2,1)S(1)}, u32[]{:S(2)}, u32[]{:S(2)}) collective-permute-start(bf16[128,768]{1,0:T(8,128)(2,1)} %get-tuple-element.98.refs_0_), channel_id=1, source_target_pairs={{0,1},{1,0},{2,3},{3,2},{4,5},{5,4},{6,7},{7,6},{8,9},{9,8},{10,11... | collective-permute-start | bytes 589832 | tf_op jit(solution)/shard_map/ppermute | solution.py:359
  179.6 1.4 collective-permute-start.33
  191.2 58.8 %all-to-all-start.3 = ((bf16[8,96,768]{2,1,0:T(8,128)(2,1)}), bf16[8,96,768]{2,1,0:T(8,128)(2,1)S(1)}, u32[]{:S(2)}, u32[]{:S(2)}) async-start(bf16[8,96,768]{2,1,0:T(8,128)(2,1)} %bitcast.45), calls=%async_computation.3 | async-start | bytes 2359296 | tf_op jit(solution)/shard_map/all_to_all | solution.py:386
  196.5 9.2 %copy-start.15 = (bf16[128,768]{1,0:T(8,128)(2,1)S(1)}, bf16[128,768]{1,0:T(8,128)(2,1)}, u32[]{:S(2)}) copy-start(bf16[128,768]{1,0:T(8,128)(2,1)} %get-tuple-element.81.refs_0_) | copy-start | bytes 589828
  201.1 1.7 collective-permute-start.35
  203.8 3.2 %collective-permute-start.41 = (f32[16,768]{1,0:T(8,128)}, f32[16,768]{1,0:T(8,128)S(1)}, u32[]{:S(2)}, u32[]{:S(2)}) collective-permute-start(f32[16,768]{1,0:T(8,128)} %get-tuple-element.113), channel_id=1, source_target_pairs={{0,1},{1,0},{2,3},{3,2},{4,5},{5,4},{6,7},{7,6},{8,9},{9,8},{10,11... | collective-permute-start | bytes 147464 | tf_op jit(solution)/shard_map/ppermute | solution.py:359
  204.0 4.3 %collective-permute-start.42 = (f32[16,768]{1,0:T(8,128)}, f32[16,768]{1,0:T(8,128)S(1)}, u32[]{:S(2)}, u32[]{:S(2)}) collective-permute-start(f32[16,768]{1,0:T(8,128)} %get-tuple-element.113), channel_id=1, source_target_pairs={{0,2},{1,3},{2,0},{3,1},{4,6},{5,7},{6,4},{7,5},{8,10},{9,11},{10,... | collective-permute-start | bytes 147464 | tf_op jit(solution)/shard_map/ppermute | solution.py:359
  205.2 4.0 %collective-permute-start.43 = (f32[16,768]{1,0:T(8,128)}, f32[16,768]{1,0:T(8,128)S(1)}, u32[]{:S(2)}, u32[]{:S(2)}) collective-permute-start(f32[16,768]{1,0:T(8,128)} %get-tuple-element.113), channel_id=1, source_target_pairs={{0,3},{1,2},{2,1},{3,0},{4,7},{5,6},{6,5},{7,4},{8,11},{9,10},{10,... | collective-permute-start | bytes 147464 | tf_op jit(solution)/shard_map/ppermute | solution.py:359
  205.7 13.7 %collective-permute-start.16 = (bf16[128,768]{1,0:T(8,128)(2,1)S(1)}, bf16[128,768]{1,0:T(8,128)(2,1)S(1)}, u32[]{:S(2)}, u32[]{:S(2)}) collective-permute-start(bf16[128,768]{1,0:T(8,128)(2,1)S(1)} %copy-done.15), channel_id=1, source_target_pairs={{0,2},{1,3},{2,0},{3,1},{4,6},{5,7},{6,4},{7,5},{8,10},{9,11},{10,... | collective-permute-start | bytes 589832 | tf_op jit(solution)/shard_map/ppermute | solution.py:359
  210.0 9.8 %collective-permute-start.44 = (f32[16,768]{1,0:T(8,128)S(1)}, f32[16,768]{1,0:T(8,128)S(1)}, u32[]{:S(2)}, u32[]{:S(2)}) collective-permute-start(f32[16,768]{1,0:T(8,128)S(1)} %add_add_fusion.1), channel_id=1, source_target_pairs={{0,4},{4,0},{8,12},{12,8},{1,5},{5,1},{9,13},{13,9},{2,6},{6,2},{1... | collective-permute-start | bytes 147464 | tf_op jit(solution)/shard_map/ppermute | solution.py:359
  212.1 15.7 %collective-permute-start.45 = (f32[16,768]{1,0:T(8,128)S(1)}, f32[16,768]{1,0:T(8,128)S(1)}, u32[]{:S(2)}, u32[]{:S(2)}) collective-permute-start(f32[16,768]{1,0:T(8,128)S(1)} %add_add_fusion.1), channel_id=1, source_target_pairs={{0,8},{4,12},{8,0},{12,4},{1,9},{5,13},{9,1},{13,5},{2,10},{6,14},... | collective-permute-start | bytes 147464 | tf_op jit(solution)/shard_map/ppermute | solution.py:359
  214.5 14.6 %collective-permute-start.46 = (f32[16,768]{1,0:T(8,128)S(1)}, f32[16,768]{1,0:T(8,128)S(1)}, u32[]{:S(2)}, u32[]{:S(2)}) collective-permute-start(f32[16,768]{1,0:T(8,128)S(1)} %add_add_fusion.1), channel_id=1, source_target_pairs={{0,12},{4,8},{8,4},{12,0},{1,13},{5,9},{9,5},{13,1},{2,14},{6,10},... | collective-permute-start | bytes 147464 | tf_op jit(solution)/shard_map/ppermute | solution.py:359
  219.3 16.0 %collective-permute-start.15 = (bf16[128,768]{1,0:T(8,128)(2,1)S(1)}, bf16[128,768]{1,0:T(8,128)(2,1)S(1)}, u32[]{:S(2)}, u32[]{:S(2)}) collective-permute-start(bf16[128,768]{1,0:T(8,128)(2,1)S(1)} %copy-done.15), channel_id=1, source_target_pairs={{0,1},{1,0},{2,3},{3,2},{4,5},{5,4},{6,7},{7,6},{8,9},{9,8},{10,11... | collective-permute-start | bytes 589832 | tf_op jit(solution)/shard_map/ppermute | solution.py:359
  219.4 15.8 %copy-start.16 = (bf16[128,768]{1,0:T(8,128)(2,1)}, bf16[128,768]{1,0:T(8,128)(2,1)S(1)}, u32[]{:S(2)}) copy-start(bf16[128,768]{1,0:T(8,128)(2,1)S(1)} %collective-permute-done.16.refs_2_) | copy-start | bytes 589828
  219.4 15.9 %collective-permute-start.17 = (bf16[128,768]{1,0:T(8,128)(2,1)S(1)}, bf16[128,768]{1,0:T(8,128)(2,1)S(1)}, u32[]{:S(2)}, u32[]{:S(2)}) collective-permute-start(bf16[128,768]{1,0:T(8,128)(2,1)S(1)} %collective-permute-done.16.refs_2_), channel_id=1, source_target_pairs={{0,1},{1,0},{2,3},{3,2},{4,5},{5,4},{6,7},{7,6},{8,9},{9,8},{10,11... | collective-permute-start | bytes 589832 | tf_op jit(solution)/shard_map/ppermute | solution.py:359
  219.8 20.5 %collective-permute-start.34 = (bf16[128,768]{1,0:T(8,128)(2,1)S(1)}, bf16[128,768]{1,0:T(8,128)(2,1)S(1)}, u32[]{:S(2)}, u32[]{:S(2)}) collective-permute-start(bf16[128,768]{1,0:T(8,128)(2,1)S(1)} %copy-done.34), channel_id=1, source_target_pairs={{0,1},{1,0},{2,3},{3,2},{4,5},{5,4},{6,7},{7,6},{8,9},{9,8},{10,11... | collective-permute-start | bytes 589832 | tf_op jit(solution)/shard_map/ppermute | solution.py:359
  227.8 12.6 %collective-permute-start.36 = (bf16[128,768]{1,0:T(8,128)(2,1)S(1)}, bf16[128,768]{1,0:T(8,128)(2,1)S(1)}, u32[]{:S(2)}, u32[]{:S(2)}) collective-permute-start(bf16[128,768]{1,0:T(8,128)(2,1)S(1)} %add_convert_fusion.3), channel_id=1, source_target_pairs={{0,2},{1,3},{2,0},{3,1},{4,6},{5,7},{6,4},{7,5},{8,10},{9,11},{10,... | collective-permute-start | bytes 589832 | tf_op jit(solution)/shard_map/ppermute | solution.py:359
  229.1 11.3 %collective-permute-start.47 = (f32[16,768]{1,0:T(8,128)S(1)}, f32[16,768]{1,0:T(8,128)S(1)}, u32[]{:S(2)}, u32[]{:S(2)}) collective-permute-start(f32[16,768]{1,0:T(8,128)S(1)} %add_add_fusion), channel_id=1, source_target_pairs={{0,16},{16,0},{1,17},{17,1},{2,18},{18,2},{3,19},{19,3},{4,20},{20... | collective-permute-start | bytes 147464 | tf_op jit(solution)/shard_map/ppermute | solution.py:359
  243.5 5.9 %collective-permute-start.38 = (bf16[128,768]{1,0:T(8,128)(2,1)}, bf16[128,768]{1,0:T(8,128)(2,1)S(1)}, u32[]{:S(2)}, u32[]{:S(2)}) collective-permute-start(bf16[128,768]{1,0:T(8,128)(2,1)} %shard_map.207.refs_0_), channel_id=1, source_target_pairs={{0,2},{1,3},{2,0},{3,1},{4,6},{5,7},{6,4},{7,5},{8,10},{9,11},{10,... | collective-permute-start | bytes 589832 | tf_op jit(solution)/shard_map/ppermute | solution.py:359
  244.8 6.7 %collective-permute-start.37 = (bf16[128,768]{1,0:T(8,128)(2,1)}, bf16[128,768]{1,0:T(8,128)(2,1)S(1)}, u32[]{:S(2)}, u32[]{:S(2)}) collective-permute-start(bf16[128,768]{1,0:T(8,128)(2,1)} %shard_map.207.refs_0_), channel_id=1, source_target_pairs={{0,1},{1,0},{2,3},{3,2},{4,5},{5,4},{6,7},{7,6},{8,9},{9,8},{10,11... | collective-permute-start | bytes 589832 | tf_op jit(solution)/shard_map/ppermute | solution.py:359
  249.3 2.2 collective-permute-start.39
  250.2 6.7 %collective-permute-start.40 = (bf16[96,768]{1,0:T(8,128)(2,1)S(1)}, bf16[96,768]{1,0:T(8,128)(2,1)S(1)}, u32[]{:S(2)}, u32[]{:S(2)}) collective-permute-start(bf16[96,768]{1,0:T(8,128)(2,1)S(1)} %reduce_sum.82), channel_id=1, source_target_pairs={{0,16},{16,0},{1,17},{17,1},{2,18},{18,2},{3,19},{19,3},{4,20},{20... | collective-permute-start | bytes 442376 | tf_op jit(solution)/shard_map/ppermute | solution.py:359
  (22 other events, 39.7 us)
